TPU v7x, 128 devices: a whole 4x4x4 slice. The times are simulated.
128 devices in a mesh: region: 16 (over y_lo, z, core), head: 8 (over y_hi, x).
Axes of the slice: x: 4, y: 4 (y_hi: 2, y_lo: 2; y = y_hi * 2 + y_lo), z: 4, core: 2. Of those that a mesh axis runs over, the one named last changes fastest.
Arguments:
- fine_tokens: float32 [73728, 512], P(('region', 'head')), may hold values from -6 to 6
- fine_shift: int32 [1], replicated, may hold values from 1 to 143
- window_counts: int32 [128], P('region'), may hold values from 36 to 144
- fine_qkv: bfloat16 [512, 1536], replicated, may hold values from -4 to 4
- fine_proj: bfloat16 [512, 512], replicated, may hold values from -0.25 to 0.25
- fine_up: bfloat16 [512, 2048], replicated, may hold values from -0.25 to 0.25
- fine_down: bfloat16 [2048, 512], replicated, may hold values from -0.125 to 0.125
- merge_weight: bfloat16 [2048, 1024], replicated, may hold values from -0.125 to 0.125
- coarse_qkv: bfloat16 [1024, 3072], P('region', 'head'), may hold values from -4 to 4
- coarse_proj: bfloat16 [1024, 1024], P('head', 'region'), may hold values from -0.1875 to 0.1875
- coarse_up: bfloat16 [1024, 4096], P('region', 'head'), may hold values from -0.1875 to 0.1875
- coarse_down: bfloat16 [4096, 1024], P('head', 'region'), may hold values from -0.09375 to 0.09375
- expand_weight: bfloat16 [1024, 2048], replicated, may hold values from -0.1875 to 0.1875
- out_weight: bfloat16 [1024, 512], replicated, may hold values from -0.1875 to 0.1875
Outputs:
- fine_result: float32 [73728, 512], P(('region', 'head'))
All inputs are finite; a program needn't handle non-finite values.
Results may differ from a plain program's by a relative error of at most 0.012.
Values may be sent and summed in bfloat16 or wider, within the bound.
No kernel may reach another device: no remote copies, remote signals or barrier semaphores. Data moves between devices by JAX's collectives and lax.ppermute only.
A program may use at most 128 MiB of HBM per device.

v0:
```python
import jax
import jax.numpy as jnp
from jax import lax
from jax.sharding import PartitionSpec as P

C = 512
HD = 64
HF = 8
HC = 16
WIN = 144


def with_halo(value, sides, width):
    edges = {}
    for axis, dim in sides:
        devices, length = (lax.axis_size(axis), value.shape[dim])
        up = [(i, (i + 1) % devices) for i in range(devices)]
        last = lax.slice_in_dim(value, length - width, length, axis=dim)
        initial = lax.slice_in_dim(value, 0, width, axis=dim)
        edges[dim] = (
            lax.ppermute(last, axis, up),
            lax.ppermute(initial, axis, [(b, a) for a, b in up]),
        )
    done = []
    for _, dim in sides:
        low, high = edges[dim]
        around = [(width, width) if d in done else (0, 0) for d in range(value.ndim)]
        value = jnp.concatenate([jnp.pad(low, around), value, jnp.pad(high, around)], axis=dim)
        done.append(dim)
    return value


def from_everyone(value, axis):
    devices = lax.axis_size(axis)
    return lax.all_to_all(
        jnp.broadcast_to(value[None], (devices, *value.shape)), axis, 0, 0, tiled=True
    )


def laid_out(blocks, dim):
    blocks = jnp.moveaxis(blocks, 0, dim)
    shape = blocks.shape
    return blocks.reshape(*shape[:dim], shape[dim] * shape[dim + 1], *shape[dim + 2 :])


def gathered_copies(value, axis, dim):
    blocks = from_everyone(value, axis)
    return laid_out(blocks, dim)


def turned_gather(arrays, axis, dims):
    turned = [jnp.moveaxis(a, dim, 0) for a, dim in zip(arrays, dims)]
    both = jnp.concatenate([t.reshape(len(t), -1) for t in turned], axis=1)
    filled, at, gathered = (lax.all_gather(both, axis, axis=0, tiled=True), 0, [])
    for t, dim in zip(turned, dims):
        share = filled[:, at : at + t[0].size].reshape(-1, *t.shape[1:])
        gathered.append(jnp.moveaxis(share, 0, dim))
        at += t[0].size
    return tuple(gathered)


def layer_norm(values):
    average = jnp.mean(values, axis=-1, keepdims=True)
    centred = values - average
    spread = jnp.mean(centred * centred, axis=-1, keepdims=True)
    return centred * lax.rsqrt(spread + 1e-05)


def window_attention(normed, qkv_weight, proj_weight, head_count, head_size, window, counts):
    row_count = normed.shape[0]
    window_total = row_count // window
    weight_heads = qkv_weight.reshape(qkv_weight.shape[0], head_count, 3 * head_size)
    packed = jnp.einsum(
        "nc,chj->hnj", normed, weight_heads, preferred_element_type=jnp.float32
    ).astype(jnp.bfloat16)
    packed = packed.reshape(head_count, window_total, window, 3 * head_size)
    queries = packed[..., :head_size]
    key_part = packed[..., head_size : 2 * head_size]
    value_part = packed[..., 2 * head_size :]
    scores = jnp.einsum(
        "hwqd,hwkd->hwqk", queries, key_part, preferred_element_type=jnp.float32
    ) * head_size ** (-0.5)
    if counts is not None:
        position = jnp.arange(window, dtype=jnp.int32)
        visible = position[None, :] < counts[:, None]
        scores = jnp.where(visible[None, :, None, :], scores, -1e30)
    row_max = jnp.max(scores, axis=-1, keepdims=True)
    raised = jnp.exp(scores - row_max)
    weights = (raised / jnp.sum(raised, axis=-1, keepdims=True)).astype(jnp.bfloat16)
    blended = jnp.einsum(
        "hwqk,hwkd->hwqd", weights, value_part, preferred_element_type=jnp.float32
    ).astype(jnp.bfloat16)
    blended = blended.reshape(head_count, row_count, head_size)
    proj_heads = proj_weight.reshape(head_count, head_size, proj_weight.shape[1])
    return jnp.einsum("hnd,hdc->nc", blended, proj_heads, preferred_element_type=jnp.float32)


def hidden_layer(normed, up_weight):
    hidden = jnp.dot(normed, up_weight, preferred_element_type=jnp.float32)
    return jax.nn.gelu(hidden, approximate=False).astype(jnp.bfloat16)


def body(
    fine_tokens,
    fine_shift,
    window_counts,
    fine_qkv,
    fine_proj,
    fine_up,
    fine_down,
    merge_weight,
    coarse_qkv,
    coarse_proj,
    coarse_up,
    coarse_down,
    expand_weight,
    out_weight,
):
    offset = fine_shift[0]
    local_rows = fine_tokens.shape[0]
    normed = layer_norm(fine_tokens).astype(jnp.bfloat16)
    extended = with_halo(normed, ((("region", "head"), 0),), WIN)
    rolled = lax.dynamic_slice_in_dim(extended, offset, local_rows + WIN, 0)
    attended = window_attention(rolled, fine_qkv, fine_proj, HF, HD, WIN, None)
    restored = lax.dynamic_slice_in_dim(attended, WIN - offset, local_rows, 0)
    fine_mid = fine_tokens + restored
    fine_hidden = hidden_layer(layer_norm(fine_mid).astype(jnp.bfloat16), fine_up)
    fine_out = fine_mid + jnp.dot(fine_hidden, fine_down, preferred_element_type=jnp.float32)
    merged = fine_out.reshape(local_rows // 4, 4 * C)
    grouped = layer_norm(merged).astype(jnp.bfloat16)
    coarse = jnp.dot(grouped, merge_weight, preferred_element_type=jnp.float32)
    coarse_norm = layer_norm(coarse).astype(jnp.bfloat16)
    weight_parts = (coarse_qkv, coarse_proj, coarse_up, coarse_down)
    columns = (
        gathered_copies(weight_parts[0], "head", 1),
        gathered_copies(weight_parts[1], "head", 0),
        gathered_copies(weight_parts[2], "head", 1),
        gathered_copies(weight_parts[3], "head", 0),
    )
    qkv_full, proj_full, up_full, down_full = turned_gather(
        (columns[0], columns[1], columns[2], columns[3]), "region", (0, 1, 0, 1)
    )
    window_total = coarse_norm.shape[0] // WIN
    own_counts = lax.dynamic_slice_in_dim(
        window_counts, lax.axis_index("head") * window_total, window_total, 0
    )
    coarse_mid = coarse + window_attention(
        coarse_norm, qkv_full, proj_full, HC, HD, WIN, own_counts
    )
    coarse_hidden = hidden_layer(layer_norm(coarse_mid).astype(jnp.bfloat16), up_full)
    coarse_out = coarse_mid + jnp.dot(coarse_hidden, down_full, preferred_element_type=jnp.float32)
    expanded = jnp.dot(
        coarse_out.astype(jnp.bfloat16), expand_weight, preferred_element_type=jnp.float32
    ).astype(jnp.bfloat16)
    spread_rows = expanded.reshape(local_rows, C)
    joined = jnp.concatenate([fine_out.astype(jnp.bfloat16), spread_rows], axis=1)
    return jnp.dot(joined, out_weight, preferred_element_type=jnp.float32)


def solution(mesh):
    in_specs = (
        P(("region", "head"), None),
        P(),
        P("region"),
        P(),
        P(),
        P(),
        P(),
        P(),
        P("region", "head"),
        P("head", "region"),
        P("region", "head"),
        P("head", "region"),
        P(),
        P(),
    )
    out_specs = P(("region", "head"), None)
    return jax.shard_map(body, mesh=mesh, in_specs=in_specs, out_specs=out_specs, check_vma=False)
```

profile of v0, /device:TPU:1, one launch (start us, length us, event | category | flops | bytes accessed | tf_op | source)
XLA Modules:
  0.0 256.0 jit_solution(4802875899977580490)
XLA Ops:
  7.4 14.3 %all_to_all.20 = bf16[8,128,64]{1,2,0:T(8,128)(2,1)} all-to-all(bf16[8,128,64]{1,2,0:T(8,128)(2,1)S(1)} %broadcast_in_dim.18), channel_id=1, replica_groups=mesh['region'=16,'head'=8] {'head'}, dimensions={0} | all-to-all | bytes 262144 | tf_op jit(solution)/shard_map/all_to_all | solution.py:35
  22.6 11.0 %all_to_all.21 = bf16[8,64,384]{2,1,0:T(8,128)(2,1)S(1)} all-to-all(bf16[8,64,384]{2,1,0:T(8,128)(2,1)S(1)} %broadcast_in_dim.17), channel_id=1, replica_groups=mesh['region'=16,'head'=8] {'head'}, dimensions={0} | all-to-all | bytes 786432 | tf_op jit(solution)/shard_map/all_to_all | solution.py:35
  34.5 11.5 %all_to_all.22 = bf16[8,512,64]{1,2,0:T(8,128)(2,1)S(1)} all-to-all(bf16[8,512,64]{1,2,0:T(8,128)(2,1)S(1)} %broadcast_in_dim.20), channel_id=1, replica_groups=mesh['region'=16,'head'=8] {'head'}, dimensions={0} | all-to-all | bytes 1048576 | tf_op jit(solution)/shard_map/all_to_all | solution.py:35
  46.8 3.5 %all-to-all-start.2 = ((bf16[8,64,512]{2,1,0:T(8,128)(2,1)}), bf16[8,64,512]{2,1,0:T(8,128)(2,1)S(1)}, u32[]{:S(2)}, u32[]{:S(2)}) async-start(bf16[8,64,512]{2,1,0:T(8,128)(2,1)} %broadcast_in_dim.19), calls=%async_computation.2 | async-start | bytes 1048576 | tf_op jit(solution)/shard_map/all_to_all | solution.py:35
  53.6 5.7 %all-to-all-done.2 = bf16[8,64,512]{2,1,0:T(8,128)(2,1)S(1)} async-done(((bf16[8,64,512]{2,1,0:T(8,128)(2,1)}), bf16[8,64,512]{2,1,0:T(8,128)(2,1)S(1)}, u32[]{:S(2)}, u32[]{:S(2)}) %all-to-all-start.2) | async-done | bytes 524320 | tf_op jit(solution)/shard_map/all_to_all | solution.py:35
  59.4 2.5 pad_maximum_fusion
  64.8 5.9 %collective-permute-start.1 = (bf16[144,512]{1,0:T(8,128)(2,1)S(1)}, bf16[144,512]{1,0:T(8,128)(2,1)}, u32[]{:S(2)}, u32[]{:S(2)}) collective-permute-start(bf16[144,512]{1,0:T(8,128)(2,1)S(1)} %get-tuple-element.9), channel_id=1, source_target_pairs={{1,0},{2,1},{3,2},{4,3},{5,4},{6,5},{7,6},{8,7},{9,8},{10,9},{11,1... | collective-permute-start | bytes 442376 | tf_op jit(solution)/shard_map/ppermute | solution.py:22
  73.9 4.0 %fusion.94 = f32[720,1536]{0,1:S(1)} fusion(bf16[512,1536]{1,0:T(8,128)(2,1)} %param.17, s32[]{:T(128)S(6)} %select_n.14, bf16[144,512]{1,0:T(8,128)(2,1)} %collective-permute-done, bf16[576,512]{1,0:T(8,128)(2,1)} %copy-done.6, bf16[144,512]{1,0:T(8,128)(2,1)} %collective-permute-done.1), kind=kOutput, calls=%fused_computation.122 | convolution fusion | flops 1134673920 | bytes 7176196
  79.6 4.5 %copy.55 = bf16[8,720,192]{2,1,0:T(8,128)(2,1)} copy(bf16[8,720,192]{1,2,0:T(8,128)(2,1)} %convert_bitcast_fusion) | data formatting | bytes 4423680 | tf_op jit(solution)/shard_map/convert_element_type | solution.py:75
  84.1 2.9 %fusion.35 = f32[8,5,144,144]{2,3,1,0:T(8,128)S(1)} fusion(bf16[8,5,144,192]{3,2,1,0:T(8,128)(2,1)} %bitcast.89), kind=kOutput, calls=%fused_computation.61 | convolution fusion | flops 106168320 | bytes 5529600 | tf_op jit(solution)/shard_map/hwqd,hwkd->hwqk/dot_general | solution.py:80
  87.1 5.6 %fusion.182 = (f32[8,5,144]{2,1,0:T(8,128)S(1)}, f32[8,5,144,144]{2,3,1,0:T(8,128)S(1)}) fusion(f32[8,5,144,144]{2,3,1,0:T(8,128)S(1)} %fusion.35), kind=kOutput, calls=%fused_computation.223 | output fusion | flops 3317903 | bytes 6658560 | tf_op jit(solution)/shard_map/sub | solution.py:88
  94.6 2.7 %copy.60 = bf16[8,5,144,64]{3,2,1,0:T(8,128)(2,1)} copy(bf16[8,5,144,64]{2,3,1,0:T(8,128)(2,1)} %fusion.34) | data formatting | bytes 1474560 | tf_op jit(solution)/shard_map/convert_element_type | solution.py:92
  101.1 14.3 %fusion.183 = (f32[576]{0:T(1024)S(1)}, f32[576,512]{1,0:T(8,128)S(1)}) fusion(f32[576,512]{1,0:T(8,128)} %copy-done.4, bf16[2048,512]{1,0:T(8,128)(2,1)S(1)} %copy-done, bf16[512,2048]{1,0:T(8,128)(2,1)} %param.19, f32[576]{0:T(1024)S(1)} %add_rsqrt_fusion, f32[576]{0:T(1024)S(1)} %broadcast_multiply_fusion), kind=kOutput, calls=%fused_computation.224 | convolution fusion | flops 2494070272 | bytes 6560512 | tf_op jit(solution)/shard_map/dot_general | solution.py:128
  117.7 3.3 %fusion.184 = (f32[144]{0:T(256)S(1)}, f32[144,1024]{1,0:T(8,128)S(1)}) fusion(bf16[2048,1024]{1,0:T(8,128)(2,1)} %param.21, f32[144,2048]{1,0:T(8,128)S(1)} %reshape.155, f32[144]{0:T(256)S(1)} %add_rsqrt_fusion.4, f32[144]{0:T(256)S(1)} %broadcast_multiply_fusion.4), kind=kOutput, calls=%fused_computation.225 | convolution fusion | flops 605011840 | bytes 5965504 | tf_op jit(solution)/shard_map/dot_general | solution.py:131
  121.3 75.4 %all-gather.2.cloned.1.call-done = bf16[1024,12288]{1,0:T(8,128)(2,1)} async-done(((bf16[64,12288]{1,0:T(8,128)(2,1)}), bf16[1024,12288]{1,0:T(8,128)(2,1)}) %all-gather.2.cloned.1.call-update) | async-done | bytes 25165840 | tf_op jit(solution)/shard_map/all_gather | solution.py:54
  196.7 5.9 %slice.53 = bf16[1024,3072]{1,0:T(8,128)(2,1)} slice(bf16[1024,12288]{1,0:T(8,128)(2,1)} %all-gather.2.cloned.1.call-done), slice={[0:1024], [0:3072]} | slice | bytes 12582912 | tf_op jit(solution)/shard_map/slice | solution.py:56
  202.6 8.6 %copy.66 = bf16[1024,3072]{0,1:T(8,128)(2,1)} copy(bf16[1024,3072]{1,0:T(8,128)(2,1)} %slice.53) | data formatting | bytes 12582912 | tf_op jit(solution)/shard_map/slice | solution.py:56
  213.0 2.6 %copy.71 = bf16[1024,1024]{1,0:T(8,128)(2,1)} copy(bf16[1024,1024]{0,1:T(8,128)(2,1)S(1)} %slice_bitcast_fusion) | data formatting | bytes 4194304 | tf_op jit(solution)/shard_map/transpose | solution.py:57
  215.5 6.2 %fusion.39 = bf16[16,1,144,192]{3,2,0,1:T(8,128)(2,1)} fusion(bf16[1024,16,192]{0,2,1:T(8,128)(2,1)} %bitcast.91, f32[144,1024]{1,0:T(8,128)S(1)} %get-tuple-element.16, f32[144]{0:T(256)S(1)} %add_rsqrt_fusion.3, f32[144]{0:T(256)S(1)} %broadcast_multiply_fusion.3), kind=kOutput, calls=%fused_computation.66 | convolution fusion | flops 906854400 | bytes 7767168 | tf_op jit(solution)/shard_map/nc,chj->hnj/dot_general | solution.py:73
  221.7 3.8 %fusion.185 = (f32[16,144]{1,0:T(8,128)S(1)}, f32[16,144,144]{1,2,0:T(8,128)}) fusion(pred[144]{0:T(512)(128)(4,1)S(1)} %iota_compare_fusion, bf16[16,1,144,192]{3,2,0,1:T(8,128)(2,1)} %fusion.39), kind=kOutput, calls=%fused_computation.226 | convolution fusion | flops 43794576 | bytes 2221200 | tf_op jit(solution)/shard_map/sub | solution.py:88
  225.5 2.7 %fusion.186 = (f32[144]{0:T(256)S(1)}, f32[144,1024]{1,0:T(8,128)S(1)}) fusion(f32[144,1024]{1,0:T(8,128)S(1)} %get-tuple-element.16, bf16[16,64,1024]{2,1,0:T(8,128)(2,1)S(1)} %bitcast.93, f32[16,144,144]{1,2,0:T(8,128)} %get-tuple-element.18, f32[16,144]{1,0:T(8,128)S(1)} %get-tuple-element.17, bf16[16,1,144,192]{3,2,0,1:T(8,128)(2,1)} %fusion.39), kind=kOutput, calls=%fused_computation.227 | convolution fusion | flops 345563008 | bytes 6235712 | tf_op jit(solution)/shard_map/hnd,hdc->nc/dot_general | solution.py:95
  228.5 13.2 %fusion.47 = bf16[144,1024]{1,0:T(8,128)(2,1)S(1)} fusion(f32[144,1024]{1,0:T(8,128)S(1)} %get-tuple-element.20, bf16[1024,12288]{1,0:T(8,128)(2,1)} %all-gather.2.cloned.1.call-done, f32[144]{0:T(256)S(1)} %add_rsqrt_fusion.2, f32[144]{0:T(256)S(1)} %broadcast_multiply_fusion.2), kind=kOutput, calls=%fused_computation.72 | convolution fusion | flops 2454994944 | bytes 18253824 | tf_op jit(solution)/shard_map/dot_general | solution.py:151
  241.7 3.0 %convolution_convert_fusion = bf16[144,2048]{1,0:T(8,128)(2,1)S(1)} fusion(bf16[144,1024]{1,0:T(8,128)(2,1)S(1)} %fusion.47, bf16[1024,2048]{1,0:T(8,128)(2,1)} %param.26), kind=kOutput, calls=%fused_computation.32 | convolution fusion | flops 604274688 | bytes 5079040 | tf_op jit(solution)/shard_map/dot_general | solution.py:152
  245.9 3.2 %fusion.55 = f32[576,512]{1,0:T(8,128)} fusion(bf16[1024,512]{1,0:T(8,128)(2,1)} %param.27, bf16[576,512]{1,0:T(8,128)(2,1)} %reshape.166, bf16[576,512]{1,0:T(8,128)(2,1)S(1)} %copy-done.7), kind=kOutput, calls=%fused_computation.73 | convolution fusion | flops 606339072 | bytes 3407872 | tf_op jit(solution)/shard_map/dot_general | solution.py:157
  (66 shorter events, 25.1 us)
Async XLA Ops:
  6.5 94.6 %copy-start = (bf16[2048,512]{1,0:T(8,128)(2,1)S(1)}, bf16[2048,512]{1,0:T(8,128)(2,1)}, u32[]{:S(2)}) copy-start(bf16[2048,512]{1,0:T(8,128)(2,1)} %param.20) | copy-start | bytes 6291460
  6.5 39.5 %copy-start.8 = (bf16[64,512]{1,0:T(8,128)(2,1)S(1)}, bf16[64,512]{1,0:T(8,128)(2,1)}, u32[]{:S(2)}) copy-start(bf16[64,512]{1,0:T(8,128)(2,1)} %param.24) | copy-start | bytes 196612
  46.8 12.5 %all-to-all-start.2 = ((bf16[8,64,512]{2,1,0:T(8,128)(2,1)}), bf16[8,64,512]{2,1,0:T(8,128)(2,1)S(1)}, u32[]{:S(2)}, u32[]{:S(2)}) async-start(bf16[8,64,512]{2,1,0:T(8,128)(2,1)} %broadcast_in_dim.19), calls=%async_computation.2 | async-start | bytes 1048576 | tf_op jit(solution)/shard_map/all_to_all | solution.py:35
  50.3 146.3 %all-gather.2.cloned.1.call-start = ((), (), s32[]{:S(2)}) async-start(), calls=%async_computation.4 | async-start | bytes 26738688 | tf_op jit(solution)/shard_map/all_gather | solution.py:54
  59.4 2.6 %copy-start.2 = (f32[576,512]{1,0:T(8,128)S(1)}, f32[576,512]{1,0:T(8,128)}, u32[]{:S(2)}) copy-start(f32[576,512]{1,0:T(8,128)} %param.14) | copy-start | bytes 3538948
  62.0 9.4 %copy-start.9 = (s32[8]{0:T(128)S(1)}, s32[8]{0:T(128)}, u32[]{:S(2)}) copy-start(s32[8]{0:T(128)} %param.16) | copy-start | bytes 100
  62.7 0.8 copy-start.6
  64.2 9.7 %collective-permute-start = (bf16[144,512]{1,0:T(8,128)(2,1)}, bf16[144,512]{1,0:T(8,128)(2,1)}, u32[]{:S(2)}, u32[]{:S(2)}) collective-permute-start(bf16[144,512]{1,0:T(8,128)(2,1)} %get-tuple-element.10), channel_id=1, source_target_pairs={{0,1},{1,2},{2,3},{3,4},{4,5},{5,6},{6,7},{7,8},{8,9},{9,10},{10,1... | collective-permute-start | bytes 442376 | tf_op jit(solution)/shard_map/ppermute | solution.py:21
  64.8 9.1 %collective-permute-start.1 = (bf16[144,512]{1,0:T(8,128)(2,1)S(1)}, bf16[144,512]{1,0:T(8,128)(2,1)}, u32[]{:S(2)}, u32[]{:S(2)}) collective-permute-start(bf16[144,512]{1,0:T(8,128)(2,1)S(1)} %get-tuple-element.9), channel_id=1, source_target_pairs={{1,0},{2,1},{3,2},{4,3},{5,4},{6,5},{7,6},{8,7},{9,8},{10,9},{11,1... | collective-permute-start | bytes 442376 | tf_op jit(solution)/shard_map/ppermute | solution.py:22
  87.1 5.6 %copy-start.3 = (bf16[8,720,192]{2,1,0:T(8,128)(2,1)S(1)}, bf16[8,720,192]{2,1,0:T(8,128)(2,1)}, u32[]{:S(2)}) copy-start(bf16[8,720,192]{2,1,0:T(8,128)(2,1)} %copy.55) | copy-start | bytes 6635524
  99.8 1.0 copy-start.4
  221.7 3.8 %copy-start.5 = (bf16[1024,1024]{1,0:T(8,128)(2,1)S(1)}, bf16[1024,1024]{1,0:T(8,128)(2,1)}, u32[]{:S(2)}) copy-start(bf16[1024,1024]{1,0:T(8,128)(2,1)} %copy.71) | copy-start | bytes 6291460
  241.7 4.2 %copy-start.7 = (bf16[576,512]{1,0:T(8,128)(2,1)S(1)}, bf16[576,512]{1,0:T(8,128)(2,1)}, u32[]{:S(2)}) copy-start(bf16[576,512]{1,0:T(8,128)(2,1)} %get-tuple-element.7) | copy-start | bytes 1769476
  244.8 4.4 %copy-start.1 = (bf16[2048,512]{1,0:T(8,128)(2,1)S(1)}, bf16[2048,512]{1,0:T(8,128)(2,1)}, u32[]{:S(2)}) copy-start(bf16[2048,512]{1,0:T(8,128)(2,1)} %param.20) | copy-start | bytes 6291460
Sparse Core Ops, SparseCore 0:
  62.1 134.5 all-gather.1
where the time goes:
time: 258 us; the launch traced here: 256 us
  waiting for transfers between devices  82.4 us (32%)
  matrix products  60.8 us (24%)
  local copies, waits for them, and re-layouts  38 us (15%)
  blocking collectives  36.9 us (14%)
  between operations  14.3 us (6%)
  other arithmetic  13.6 us (5%)
  starting transfers between devices  10 us (4%)
    all_gather x1, waiting for transfers between devices, turned_gather(): lax.all_gather(both, axis, axis=0, tiled=True)  75.4 us
    all_to_all x3, blocking collectives, from_everyone(): lax.all_to_all(jnp.broadcast_to(value[None], (devices, *value.shape)), ax...  36.9 us
    slice x2, local copies, waits for them, and re-layouts, turned_gather(): share = filled[:, at:at + t[0].size].reshape(-1, *t.shape[1:])  14.5 us
    dot_general x1, matrix products, body(): jnp.dot(fine_hidden, fine_down, preferred_element_type=jnp.float32)  14.3 us
    dot_general x1, matrix products, body(): jnp.dot(coarse_hidden, down_full, preferred_element_type=jnp.float32)  13.2 us
    dot_general x1, matrix products, window_attention(): jnp.einsum('nc,chj->hnj', normed, weight_heads, preferred_element_type=jn...  6.16 us
    ppermute x1, starting transfers between devices, with_halo(): lax.ppermute(initial, axis, [(b, a) for a, b in up])  5.95 us
    all_to_all x1, waiting for transfers between devices, from_everyone(): lax.all_to_all(jnp.broadcast_to(value[None], (devices, *value.shape)), ax...  5.71 us
  transfers between devices with their start and end apart: 4, of which 3 were waited for; matrix products, arithmetic and copies ran while one was open for 20% of the time, Pallas kernels for 0%

commit v1 on v0

v1 whole, which is shorter than its diff:
```python
import jax
import jax.numpy as jnp
from jax import lax
from jax.experimental import pallas as pl
from jax.experimental.pallas import tpu as pltpu
from jax.sharding import Mesh, PartitionSpec as P

C = 512
HD = 64
HF = 8
HC = 16
WIN = 144
AXES = ("ylo", "z", "core", "yhi", "x")
STEPS = (0, 1, -1, 2)
F32 = jnp.float32
BF16 = jnp.bfloat16
MIB = 1024 * 1024


def hopped(value, dims, steps):
    pairs = []
    for source in range(128):
        rest, here = source, {}
        for name, size in (("x", 4), ("yhi", 2), ("core", 2), ("z", 4), ("ylo", 2)):
            here[name] = rest % size
            rest //= size
        there = {"x": here["x"], "y": here["yhi"] * 2 + here["ylo"], "z": here["z"]}
        core = here["core"]
        there[dims[core]] = (there[dims[core]] + steps[core]) % 4
        ylo, yhi = there["y"] % 2, there["y"] // 2
        pairs.append((source, (((ylo * 4 + there["z"]) * 2 + core) * 2 + yhi) * 4 + there["x"]))
    return lax.ppermute(value, AXES, pairs)


def direct(value, dims):
    return [value if step == 0 else hopped(value, dims, (step, step)) for step in STEPS]


def core_swap(value):
    return lax.ppermute(value, "core", [(0, 1), (1, 0)])


def normalised(values):
    average = jnp.mean(values, axis=-1, keepdims=True)
    centred = values - average
    spread_of = jnp.mean(centred * centred, axis=-1, keepdims=True)
    return centred * lax.rsqrt(spread_of + 1e-05)


def gelu(hidden):
    return 0.5 * hidden * (1.0 + lax.erf(hidden * (0.5**0.5)))


def dot(a, b):
    return lax.dot_general(a, b, (((1,), (0,)), ((), ())), preferred_element_type=F32)


def dot_t(a, b):
    return lax.dot_general(a, b, (((1,), (1,)), ((), ())), preferred_element_type=F32)


def attend(packed, count):
    queries = packed[:, :HD]
    keys = packed[:, HD : 2 * HD]
    values = packed[:, 2 * HD :]
    scores = dot_t(queries, keys) * HD ** (-0.5)
    if count is not None:
        position = lax.broadcasted_iota(jnp.int32, scores.shape, 1)
        scores = jnp.where(position < count, scores, -1e30)
    row_max = jnp.max(scores, axis=-1, keepdims=True)
    raised = jnp.exp(scores - row_max)
    weights = (raised / jnp.sum(raised, axis=-1, keepdims=True)).astype(BF16)
    return dot(weights, values).astype(BF16)


def vmem(count):
    return [pl.BlockSpec(memory_space=pltpu.VMEM)] * count


def params(mib):
    return pltpu.CompilerParams(vmem_limit_bytes=mib * MIB)


def prepare_kernel(place, tokens, qkv, proj_t, up, down_t, normed, mine, theirs):
    normed[...] = normalised(tokens[...]).astype(BF16)
    halves = [
        (
            jnp.concatenate(
                [qkv[:, 192 * c : 192 * (c + 1)], proj_t[:, HD * c : HD * (c + 1)]], axis=1
            ),
            up[:, 256 * c : 256 * (c + 1)],
            down_t[:, 256 * c : 256 * (c + 1)],
        )
        for c in range(2)
    ]
    for core in range(2):

        @pl.when(place[3] == core)
        def _():
            for unit in range(3):
                mine[unit] = halves[core][unit]
                theirs[unit] = halves[1 - core][unit]


def prepare(place, tokens, qkv, proj_t, up, down_t):
    part = jax.ShapeDtypeStruct((3, 64, 256), BF16)
    return pl.pallas_call(
        prepare_kernel,
        out_shape=(jax.ShapeDtypeStruct(tokens.shape, BF16), part, part),
        in_specs=[pl.BlockSpec(memory_space=pltpu.SMEM)] + vmem(5),
        out_specs=tuple(vmem(3)),
        compiler_params=params(8),
        cost_estimate=pl.CostEstimate(flops=3_000_000, bytes_accessed=2_500_000, transcendentals=0),
        name="prepare",
    )(place, tokens, qkv, proj_t, up, down_t)


def arrange_kernel(kind, place, own, r1, r2, r3, out):
    if kind == "d":
        here = place[2]
    else:
        here = jnp.where(place[3] == 0, place[0], place[1])
    for part, step in zip((own, r1, r2, r3), STEPS):
        at = along(here, -step)
        for unit in range(own.shape[0]):
            out[unit, at] = part[unit]


def arrange(kind, place, parts):
    units = parts[0].shape[0]
    return pl.pallas_call(
        lambda *refs: arrange_kernel(kind, *refs),
        out_shape=jax.ShapeDtypeStruct((units, 4, 128, 256), BF16),
        in_specs=[pl.BlockSpec(memory_space=pltpu.SMEM)] + vmem(4),
        out_specs=pl.BlockSpec(memory_space=pltpu.VMEM),
        compiler_params=params(6),
        cost_estimate=pl.CostEstimate(flops=0, bytes_accessed=1_000_000, transcendentals=0),
        name="arrange_" + kind,
    )(place, *parts)


def along(i, step):
    return lax.rem(i + step + 4, 4)


def fine_attention_kernel(offset, tokens, normed, low, high, qkv, proj, out, ext, packed, blend):
    rows = normed.shape[0]
    shift = offset[0]
    ext[0:WIN, :] = low[...].astype(F32)
    ext[WIN : WIN + rows, :] = normed[...].astype(F32)
    ext[WIN + rows :, :] = high[...].astype(F32)
    rolled = pltpu.roll(ext[...], ext.shape[0] - shift, 0)[: rows + WIN].astype(BF16)
    packed[...] = dot(rolled, qkv[...]).astype(BF16)

    def window(w, carry):
        start = pl.multiple_of(w * WIN, WIN)
        for head in range(HF):
            part = packed[pl.ds(start, WIN), head * 3 * HD : (head + 1) * 3 * HD]
            blend[pl.ds(start, WIN), head * HD : (head + 1) * HD] = attend(part, None)
        return carry

    lax.fori_loop(0, (rows + WIN) // WIN, window, 0)
    ext[0 : rows + WIN, :] = dot(blend[...], proj[...])
    back = pltpu.roll(ext[...], shift + rows + WIN, 0)
    out[...] = tokens[...] + back[:rows]


def fine_attention(offset, tokens, normed, low, high, qkv, proj):
    rows = tokens.shape[0]
    return pl.pallas_call(
        fine_attention_kernel,
        out_shape=jax.ShapeDtypeStruct((rows, C), F32),
        in_specs=[pl.BlockSpec(memory_space=pltpu.SMEM)] + vmem(6),
        out_specs=pl.BlockSpec(memory_space=pltpu.VMEM),
        scratch_shapes=[
            pltpu.VMEM((rows + 2 * WIN, C), F32),
            pltpu.VMEM((rows + WIN, 3 * C), BF16),
            pltpu.VMEM((rows + WIN, C), BF16),
        ],
        compiler_params=params(26),
        cost_estimate=pl.CostEstimate(flops=2_500_000_000, bytes_accessed=6_000_000, transcendentals=900_000),
        name="fine_attention",
    )(offset, tokens, normed, low, high, qkv, proj)


def fine_mlp_kernel(place, counts, mid, up, down, merge, out_weight, skip, coarse, total, lanes):
    rows = mid.shape[0]
    fine = normalised(mid[...]).astype(BF16)
    total[...] = mid[...]
    for part in range(4):
        hidden = gelu(dot(fine, up[:, part * C : (part + 1) * C])).astype(BF16)
        total[...] += dot(hidden, down[part * C : (part + 1) * C, :])
    skip[...] = dot(total[...].astype(BF16), out_weight[:C, :])
    for k in range(4):
        lanes[k] = total[:, k * 128 : (k + 1) * 128]
    pieces = [
        jnp.concatenate([lanes[k, pl.ds(j, rows // 4, stride=4), :] for k in range(4)], axis=1)
        for j in range(4)
    ]
    average = sum(jnp.sum(p, axis=-1, keepdims=True) for p in pieces) * (1.0 / (4 * C))
    pieces = [p - average for p in pieces]
    square = sum(jnp.sum(p * p, axis=-1, keepdims=True) for p in pieces) * (1.0 / (4 * C))
    scale = lax.rsqrt(square + 1e-05)
    result = None
    for j, p in enumerate(pieces):
        term = dot((p * scale).astype(BF16), merge[j * C : (j + 1) * C, :])
        result = term if result is None else result + term
    coarse[:WIN, :] = result
    count = counts[place[1] // 2 * 4 + place[0]]
    coarse[WIN:, :] = jnp.full((8, 2 * C), count, jnp.int32).astype(F32)


def fine_mlp(place, counts, mid, up, down, merge, out_weight):
    rows = mid.shape[0]
    return pl.pallas_call(
        fine_mlp_kernel,
        out_shape=(
            jax.ShapeDtypeStruct((rows, C), F32),
            jax.ShapeDtypeStruct((rows // 4 + 8, 2 * C), F32),
        ),
        in_specs=[pl.BlockSpec(memory_space=pltpu.SMEM)] * 2 + vmem(5),
        out_specs=tuple(vmem(2)),
        scratch_shapes=[pltpu.VMEM((rows, C), F32), pltpu.VMEM((4, rows, 128), F32)],
        compiler_params=params(32),
        cost_estimate=pl.CostEstimate(flops=3_500_000_000, bytes_accessed=12_000_000, transcendentals=1_200_000),
        name="fine_mlp",
    )(place, counts, mid, up, down, merge, out_weight)


def fetch_turned(place, parts, weight, sems):
    x, y, z = place[0], place[1], place[2]
    copies = []
    for at, part in enumerate(parts):
        for slot in range(4):
            sem = sems.at[at * 4 + slot]
            source = part.at[slot]
            from_y, from_z = along(y, -STEPS[slot]), along(z, -STEPS[at])
            zero = pltpu.make_async_copy(
                source, weight.at[lax.div(from_y, 2), :, lax.rem(from_y, 2), from_z], sem
            )
            across_z, across_x = along(z, -STEPS[slot]), along(x, -STEPS[at])
            ones = [
                pltpu.make_async_copy(
                    source.at[pl.ds(2 * yhi, 2)], weight.at[yhi, across_x, :, across_z], sem
                )
                for yhi in range(2)
            ]

            @pl.when(place[3] == 0)
            def _():
                zero.start()

            @pl.when(place[3] == 1)
            def _():
                for one in ones:
                    one.start()

            copies.append(zero)
    return copies


def fetch_down(place, parts, weight, sems):
    x, y = place[0], place[1]
    turn = 1 - 2 * place[3]
    copies = []
    for at, (part, step) in enumerate(zip(parts, (0, -turn, turn, 2))):
        from_y = along(y, step)
        for slot in range(4):
            copy = pltpu.make_async_copy(
                part.at[slot],
                weight.at[lax.div(from_y, 2), along(x, -STEPS[slot]), lax.rem(from_y, 2)],
                sems.at[at * 4 + slot],
            )
            copy.start()
            copies.append(copy)
    return copies


def whole(weight, head):
    return weight[head // 4, head % 4].reshape(2 * C, 256)


def coarse_attention_kernel(place, own, other, a0, a1, a2, a3, out, weight, x, blend, proj, sems):
    copies = fetch_turned(place, (a0, a1, a2, a3), weight, sems)
    x[:WIN, :] = normalised(own[:WIN, :]).astype(BF16)
    x[WIN:, :] = normalised(other[:WIN, :]).astype(BF16)
    counts = [part[WIN : WIN + 1, :1].astype(jnp.int32) for part in (own, other)]
    for copy in copies:
        copy.wait()
    for head in range(8):
        both = whole(weight, head)
        packed = dot(x[...], both[:, : 3 * HD]).astype(BF16)
        for w in range(2):
            blend[w * WIN : (w + 1) * WIN, head * HD : (head + 1) * HD] = attend(
                packed[w * WIN : (w + 1) * WIN], counts[w]
            )
        proj[:, head * HD : (head + 1) * HD] = both[:, 3 * HD :]
    out[...] = dot_t(blend[...], proj[...]).astype(BF16).reshape(out.shape)


def coarse_attention(place, own, other, parts):
    return pl.pallas_call(
        coarse_attention_kernel,
        out_shape=jax.ShapeDtypeStruct((2, WIN, 2 * C), BF16),
        in_specs=[pl.BlockSpec(memory_space=pltpu.SMEM)]
        + vmem(2)
        + [pl.BlockSpec(memory_space=pl.ANY)] * 4,
        out_specs=pl.BlockSpec(memory_space=pltpu.VMEM),
        scratch_shapes=[
            pltpu.VMEM((2, 4, 2, 4, 128, 256), BF16),
            pltpu.VMEM((2 * WIN, 2 * C), BF16),
            pltpu.VMEM((2 * WIN, C), BF16),
            pltpu.VMEM((2 * C, C), BF16),
            pltpu.SemaphoreType.DMA((16,)),
        ],
        compiler_params=params(24),
        cost_estimate=pl.CostEstimate(flops=1_400_000_000, bytes_accessed=7_000_000, transcendentals=400_000),
        name="coarse_attention",
    )(place, own, other, *parts)


def coarse_mlp_kernel(
    place, own, other, sent, came, u0, u1, u2, u3, d0, d1, d2, d3, base, give, up, down, x, hid, sems, late_sems
):
    copies = fetch_turned(place, (u0, u1, u2, u3), up, sems)
    late = fetch_down(place, (d0, d1, d2, d3), down, late_sems)
    mid = own[:WIN, :] + (sent[0].astype(F32) + came[1].astype(F32))
    base[...] = mid
    x[:WIN, :] = normalised(mid).astype(BF16)
    x[WIN:, :] = normalised(other[:WIN, :] + (sent[1].astype(F32) + came[0].astype(F32))).astype(BF16)
    for copy in copies:
        copy.wait()
    for h in range(8):
        hid[h] = gelu(dot(x[...], whole(up, h))).astype(BF16)
    for copy in late:
        copy.wait()
    result = dot_t(hid[0], whole(down, 0))
    for h in range(1, 8):
        result = result + dot_t(hid[h], whole(down, h))
    base[...] += result[:WIN]
    give[...] = result[WIN:].astype(BF16)


def coarse_mlp(place, own, other, sent, came, ups, downs):
    return pl.pallas_call(
        coarse_mlp_kernel,
        out_shape=(
            jax.ShapeDtypeStruct((WIN, 2 * C), F32),
            jax.ShapeDtypeStruct((WIN, 2 * C), BF16),
        ),
        in_specs=[pl.BlockSpec(memory_space=pltpu.SMEM)]
        + vmem(4)
        + [pl.BlockSpec(memory_space=pl.ANY)] * 8,
        out_specs=tuple(vmem(2)),
        scratch_shapes=[
            pltpu.VMEM((2, 4, 2, 4, 128, 256), BF16),
            pltpu.VMEM((2, 4, 2, 4, 128, 256), BF16),
            pltpu.VMEM((2 * WIN, 2 * C), BF16),
            pltpu.VMEM((8, 2 * WIN, 256), BF16),
            pltpu.SemaphoreType.DMA((16,)),
            pltpu.SemaphoreType.DMA((16,)),
        ],
        compiler_params=params(32),
        cost_estimate=pl.CostEstimate(flops=2_400_000_000, bytes_accessed=14_000_000, transcendentals=600_000),
        name="coarse_mlp",
    )(place, own, other, sent, came, *ups, *downs)


def tail_kernel(base, came, skip, expand, out_weight, out, lanes):
    coarse_out = (base[...] + came[...].astype(F32)).astype(BF16)
    for j in range(4):
        rows = dot(coarse_out, expand[:, j * C : (j + 1) * C]).astype(BF16)
        spread_rows = dot(rows, out_weight[C:, :])
        for k in range(4):
            lanes[k, pl.ds(j, WIN, stride=4), :] = spread_rows[:, k * 128 : (k + 1) * 128]
    for k in range(4):
        at = slice(k * 128, (k + 1) * 128)
        out[:, at] = skip[:, at] + lanes[k]


def tail(base, came, skip, expand, out_weight):
    return pl.pallas_call(
        tail_kernel,
        out_shape=jax.ShapeDtypeStruct(skip.shape, F32),
        in_specs=vmem(5),
        out_specs=pl.BlockSpec(memory_space=pltpu.VMEM),
        scratch_shapes=[pltpu.VMEM((4, skip.shape[0], 128), F32)],
        compiler_params=params(20),
        cost_estimate=pl.CostEstimate(flops=900_000_000, bytes_accessed=8_000_000, transcendentals=0),
        name="tail",
    )(base, came, skip, expand, out_weight)


def body(
    fine_tokens,
    fine_shift,
    window_counts,
    fine_qkv,
    fine_proj,
    fine_up,
    fine_down,
    merge_weight,
    coarse_qkv,
    coarse_proj,
    coarse_up,
    coarse_down,
    expand_weight,
    out_weight,
):
    core = lax.axis_index("core")
    y = lax.axis_index("yhi") * 2 + lax.axis_index("ylo")
    place = jnp.stack([lax.axis_index("x"), y, lax.axis_index("z"), core]).astype(jnp.int32)
    normed, mine, theirs = prepare(
        place, fine_tokens, coarse_qkv, coarse_proj.T, coarse_up, coarse_down.T
    )
    got = core_swap(theirs)
    devices = lax.axis_size(AXES)
    up_one = [(i, (i + 1) % devices) for i in range(devices)]
    low = lax.ppermute(normed[-WIN:], AXES, up_one)
    high = lax.ppermute(normed[:WIN], AXES, [(b, a) for a, b in up_one])
    blocks = jnp.where(
        core == 0, jnp.concatenate([mine, got], axis=1), jnp.concatenate([got, mine], axis=1)
    )

    qu = arrange("qu", place, direct(blocks[:2], ("x", "y")))
    d = arrange("d", place, direct(blocks[2:], ("z", "z")))
    qu_two = direct(qu, ("y", "z"))
    d_two = jnp.stack([v[0] for v in direct(d, ("x", "x"))])
    q_two, u_two = (jnp.stack([v[unit] for v in qu_two]) for unit in range(2))
    q_two, u_two, d_two, low, high, normed = lax.optimization_barrier(
        (q_two, u_two, d_two, low, high, normed)
    )
    q_parts = direct(q_two, ("z", "x"))
    d_one = hopped(d_two, ("y", "y"), (1, -1))
    d_other = hopped(d_two, ("y", "y"), (-1, 1))

    mid = fine_attention(fine_shift, fine_tokens, normed, low, high, fine_qkv, fine_proj)
    skip, coarse = fine_mlp(place, window_counts, mid, fine_up, fine_down, merge_weight, out_weight)
    d_one, u_two, coarse = lax.optimization_barrier((d_one, u_two, coarse))
    d_far = hopped(d_one, ("y", "y"), (1, -1))
    u_parts = direct(u_two, ("z", "x"))
    other = core_swap(coarse)
    sent = coarse_attention(place, coarse, other, q_parts)
    came = core_swap(sent)
    base, give = coarse_mlp(
        place, coarse, other, sent, came, u_parts, (d_two, d_one, d_other, d_far)
    )
    return tail(base, core_swap(give), skip, expand_weight, out_weight)


def solution(mesh):
    wide = Mesh(mesh.devices.reshape(2, 4, 2, 2, 4), AXES)
    region, head = ("ylo", "z", "core"), ("yhi", "x")
    in_specs = (
        P(AXES, None),
        P(),
        P(region),
        P(),
        P(),
        P(),
        P(),
        P(),
        P(region, head),
        P(head, region),
        P(region, head),
        P(head, region),
        P(),
        P(),
    )
    return jax.shard_map(body, mesh=wide, in_specs=in_specs, out_specs=P(AXES, None), check_vma=False)
```

time: 258 us -> 118 us (0.46)
  matrix products: 60.8 us -> 0 us
  waiting for transfers between devices: 82.4 us -> 27.2 us
  Pallas kernels: 0 us -> 42.5 us
  blocking collectives: 36.9 us -> 0 us
  local copies, waits for them, and re-layouts: 38 us -> 4.69 us
  starting transfers between devices: 10 us -> 41.7 us
  between operations: 14.3 us -> 1.16 us
  other arithmetic: 13.6 us -> 0.54 us
    all_gather x1 -> x0, waiting for transfers between devices: 75.4 us -> none  [turned_gather(): lax.all_gather(both, axis, axis=0, tiled=True)]
    dot_general x10 -> x0, matrix products: 53 us -> none  [the longest x1 14.3 us: body(): jnp.dot(fine_hidden, fine_down, preferred_element_type=jnp.float32)]
    pallas_call x0 -> x8, Pallas kernels: none -> 42.5 us  [the longest x1 14.3 us: coarse_attention(): pl.pallas_call(coarse_attention_kernel, out_shape=jax.ShapeDtypeStruct((2...]
    all_to_all x3 -> x0, blocking collectives: 36.9 us -> none  [from_everyone(): lax.all_to_all(jnp.broadcast_to(value[None], (devices, *value.shape)), ax...]
    ppermute x2 -> x27, starting transfers between devices: 6.51 us -> 41.7 us  [the longest x21 25.2 us: hopped(): return lax.ppermute(value, AXES, pairs)]
    ppermute x2 -> x27, waiting for transfers between devices: 1.22 us -> 27.2 us  [the longest x21 24.7 us: hopped(): return lax.ppermute(value, AXES, pairs)]
    slice x3 -> x7, local copies, waits for them, and re-layouts: 15.2 us -> 0.18 us  [the longest x4 0.14 us: body(): q_two, u_two = (jnp.stack([v[unit] for v in qu_two]) for unit in range(2))]
    convert_element_type x2 -> x0, local copies, waits for them, and re-layouts: 7.19 us -> none  [the longest x1 4.51 us: window_attention(): packed = jnp.einsum('nc,chj->hnj', normed, weight_heads, preferred_elemen...]
  transfers between devices with their start and end apart: 4 -> 27, of which waited for: 3 -> 9; matrix products, arithmetic and copies ran while one was open for 20% -> 0% of each run, Pallas kernels for 0% -> 26%
where the time goes in v1:
time: 118 us
  Pallas kernels  42.5 us (36%)
  starting transfers between devices  41.7 us (35%)
  waiting for transfers between devices  27.2 us (23%)
  local copies, waits for them, and re-layouts  4.69 us (4%)
    ppermute x21, starting transfers between devices, hopped(): return lax.ppermute(value, AXES, pairs)  25.2 us
    ppermute x21, waiting for transfers between devices, hopped(): return lax.ppermute(value, AXES, pairs)  24.7 us
    pallas_call x1, Pallas kernels, coarse_attention(): pl.pallas_call(coarse_attention_kernel, out_shape=jax.ShapeDtypeStruct((2...  14.3 us
    pallas_call x1, Pallas kernels, fine_attention(): pl.pallas_call(fine_attention_kernel, out_shape=jax.ShapeDtypeStruct((row...  11 us
    ppermute x1, starting transfers between devices, body(): high = lax.ppermute(normed[:WIN], AXES, [(b, a) for a, b in up_one])  9.36 us
    pallas_call x1, Pallas kernels, coarse_mlp(): pl.pallas_call(coarse_mlp_kernel, out_shape=(jax.ShapeDtypeStruct((WIN, 2...  7.81 us
    ppermute x4, starting transfers between devices, core_swap(): return lax.ppermute(value, 'core', [(0, 1), (1, 0)])  7.14 us
    pallas_call x1, Pallas kernels, fine_mlp(): pl.pallas_call(fine_mlp_kernel, out_shape=(jax.ShapeDtypeStruct((rows, C)...  4.61 us
  transfers between devices with their start and end apart: 27, of which 9 were waited for; matrix products, arithmetic and copies ran while one was open for 0% of the time, Pallas kernels for 26%

profile of v1, /device:TPU:1, one launch (start us, length us, event | category | flops | bytes accessed | tf_op | source)
XLA Modules:
  0.0 117.8 jit_solution(633465765218971736)
XLA Ops:
  0.1 1.3 %copy-done.1 = f32[576,512]{1,0:T(8,128)S(1)} copy-done((f32[576,512]{1,0:T(8,128)S(1)}, f32[576,512]{1,0:T(8,128)}, u32[]{:S(2)}) %copy-start.1) | copy-done | bytes 1179672
  5.4 1.5 %collective-permute-start = (bf16[3,64,256]{2,1,0:T(8,128)(2,1)S(1)}, bf16[3,64,256]{2,1,0:T(8,128)(2,1)S(1)}, u32[]{:S(2)}, u32[]{:S(2)}) collective-permute-start(bf16[3,64,256]{2,1,0:T(8,128)(2,1)S(1)} %get-tuple-element.22), channel_id=1, source_target_pairs={{0,8},{8,0},{1,9},{9,1},{2,10},{10,2},{3,11},{11,3},{4,12},{12,4},... | collective-permute-start | bytes 294920 | tf_op jit(solution)/shard_map/ppermute | solution.py:40
  8.0 3.8 %collective-permute-start.9 = (bf16[1,128,256]{2,1,0:T(8,128)(2,1)S(1)}, bf16[1,128,256]{2,1,0:T(8,128)(2,1)S(1)}, u32[]{:S(2)}, u32[]{:S(2)}) collective-permute-start(bf16[1,128,256]{2,1,0:T(8,128)(2,1)S(1)} %slice.57.refs_1_), channel_id=1, source_target_pairs={{0,32},{1,33},{2,34},{3,35},{4,36},{5,37},{6,38},{7,39},{8,40},{9,... | collective-permute-start | bytes 196616 | tf_op jit(solution)/shard_map/ppermute | solution.py:32
  11.7 3.0 %collective-permute-start.3 = (bf16[2,128,256]{2,1,0:T(8,128)(2,1)S(1)}, bf16[2,128,256]{2,1,0:T(8,128)(2,1)S(1)}, u32[]{:S(2)}, u32[]{:S(2)}) collective-permute-start(bf16[2,128,256]{2,1,0:T(8,128)(2,1)S(1)} %slice.48.refs_1_), channel_id=1, source_target_pairs={{0,2},{1,3},{2,0},{3,1},{4,6},{5,7},{6,4},{7,5},{8,12},{9,13},{10,... | collective-permute-start | bytes 393224 | tf_op jit(solution)/shard_map/ppermute | solution.py:32
  16.6 1.0 collective-permute-start.7
  17.7 1.9 %collective-permute-done.8.refs_3_ = bf16[1,128,256]{2,1,0:T(8,128)(2,1)S(1)} collective-permute-done((bf16[1,128,256]{2,1,0:T(8,128)(2,1)S(1)}, bf16[1,128,256]{2,1,0:T(8,128)(2,1)S(1)}, u32[]{:S(2)}, u32[]{:S(2)}) %collective-permute-start.8) | collective-permute-done | bytes 65568 | tf_op jit(solution)/shard_map/ppermute | solution.py:32
  19.6 1.6 %collective-permute-done.7.refs_2_ = bf16[1,128,256]{2,1,0:T(8,128)(2,1)S(1)} collective-permute-done((bf16[1,128,256]{2,1,0:T(8,128)(2,1)S(1)}, bf16[1,128,256]{2,1,0:T(8,128)(2,1)S(1)}, u32[]{:S(2)}, u32[]{:S(2)}) %collective-permute-start.7) | collective-permute-done | bytes 65568 | tf_op jit(solution)/shard_map/ppermute | solution.py:32
  21.8 2.9 %collective-permute-start.12 = (bf16[1,4,128,256]{3,2,1,0:T(8,128)(2,1)S(1)}, bf16[1,4,128,256]{3,2,1,0:T(8,128)(2,1)S(1)}, u32[]{:S(2)}, u32[]{:S(2)}) collective-permute-start(bf16[1,4,128,256]{3,2,1,0:T(8,128)(2,1)S(1)} %arrange_d.1), channel_id=1, source_target_pairs={{0,2},{1,3},{2,0},{3,1},{4,6},{5,7},{6,4},{7,5},{8,10},{9,11},{10,... | collective-permute-start | bytes 786440 | tf_op jit(solution)/shard_map/ppermute | solution.py:32
  27.8 1.4 %collective-permute-start.5 = (bf16[2,4,128,256]{3,2,1,0:T(8,128)(2,1)S(1)}, bf16[2,4,128,256]{3,2,1,0:T(8,128)(2,1)S(1)}, u32[]{:S(2)}, u32[]{:S(2)}) collective-permute-start(bf16[2,4,128,256]{3,2,1,0:T(8,128)(2,1)S(1)} %arrange_qu.1), channel_id=1, source_target_pairs={{0,68},{1,69},{2,70},{3,71},{4,64},{5,65},{6,66},{7,67},{8,56},{9,... | collective-permute-start | bytes 1572872 | tf_op jit(solution)/shard_map/ppermute | solution.py:32
  30.1 9.4 %collective-permute-start.14 = (bf16[144,512]{1,0:T(8,128)(2,1)S(1)}, bf16[144,512]{1,0:T(8,128)(2,1)S(1)}, u32[]{:S(2)}, u32[]{:S(2)}) collective-permute-start(bf16[144,512]{1,0:T(8,128)(2,1)S(1)} %get-tuple-element.37), channel_id=1, source_target_pairs={{1,0},{2,1},{3,2},{4,3},{5,4},{6,5},{7,6},{8,7},{9,8},{10,9},{11,1... | collective-permute-start | bytes 442376 | tf_op jit(solution)/shard_map/ppermute | solution.py:420
  39.8 10.9 %collective-permute-done.4 = bf16[2,4,128,256]{3,2,1,0:T(8,128)(2,1)S(1)} collective-permute-done((bf16[2,4,128,256]{3,2,1,0:T(8,128)(2,1)S(1)}, bf16[2,4,128,256]{3,2,1,0:T(8,128)(2,1)S(1)}, u32[]{:S(2)}, u32[]{:S(2)}) %collective-permute-start.4) | collective-permute-done | bytes 524320 | tf_op jit(solution)/shard_map/ppermute | solution.py:32
  52.8 1.8 %collective-permute-start.18 = (bf16[4,4,128,256]{3,2,1,0:T(8,128)(2,1)S(1)}, bf16[4,4,128,256]{3,2,1,0:T(8,128)(2,1)S(1)}, u32[]{:S(2)}, u32[]{:S(2)}) collective-permute-start(bf16[4,4,128,256]{3,2,1,0:T(8,128)(2,1)S(1)} %get-tuple-element.31.a0), channel_id=1, source_target_pairs={{0,48},{1,49},{2,50},{3,51},{4,52},{5,53},{6,54},{7,55},{8,11},{9,... | collective-permute-start | bytes 3145736 | tf_op jit(solution)/shard_map/ppermute | solution.py:32
  55.1 11.0 %fine_attention.1.mid = f32[576,512]{1,0:T(8,128)S(1)} custom-call(s32[1]{0:T(128)S(6)} %copy.15.offset, f32[576,512]{1,0:T(8,128)S(1)} %copy-done.2, bf16[576,512]{1,0:T(8,128)(2,1)S(1)} %get-tuple-element.26.normed, bf16[144,512]{1,0:T(8,128)(2,1)S(1)} %collective-permute-done.13.low, bf16[144,512]{1,0:T(8,128)(2,1)S(1)} %collective-permute-done.14.high, ...), custom_call_target="tpu_custom_call" | custom-call | flops 2500000000 | bytes 6000000 | tf_op jit(solution)/shard_map/fine_attention/pallas_call | solution.py:170
  66.2 4.6 %fine_mlp.1 = (f32[576,512]{1,0:T(8,128)S(1)}, f32[152,1024]{1,0:T(8,128)S(1)}) custom-call(s32[4]{0:T(128)S(1)} %pad_add_fusion.place.refs_0_, s32[8]{0:T(128)S(1)} %copy-done.13, f32[576,512]{1,0:T(8,128)S(1)} %fine_attention.1.mid, bf16[512,2048]{1,0:T(8,128)(2,1)S(1)} %copy-done.9, bf16[2048,512]{1,0:T(8,128)(2,1)S(1)} %copy-done.10, ...), custom_call_target="tpu_custom_call" | custom-call | flops 3500000000 | bytes 12000000 | tf_op jit(solution)/shard_map/fine_mlp/pallas_call | solution.py:215
  70.8 2.3 %collective-permute-start.16 = (f32[152,1024]{1,0:T(8,128)S(1)}, f32[152,1024]{1,0:T(8,128)S(1)}, u32[]{:S(2)}, u32[]{:S(2)}) collective-permute-start(f32[152,1024]{1,0:T(8,128)S(1)} %get-tuple-element.30.own), channel_id=1, source_target_pairs={{0,8},{8,0},{1,9},{9,1},{2,10},{10,2},{3,11},{11,3},{4,12},{12,4},... | collective-permute-start | bytes 1867784 | tf_op jit(solution)/shard_map/ppermute | solution.py:40
  73.3 2.6 %collective-permute-start.25 = (bf16[4,4,128,256]{3,2,1,0:T(8,128)(2,1)S(1)}, bf16[4,4,128,256]{3,2,1,0:T(8,128)(2,1)S(1)}, u32[]{:S(2)}, u32[]{:S(2)}) collective-permute-start(bf16[4,4,128,256]{3,2,1,0:T(8,128)(2,1)S(1)} %collective-permute-done.15.d1), channel_id=1, source_target_pairs={{0,64},{1,65},{2,66},{3,67},{4,68},{5,69},{6,70},{7,71},{8,76},{9,... | collective-permute-start | bytes 3145736 | tf_op jit(solution)/shard_map/ppermute | solution.py:32
  75.9 3.0 %collective-permute-done.18.a2 = bf16[4,4,128,256]{3,2,1,0:T(8,128)(2,1)S(1)} collective-permute-done((bf16[4,4,128,256]{3,2,1,0:T(8,128)(2,1)S(1)}, bf16[4,4,128,256]{3,2,1,0:T(8,128)(2,1)S(1)}, u32[]{:S(2)}, u32[]{:S(2)}) %collective-permute-start.18) | collective-permute-done | bytes 1048608 | tf_op jit(solution)/shard_map/ppermute | solution.py:32
  79.5 1.7 %collective-permute-start.22 = (bf16[4,4,128,256]{3,2,1,0:T(8,128)(2,1)S(1)}, bf16[4,4,128,256]{3,2,1,0:T(8,128)(2,1)S(1)}, u32[]{:S(2)}, u32[]{:S(2)}) collective-permute-start(bf16[4,4,128,256]{3,2,1,0:T(8,128)(2,1)S(1)} %get-tuple-element.32.u0), channel_id=1, source_target_pairs={{0,48},{1,49},{2,50},{3,51},{4,52},{5,53},{6,54},{7,55},{8,11},{9,... | collective-permute-start | bytes 3145736 | tf_op jit(solution)/shard_map/ppermute | solution.py:32
  81.7 14.3 %coarse_attention.1.sent = bf16[2,144,1024]{2,1,0:T(8,128)(2,1)S(1)} custom-call(s32[4]{0:T(128)S(1)} %pad_add_fusion.place.refs_0_, f32[152,1024]{1,0:T(8,128)S(1)} %get-tuple-element.30.own, f32[152,1024]{1,0:T(8,128)S(1)} %collective-permute-done.16.other, bf16[4,4,128,256]{3,2,1,0:T(8,128)(2,1)S(1)} %get-tuple-element.31.a0, ...), custom_call_target="tpu_custom_call" | custom-call | flops 1400000000 | bytes 7000000 | tf_op jit(solution)/shard_map/coarse_attention/pallas_call | solution.py:302
  96.0 3.2 %collective-permute-start.20 = (bf16[2,144,1024]{2,1,0:T(8,128)(2,1)S(1)}, bf16[2,144,1024]{2,1,0:T(8,128)(2,1)S(1)}, u32[]{:S(2)}, u32[]{:S(2)}) collective-permute-start(bf16[2,144,1024]{2,1,0:T(8,128)(2,1)S(1)} %coarse_attention.1.sent), channel_id=1, source_target_pairs={{0,8},{8,0},{1,9},{9,1},{2,10},{10,2},{3,11},{11,3},{4,12},{12,4},... | collective-permute-start | bytes 1769480 | tf_op jit(solution)/shard_map/ppermute | solution.py:40
  99.2 6.1 %collective-permute-done.22.u2 = bf16[4,4,128,256]{3,2,1,0:T(8,128)(2,1)S(1)} collective-permute-done((bf16[4,4,128,256]{3,2,1,0:T(8,128)(2,1)S(1)}, bf16[4,4,128,256]{3,2,1,0:T(8,128)(2,1)S(1)}, u32[]{:S(2)}, u32[]{:S(2)}) %collective-permute-start.22) | collective-permute-done | bytes 1048608 | tf_op jit(solution)/shard_map/ppermute | solution.py:32
  105.6 7.8 %coarse_mlp.1 = (f32[144,1024]{1,0:T(8,128)S(1)}, bf16[144,1024]{1,0:T(8,128)(2,1)S(1)}) custom-call(s32[4]{0:T(128)S(1)} %pad_add_fusion.place.refs_0_, f32[152,1024]{1,0:T(8,128)S(1)} %get-tuple-element.30.own, f32[152,1024]{1,0:T(8,128)S(1)} %collective-permute-done.16.other, bf16[2,144,1024]{2,1,0:T(8,128)(2,1)S(1)} %coarse_attention.1.sent, ...), custom_call_target="tpu_custom_call" | custom-call | flops 2400000000 | bytes 14000000 | tf_op jit(solution)/shard_map/coarse_mlp/pallas_call | solution.py:345
  113.5 1.6 %collective-permute-done.26.came = bf16[144,1024]{1,0:T(8,128)(2,1)S(1)} collective-permute-done((bf16[144,1024]{1,0:T(8,128)(2,1)S(1)}, bf16[144,1024]{1,0:T(8,128)(2,1)S(1)}, u32[]{:S(2)}, u32[]{:S(2)}) %collective-permute-start.26) | collective-permute-done | bytes 294944 | tf_op jit(solution)/shard_map/ppermute | solution.py:40
  115.0 2.7 %tail.1 = f32[576,512]{1,0:T(8,128)} custom-call(f32[144,1024]{1,0:T(8,128)S(1)} %get-tuple-element.34.base, bf16[144,1024]{1,0:T(8,128)(2,1)S(1)} %collective-permute-done.26.came, f32[576,512]{1,0:T(8,128)S(1)} %get-tuple-element.36.skip, bf16[1024,2048]{1,0:T(8,128)(2,1)S(1)} %copy-done, bf16[1024,512]{1,0:T(8,128)(2,1)S(1)} %copy-done.3), custom_call_target="tpu_custom_call" | custom-call | flops 900000000 | bytes 8000000 | tf_op jit(solution)/shard_map/tail/pallas_call | solution.py:382
  (77 shorter events, 15.2 us)
Async XLA Ops:
  8.0 8.7 %collective-permute-start.9 = (bf16[1,128,256]{2,1,0:T(8,128)(2,1)S(1)}, bf16[1,128,256]{2,1,0:T(8,128)(2,1)S(1)}, u32[]{:S(2)}, u32[]{:S(2)}) collective-permute-start(bf16[1,128,256]{2,1,0:T(8,128)(2,1)S(1)} %slice.57.refs_1_), channel_id=1, source_target_pairs={{0,32},{1,33},{2,34},{3,35},{4,36},{5,37},{6,38},{7,39},{8,40},{9,... | collective-permute-start | bytes 196616 | tf_op jit(solution)/shard_map/ppermute | solution.py:32
  11.7 13.5 %collective-permute-start.3 = (bf16[2,128,256]{2,1,0:T(8,128)(2,1)S(1)}, bf16[2,128,256]{2,1,0:T(8,128)(2,1)S(1)}, u32[]{:S(2)}, u32[]{:S(2)}) collective-permute-start(bf16[2,128,256]{2,1,0:T(8,128)(2,1)S(1)} %slice.48.refs_1_), channel_id=1, source_target_pairs={{0,2},{1,3},{2,0},{3,1},{4,6},{5,7},{6,4},{7,5},{8,12},{9,13},{10,... | collective-permute-start | bytes 393224 | tf_op jit(solution)/shard_map/ppermute | solution.py:32
  14.7 11.5 %collective-permute-start.2 = (bf16[2,128,256]{2,1,0:T(8,128)(2,1)S(1)}, bf16[2,128,256]{2,1,0:T(8,128)(2,1)S(1)}, u32[]{:S(2)}, u32[]{:S(2)}) collective-permute-start(bf16[2,128,256]{2,1,0:T(8,128)(2,1)S(1)} %slice.48.refs_1_), channel_id=1, source_target_pairs={{0,3},{1,0},{2,1},{3,2},{4,7},{5,4},{6,5},{7,6},{8,76},{9,77},{10,... | collective-permute-start | bytes 393224 | tf_op jit(solution)/shard_map/ppermute | solution.py:32
  15.5 10.7 %collective-permute-start.1 = (bf16[2,128,256]{2,1,0:T(8,128)(2,1)S(1)}, bf16[2,128,256]{2,1,0:T(8,128)(2,1)S(1)}, u32[]{:S(2)}, u32[]{:S(2)}) collective-permute-start(bf16[2,128,256]{2,1,0:T(8,128)(2,1)S(1)} %slice.48.refs_1_), channel_id=1, source_target_pairs={{0,1},{1,2},{2,3},{3,0},{4,5},{5,6},{6,7},{7,4},{8,72},{9,73},{10,... | collective-permute-start | bytes 393224 | tf_op jit(solution)/shard_map/ppermute | solution.py:32
  16.6 4.6 %collective-permute-start.7 = (bf16[1,128,256]{2,1,0:T(8,128)(2,1)S(1)}, bf16[1,128,256]{2,1,0:T(8,128)(2,1)S(1)}, u32[]{:S(2)}, u32[]{:S(2)}) collective-permute-start(bf16[1,128,256]{2,1,0:T(8,128)(2,1)S(1)} %slice.57.refs_1_), channel_id=1, source_target_pairs={{0,16},{1,17},{2,18},{3,19},{4,20},{5,21},{6,22},{7,23},{8,24},{9,... | collective-permute-start | bytes 196616 | tf_op jit(solution)/shard_map/ppermute | solution.py:32
  21.8 8.3 %collective-permute-start.12 = (bf16[1,4,128,256]{3,2,1,0:T(8,128)(2,1)S(1)}, bf16[1,4,128,256]{3,2,1,0:T(8,128)(2,1)S(1)}, u32[]{:S(2)}, u32[]{:S(2)}) collective-permute-start(bf16[1,4,128,256]{3,2,1,0:T(8,128)(2,1)S(1)} %arrange_d.1), channel_id=1, source_target_pairs={{0,2},{1,3},{2,0},{3,1},{4,6},{5,7},{6,4},{7,5},{8,10},{9,11},{10,... | collective-permute-start | bytes 786440 | tf_op jit(solution)/shard_map/ppermute | solution.py:32
  24.7 14.8 %collective-permute-start.11 = (bf16[1,4,128,256]{3,2,1,0:T(8,128)(2,1)S(1)}, bf16[1,4,128,256]{3,2,1,0:T(8,128)(2,1)S(1)}, u32[]{:S(2)}, u32[]{:S(2)}) collective-permute-start(bf16[1,4,128,256]{3,2,1,0:T(8,128)(2,1)S(1)} %arrange_d.1), channel_id=1, source_target_pairs={{0,3},{1,0},{2,1},{3,2},{4,7},{5,4},{6,5},{7,6},{8,11},{9,8},{10,9... | collective-permute-start | bytes 786440 | tf_op jit(solution)/shard_map/ppermute | solution.py:32
  25.2 14.3 %collective-permute-start.10 = (bf16[1,4,128,256]{3,2,1,0:T(8,128)(2,1)S(1)}, bf16[1,4,128,256]{3,2,1,0:T(8,128)(2,1)S(1)}, u32[]{:S(2)}, u32[]{:S(2)}) collective-permute-start(bf16[1,4,128,256]{3,2,1,0:T(8,128)(2,1)S(1)} %arrange_d.1), channel_id=1, source_target_pairs={{0,1},{1,2},{2,3},{3,0},{4,5},{5,6},{6,7},{7,4},{8,9},{9,10},{10,1... | collective-permute-start | bytes 786440 | tf_op jit(solution)/shard_map/ppermute | solution.py:32
  26.8 12.9 %collective-permute-start.6 = (bf16[2,4,128,256]{3,2,1,0:T(8,128)(2,1)S(1)}, bf16[2,4,128,256]{3,2,1,0:T(8,128)(2,1)S(1)}, u32[]{:S(2)}, u32[]{:S(2)}) collective-permute-start(bf16[2,4,128,256]{3,2,1,0:T(8,128)(2,1)S(1)} %arrange_qu.1), channel_id=1, source_target_pairs={{0,4},{1,5},{2,6},{3,7},{4,0},{5,1},{6,2},{7,3},{8,40},{9,41},{10,... | collective-permute-start | bytes 1572872 | tf_op jit(solution)/shard_map/ppermute | solution.py:32
  27.8 12.0 %collective-permute-start.5 = (bf16[2,4,128,256]{3,2,1,0:T(8,128)(2,1)S(1)}, bf16[2,4,128,256]{3,2,1,0:T(8,128)(2,1)S(1)}, u32[]{:S(2)}, u32[]{:S(2)}) collective-permute-start(bf16[2,4,128,256]{3,2,1,0:T(8,128)(2,1)S(1)} %arrange_qu.1), channel_id=1, source_target_pairs={{0,68},{1,69},{2,70},{3,71},{4,64},{5,65},{6,66},{7,67},{8,56},{9,... | collective-permute-start | bytes 1572872 | tf_op jit(solution)/shard_map/ppermute | solution.py:32
  30.1 20.9 %collective-permute-start.14 = (bf16[144,512]{1,0:T(8,128)(2,1)S(1)}, bf16[144,512]{1,0:T(8,128)(2,1)S(1)}, u32[]{:S(2)}, u32[]{:S(2)}) collective-permute-start(bf16[144,512]{1,0:T(8,128)(2,1)S(1)} %get-tuple-element.37), channel_id=1, source_target_pairs={{1,0},{2,1},{3,2},{4,3},{5,4},{6,5},{7,6},{8,7},{9,8},{10,9},{11,1... | collective-permute-start | bytes 442376 | tf_op jit(solution)/shard_map/ppermute | solution.py:420
  39.5 11.5 %collective-permute-start.13 = (bf16[144,512]{1,0:T(8,128)(2,1)S(1)}, bf16[144,512]{1,0:T(8,128)(2,1)S(1)}, u32[]{:S(2)}, u32[]{:S(2)}) collective-permute-start(bf16[144,512]{1,0:T(8,128)(2,1)S(1)} %get-tuple-element.38), channel_id=1, source_target_pairs={{0,1},{1,2},{2,3},{3,4},{4,5},{5,6},{6,7},{7,8},{8,9},{9,10},{10,1... | collective-permute-start | bytes 442376 | tf_op jit(solution)/shard_map/ppermute | solution.py:419
  39.5 11.2 %collective-permute-start.4 = (bf16[2,4,128,256]{3,2,1,0:T(8,128)(2,1)S(1)}, bf16[2,4,128,256]{3,2,1,0:T(8,128)(2,1)S(1)}, u32[]{:S(2)}, u32[]{:S(2)}) collective-permute-start(bf16[2,4,128,256]{3,2,1,0:T(8,128)(2,1)S(1)} %arrange_qu.1), channel_id=1, source_target_pairs={{0,64},{1,65},{2,66},{3,67},{4,68},{5,69},{6,70},{7,71},{8,24},{9,... | collective-permute-start | bytes 1572872 | tf_op jit(solution)/shard_map/ppermute | solution.py:32
  51.0 19.8 %collective-permute-start.15 = (bf16[4,4,128,256]{3,2,1,0:T(8,128)(2,1)S(1)}, bf16[4,4,128,256]{3,2,1,0:T(8,128)(2,1)S(1)}, u32[]{:S(2)}, u32[]{:S(2)}) collective-permute-start(bf16[4,4,128,256]{3,2,1,0:T(8,128)(2,1)S(1)} %pad_maximum_fusion.2.d0), channel_id=1, source_target_pairs={{0,64},{1,65},{2,66},{3,67},{4,68},{5,69},{6,70},{7,71},{8,76},{9,... | collective-permute-start | bytes 3145736 | tf_op jit(solution)/shard_map/ppermute | solution.py:32
  52.0 21.3 %collective-permute-start.19 = (bf16[4,4,128,256]{3,2,1,0:T(8,128)(2,1)S(1)}, bf16[4,4,128,256]{3,2,1,0:T(8,128)(2,1)S(1)}, u32[]{:S(2)}, u32[]{:S(2)}) collective-permute-start(bf16[4,4,128,256]{3,2,1,0:T(8,128)(2,1)S(1)} %get-tuple-element.31.a0), channel_id=1, source_target_pairs={{0,32},{1,33},{2,34},{3,35},{4,36},{5,37},{6,38},{7,39},{8,10},{9,... | collective-permute-start | bytes 3145736 | tf_op jit(solution)/shard_map/ppermute | solution.py:32
  52.8 26.0 %collective-permute-start.18 = (bf16[4,4,128,256]{3,2,1,0:T(8,128)(2,1)S(1)}, bf16[4,4,128,256]{3,2,1,0:T(8,128)(2,1)S(1)}, u32[]{:S(2)}, u32[]{:S(2)}) collective-permute-start(bf16[4,4,128,256]{3,2,1,0:T(8,128)(2,1)S(1)} %get-tuple-element.31.a0), channel_id=1, source_target_pairs={{0,48},{1,49},{2,50},{3,51},{4,52},{5,53},{6,54},{7,55},{8,11},{9,... | collective-permute-start | bytes 3145736 | tf_op jit(solution)/shard_map/ppermute | solution.py:32
  54.6 24.9 %collective-permute-start.17 = (bf16[4,4,128,256]{3,2,1,0:T(8,128)(2,1)S(1)}, bf16[4,4,128,256]{3,2,1,0:T(8,128)(2,1)S(1)}, u32[]{:S(2)}, u32[]{:S(2)}) collective-permute-start(bf16[4,4,128,256]{3,2,1,0:T(8,128)(2,1)S(1)} %get-tuple-element.31.a0), channel_id=1, source_target_pairs={{0,16},{1,17},{2,18},{3,19},{4,20},{5,21},{6,22},{7,23},{8,9},{9,1... | collective-permute-start | bytes 3145736 | tf_op jit(solution)/shard_map/ppermute | solution.py:32
  70.8 10.4 %collective-permute-start.16 = (f32[152,1024]{1,0:T(8,128)S(1)}, f32[152,1024]{1,0:T(8,128)S(1)}, u32[]{:S(2)}, u32[]{:S(2)}) collective-permute-start(f32[152,1024]{1,0:T(8,128)S(1)} %get-tuple-element.30.own), channel_id=1, source_target_pairs={{0,8},{8,0},{1,9},{9,1},{2,10},{10,2},{3,11},{11,3},{4,12},{12,4},... | collective-permute-start | bytes 1867784 | tf_op jit(solution)/shard_map/ppermute | solution.py:40
  73.1 22.9 %collective-permute-start.24 = (bf16[4,4,128,256]{3,2,1,0:T(8,128)(2,1)S(1)}, bf16[4,4,128,256]{3,2,1,0:T(8,128)(2,1)S(1)}, u32[]{:S(2)}, u32[]{:S(2)}) collective-permute-start(bf16[4,4,128,256]{3,2,1,0:T(8,128)(2,1)S(1)} %pad_maximum_fusion.2.d0), channel_id=1, source_target_pairs={{0,68},{1,69},{2,70},{3,71},{4,64},{5,65},{6,66},{7,67},{8,72},{9,... | collective-permute-start | bytes 3145736 | tf_op jit(solution)/shard_map/ppermute | solution.py:32
  73.3 26.0 %collective-permute-start.25 = (bf16[4,4,128,256]{3,2,1,0:T(8,128)(2,1)S(1)}, bf16[4,4,128,256]{3,2,1,0:T(8,128)(2,1)S(1)}, u32[]{:S(2)}, u32[]{:S(2)}) collective-permute-start(bf16[4,4,128,256]{3,2,1,0:T(8,128)(2,1)S(1)} %collective-permute-done.15.d1), channel_id=1, source_target_pairs={{0,64},{1,65},{2,66},{3,67},{4,68},{5,69},{6,70},{7,71},{8,76},{9,... | collective-permute-start | bytes 3145736 | tf_op jit(solution)/shard_map/ppermute | solution.py:32
  78.9 20.4 %collective-permute-start.23 = (bf16[4,4,128,256]{3,2,1,0:T(8,128)(2,1)S(1)}, bf16[4,4,128,256]{3,2,1,0:T(8,128)(2,1)S(1)}, u32[]{:S(2)}, u32[]{:S(2)}) collective-permute-start(bf16[4,4,128,256]{3,2,1,0:T(8,128)(2,1)S(1)} %get-tuple-element.32.u0), channel_id=1, source_target_pairs={{0,32},{1,33},{2,34},{3,35},{4,36},{5,37},{6,38},{7,39},{8,10},{9,... | collective-permute-start | bytes 3145736 | tf_op jit(solution)/shard_map/ppermute | solution.py:32
  79.5 25.9 %collective-permute-start.22 = (bf16[4,4,128,256]{3,2,1,0:T(8,128)(2,1)S(1)}, bf16[4,4,128,256]{3,2,1,0:T(8,128)(2,1)S(1)}, u32[]{:S(2)}, u32[]{:S(2)}) collective-permute-start(bf16[4,4,128,256]{3,2,1,0:T(8,128)(2,1)S(1)} %get-tuple-element.32.u0), channel_id=1, source_target_pairs={{0,48},{1,49},{2,50},{3,51},{4,52},{5,53},{6,54},{7,55},{8,11},{9,... | collective-permute-start | bytes 3145736 | tf_op jit(solution)/shard_map/ppermute | solution.py:32
  81.2 24.3 %collective-permute-start.21 = (bf16[4,4,128,256]{3,2,1,0:T(8,128)(2,1)S(1)}, bf16[4,4,128,256]{3,2,1,0:T(8,128)(2,1)S(1)}, u32[]{:S(2)}, u32[]{:S(2)}) collective-permute-start(bf16[4,4,128,256]{3,2,1,0:T(8,128)(2,1)S(1)} %get-tuple-element.32.u0), channel_id=1, source_target_pairs={{0,16},{1,17},{2,18},{3,19},{4,20},{5,21},{6,22},{7,23},{8,9},{9,1... | collective-permute-start | bytes 3145736 | tf_op jit(solution)/shard_map/ppermute | solution.py:32
  96.0 9.5 %collective-permute-start.20 = (bf16[2,144,1024]{2,1,0:T(8,128)(2,1)S(1)}, bf16[2,144,1024]{2,1,0:T(8,128)(2,1)S(1)}, u32[]{:S(2)}, u32[]{:S(2)}) collective-permute-start(bf16[2,144,1024]{2,1,0:T(8,128)(2,1)S(1)} %coarse_attention.1.sent), channel_id=1, source_target_pairs={{0,8},{8,0},{1,9},{9,1},{2,10},{10,2},{3,11},{11,3},{4,12},{12,4},... | collective-permute-start | bytes 1769480 | tf_op jit(solution)/shard_map/ppermute | solution.py:40
  (17 other events, 106.9 us)

commit v2 on v1

--- a/solution.py
+++ b/solution.py
@@ -60,29 +60,58 @@
 
 
 def attend(packed, count):
-    queries = packed[:, :HD]
+    queries = packed[:, :HD] * jnp.asarray(HD ** (-0.5), BF16)
     keys = packed[:, HD : 2 * HD]
     values = packed[:, 2 * HD :]
-    scores = dot_t(queries, keys) * HD ** (-0.5)
+    scores = dot_t(queries, keys)
     if count is not None:
         position = lax.broadcasted_iota(jnp.int32, scores.shape, 1)
         scores = jnp.where(position < count, scores, -1e30)
     row_max = jnp.max(scores, axis=-1, keepdims=True)
     raised = jnp.exp(scores - row_max)
-    weights = (raised / jnp.sum(raised, axis=-1, keepdims=True)).astype(BF16)
-    return dot(weights, values).astype(BF16)
+    total = jnp.sum(raised, axis=-1, keepdims=True)
+    return (dot(raised.astype(BF16), values) * (1.0 / total)).astype(BF16)
 
 
 def vmem(count):
     return [pl.BlockSpec(memory_space=pltpu.VMEM)] * count
 
 
+def cost(us):
+    return pl.CostEstimate(flops=int(us * 1_150_000_000), bytes_accessed=0, transcendentals=0)
+
+
 def params(mib):
     return pltpu.CompilerParams(vmem_limit_bytes=mib * MIB)
 
 
-def prepare_kernel(place, tokens, qkv, proj_t, up, down_t, normed, mine, theirs):
+def norm_kernel(tokens, normed):
     normed[...] = normalised(tokens[...]).astype(BF16)
+
+
+def norm(tokens):
+    return pl.pallas_call(
+        norm_kernel,
+        out_shape=jax.ShapeDtypeStruct(tokens.shape, BF16),
+        in_specs=vmem(1),
+        out_specs=pl.BlockSpec(memory_space=pltpu.VMEM),
+        compiler_params=params(8),
+        cost_estimate=cost(1.0),
+        name="norm",
+    )(tokens)
+
+
+def prepare_kernel(place, *refs):
+    sources, (mine, theirs), held, sems = refs[:4], refs[4:6], refs[6:10], refs[10]
+    copies = [
+        pltpu.make_async_copy(source, target, sems.at[i])
+        for i, (source, target) in enumerate(zip(sources, held))
+    ]
+    for copy in copies:
+        copy.start()
+    for copy in copies:
+        copy.wait()
+    qkv, proj_t, up, down_t = held
     halves = [
         (
             jnp.concatenate(
@@ -102,40 +131,44 @@
                 theirs[unit] = halves[1 - core][unit]
 
 
-def prepare(place, tokens, qkv, proj_t, up, down_t):
+def prepare(place, qkv, proj_t, up, down_t):
     part = jax.ShapeDtypeStruct((3, 64, 256), BF16)
+    arrays = (qkv, proj_t, up, down_t)
     return pl.pallas_call(
         prepare_kernel,
-        out_shape=(jax.ShapeDtypeStruct(tokens.shape, BF16), part, part),
-        in_specs=[pl.BlockSpec(memory_space=pltpu.SMEM)] + vmem(5),
-        out_specs=tuple(vmem(3)),
-        compiler_params=params(8),
-        cost_estimate=pl.CostEstimate(flops=3_000_000, bytes_accessed=2_500_000, transcendentals=0),
+        out_shape=(part, part),
+        in_specs=[pl.BlockSpec(memory_space=pltpu.SMEM)]
+        + [pl.BlockSpec(memory_space=pltpu.HBM)] * 4,
+        out_specs=tuple(vmem(2)),
+        scratch_shapes=[pltpu.VMEM(v.shape, v.dtype) for v in arrays]
+        + [pltpu.SemaphoreType.DMA((4,))],
+        compiler_params=params(60),
+        cost_estimate=cost(1.5),
         name="prepare",
-    )(place, tokens, qkv, proj_t, up, down_t)
-
-
-def arrange_kernel(kind, place, own, r1, r2, r3, out):
-    if kind == "d":
-        here = place[2]
-    else:
-        here = jnp.where(place[3] == 0, place[0], place[1])
+    )(place, *arrays)
+
+
+def arrange_kernel(place, own, r1, r2, r3, turned, down):
+    here = jnp.where(place[3] == 0, place[0], place[2])
     for part, step in zip((own, r1, r2, r3), STEPS):
         at = along(here, -step)
-        for unit in range(own.shape[0]):
-            out[unit, at] = part[unit]
-
-
-def arrange(kind, place, parts):
-    units = parts[0].shape[0]
-    return pl.pallas_call(
-        lambda *refs: arrange_kernel(kind, *refs),
-        out_shape=jax.ShapeDtypeStruct((units, 4, 128, 256), BF16),
+        turned[0, at] = part[0]
+        turned[1, at] = part[1]
+        down[at] = part[2]
+
+
+def arrange(place, parts):
+    return pl.pallas_call(
+        arrange_kernel,
+        out_shape=(
+            jax.ShapeDtypeStruct((2, 4, 128, 256), BF16),
+            jax.ShapeDtypeStruct((4, 128, 256), BF16),
+        ),
         in_specs=[pl.BlockSpec(memory_space=pltpu.SMEM)] + vmem(4),
-        out_specs=pl.BlockSpec(memory_space=pltpu.VMEM),
+        out_specs=tuple(vmem(2)),
         compiler_params=params(6),
-        cost_estimate=pl.CostEstimate(flops=0, bytes_accessed=1_000_000, transcendentals=0),
-        name="arrange_" + kind,
+        cost_estimate=cost(0.7),
+        name="arrange",
     )(place, *parts)
 
 
@@ -227,53 +260,53 @@
     )(place, counts, mid, up, down, merge, out_weight)
 
 
+def fetch(place, pieces, weight, sems):
+    copies = []
+    for at, (source, y, z, x) in enumerate(pieces):
+        yhi, ylo = lax.div(y, 2), lax.rem(y, 2)
+        zero = pltpu.make_async_copy(source, weight.at[yhi, :, ylo, z], sems.at[at])
+        one = pltpu.make_async_copy(source, weight.at[yhi, x, ylo], sems.at[at])
+
+        @pl.when(place[3] == 0)
+        def _():
+            zero.start()
+
+        @pl.when(place[3] == 1)
+        def _():
+            one.start()
+
+        copies.append(zero)
+    return copies
+
+
 def fetch_turned(place, parts, weight, sems):
     x, y, z = place[0], place[1], place[2]
-    copies = []
-    for at, part in enumerate(parts):
-        for slot in range(4):
-            sem = sems.at[at * 4 + slot]
-            source = part.at[slot]
-            from_y, from_z = along(y, -STEPS[slot]), along(z, -STEPS[at])
-            zero = pltpu.make_async_copy(
-                source, weight.at[lax.div(from_y, 2), :, lax.rem(from_y, 2), from_z], sem
-            )
-            across_z, across_x = along(z, -STEPS[slot]), along(x, -STEPS[at])
-            ones = [
-                pltpu.make_async_copy(
-                    source.at[pl.ds(2 * yhi, 2)], weight.at[yhi, across_x, :, across_z], sem
-                )
-                for yhi in range(2)
-            ]
-
-            @pl.when(place[3] == 0)
-            def _():
-                zero.start()
-
-            @pl.when(place[3] == 1)
-            def _():
-                for one in ones:
-                    one.start()
-
-            copies.append(zero)
-    return copies
+    turn = 1 - 2 * place[3]
+    return fetch(
+        place,
+        [
+            (parts[at].at[slot], along(y, step), along(z, -STEPS[at]), along(x, -STEPS[at]))
+            for at in range(4)
+            for slot, step in enumerate((0, -turn, turn, 2))
+        ],
+        weight,
+        sems,
+    )
 
 
 def fetch_down(place, parts, weight, sems):
-    x, y = place[0], place[1]
+    x, y, z = place[0], place[1], place[2]
     turn = 1 - 2 * place[3]
-    copies = []
-    for at, (part, step) in enumerate(zip(parts, (0, -turn, turn, 2))):
-        from_y = along(y, step)
-        for slot in range(4):
-            copy = pltpu.make_async_copy(
-                part.at[slot],
-                weight.at[lax.div(from_y, 2), along(x, -STEPS[slot]), lax.rem(from_y, 2)],
-                sems.at[at * 4 + slot],
-            )
-            copy.start()
-            copies.append(copy)
-    return copies
+    return fetch(
+        place,
+        [
+            (part.at[slot], along(y, step), along(z, -STEPS[slot]), along(x, -STEPS[slot]))
+            for part, step in zip(parts, (0, -turn, turn, 2))
+            for slot in range(4)
+        ],
+        weight,
+        sems,
+    )
 
 
 def whole(weight, head):
@@ -410,9 +443,9 @@
     core = lax.axis_index("core")
     y = lax.axis_index("yhi") * 2 + lax.axis_index("ylo")
     place = jnp.stack([lax.axis_index("x"), y, lax.axis_index("z"), core]).astype(jnp.int32)
-    normed, mine, theirs = prepare(
-        place, fine_tokens, coarse_qkv, coarse_proj.T, coarse_up, coarse_down.T
-    )
+    mine, theirs = prepare(place, coarse_qkv, coarse_proj.T, coarse_up, coarse_down.T)
+    tokens, theirs = lax.optimization_barrier((fine_tokens, theirs))
+    normed = norm(tokens)
     got = core_swap(theirs)
     devices = lax.axis_size(AXES)
     up_one = [(i, (i + 1) % devices) for i in range(devices)]
@@ -422,25 +455,28 @@
         core == 0, jnp.concatenate([mine, got], axis=1), jnp.concatenate([got, mine], axis=1)
     )
 
-    qu = arrange("qu", place, direct(blocks[:2], ("x", "y")))
-    d = arrange("d", place, direct(blocks[2:], ("z", "z")))
-    qu_two = direct(qu, ("y", "z"))
-    d_two = jnp.stack([v[0] for v in direct(d, ("x", "x"))])
-    q_two, u_two = (jnp.stack([v[unit] for v in qu_two]) for unit in range(2))
-    q_two, u_two, d_two, low, high, normed = lax.optimization_barrier(
-        (q_two, u_two, d_two, low, high, normed)
-    )
-    q_parts = direct(q_two, ("z", "x"))
-    d_one = hopped(d_two, ("y", "y"), (1, -1))
-    d_other = hopped(d_two, ("y", "y"), (-1, 1))
-
+    qu, d = arrange(place, direct(blocks, ("x", "z")))
+    qu_one, qu_other = (hopped(qu, ("y", "y"), (step, -step)) for step in (1, -1))
+    d_near = [d] + [hopped(d, ("z", "x"), (step, step)) for step in (1, -1)]
+
+    qu, low, high, normed = lax.optimization_barrier((qu, low, high, normed))
     mid = fine_attention(fine_shift, fine_tokens, normed, low, high, fine_qkv, fine_proj)
+
+    qu_one, qu_other, d_near, mid = lax.optimization_barrier((qu_one, qu_other, d_near, mid))
+    qu_far = hopped(qu_one, ("y", "y"), (1, -1))
+    d_far = hopped(d_near[0], ("z", "x"), (2, 2))
     skip, coarse = fine_mlp(place, window_counts, mid, fine_up, fine_down, merge_weight, out_weight)
-    d_one, u_two, coarse = lax.optimization_barrier((d_one, u_two, coarse))
+
+    qu_far, d_far, coarse = lax.optimization_barrier((qu_far, d_far, coarse))
+    q_two, u_two = (jnp.stack([v[i] for v in (qu, qu_one, qu_other, qu_far)]) for i in range(2))
+    d_two = jnp.stack([*d_near, d_far])
+    q_one, q_other, q_far = (hopped(q_two, ("z", "x"), (step, step)) for step in (1, -1, 2))
+    d_one, d_other = (hopped(d_two, ("y", "y"), (step, -step)) for step in (1, -1))
+    other = core_swap(coarse)
+    q_other, u_two = lax.optimization_barrier((q_other, u_two))
+    u_parts = direct(u_two, ("z", "x"))
     d_far = hopped(d_one, ("y", "y"), (1, -1))
-    u_parts = direct(u_two, ("z", "x"))
-    other = core_swap(coarse)
-    sent = coarse_attention(place, coarse, other, q_parts)
+    sent = coarse_attention(place, coarse, other, (q_two, q_one, q_other, q_far))
     came = core_swap(sent)
     base, give = coarse_mlp(
         place, coarse, other, sent, came, u_parts, (d_two, d_one, d_other, d_far)

time: 118 us -> 111 us (0.941)
  starting transfers between devices: 41.7 us -> 59.7 us
  waiting for transfers between devices: 27.2 us -> 12.9 us
  Pallas kernels: 42.5 us -> 35.6 us
  local copies, waits for them, and re-layouts: 4.69 us -> 0.22 us
    ppermute x21 -> x18, waiting for transfers between devices: 24.7 us -> 8.13 us  [hopped(): return lax.ppermute(value, AXES, pairs)]
    ppermute x21 -> x18, starting transfers between devices: 25.2 us -> 38.8 us  [hopped(): return lax.ppermute(value, AXES, pairs)]
    ppermute x4, starting transfers between devices: 7.14 us -> 15.8 us  [core_swap(): return lax.ppermute(value, 'core', [(0, 1), (1, 0)])]
    unnamed x28 -> x22, local copies, waits for them, and re-layouts: 4.51 us -> 0.06 us
    ppermute x1, starting transfers between devices: 9.36 us -> 5 us  [body(): high = lax.ppermute(normed[:WIN], AXES, [(b, a) for a, b in up_one])]
    pallas_call x1, Pallas kernels: 14.3 us -> 10.3 us  [coarse_attention(): pl.pallas_call(coarse_attention_kernel, out_shape=jax.ShapeDtypeStruct((2...]
    pallas_call x1, Pallas kernels: 7.81 us -> 5.35 us  [coarse_mlp(): pl.pallas_call(coarse_mlp_kernel, out_shape=(jax.ShapeDtypeStruct((WIN, 2...]
    pallas_call x1, Pallas kernels: 11 us -> 9.24 us  [fine_attention(): pl.pallas_call(fine_attention_kernel, out_shape=jax.ShapeDtypeStruct((row...]
  transfers between devices with their start and end apart: 27 -> 24, of which waited for: 9 -> 10; matrix products, arithmetic and copies ran while one was open for 0% -> 0% of each run, Pallas kernels for 26% -> 23%
where the time goes in v2:
time: 111 us; the launch traced here: 110 us
  starting transfers between devices  59.7 us (54%)
  Pallas kernels  35.6 us (32%)
  waiting for transfers between devices  12.9 us (12%)
    ppermute x18, starting transfers between devices, hopped(): return lax.ppermute(value, AXES, pairs)  38.8 us
    ppermute x4, starting transfers between devices, core_swap(): return lax.ppermute(value, 'core', [(0, 1), (1, 0)])  15.8 us
    pallas_call x1, Pallas kernels, coarse_attention(): pl.pallas_call(coarse_attention_kernel, out_shape=jax.ShapeDtypeStruct((2...  10.3 us
    pallas_call x1, Pallas kernels, fine_attention(): pl.pallas_call(fine_attention_kernel, out_shape=jax.ShapeDtypeStruct((row...  9.24 us
    ppermute x18, waiting for transfers between devices, hopped(): return lax.ppermute(value, AXES, pairs)  8.13 us
    pallas_call x1, Pallas kernels, coarse_mlp(): pl.pallas_call(coarse_mlp_kernel, out_shape=(jax.ShapeDtypeStruct((WIN, 2...  5.35 us
    ppermute x1, starting transfers between devices, body(): high = lax.ppermute(normed[:WIN], AXES, [(b, a) for a, b in up_one])  5 us
    pallas_call x1, Pallas kernels, fine_mlp(): pl.pallas_call(fine_mlp_kernel, out_shape=(jax.ShapeDtypeStruct((rows, C)...  4.59 us
  transfers between devices with their start and end apart: 24, of which 10 were waited for; matrix products, arithmetic and copies ran while one was open for 0% of the time, Pallas kernels for 23%

profile of v2, /device:TPU:1, one launch (start us, length us, event | category | flops | bytes accessed | tf_op | source)
XLA Modules:
  0.0 110.4 jit_solution(16697090025702650583)
XLA Ops:
  0.6 2.5 %prepare.1 = (bf16[3,64,256]{2,1,0:T(8,128)(2,1)}, bf16[3,64,256]{2,1,0:T(8,128)(2,1)}) custom-call(s32[4]{0:T(128)} %pad_add_fusion.place, bf16[64,384]{1,0:T(8,128)(2,1)} %refs_0_.1, bf16[64,128]{1,0:T(8,128)(2,1)} %bitcast.15, bf16[64,512]{1,0:T(8,128)(2,1)} %refs_2_.1, bf16[64,512]{1,0:T(8,128)(2,1)} %bitcast.14), custom_call_target="tpu_custom_call" | custom-call | flops 1724999936 | tf_op jit(solution)/shard_map/prepare/pallas_call | solution.py:137
  3.1 1.5 %collective-permute-start = (bf16[3,64,256]{2,1,0:T(8,128)(2,1)}, bf16[3,64,256]{2,1,0:T(8,128)(2,1)S(1)}, u32[]{:S(2)}, u32[]{:S(2)}) collective-permute-start(bf16[3,64,256]{2,1,0:T(8,128)(2,1)} %get-tuple-element.32), channel_id=1, source_target_pairs={{0,8},{8,0},{1,9},{9,1},{2,10},{10,2},{3,11},{11,3},{4,12},{12,4},... | collective-permute-start | bytes 294920 | tf_op jit(solution)/shard_map/ppermute | solution.py:40
  5.9 3.8 %collective-permute-start.3 = (bf16[3,128,256]{2,1,0:T(8,128)(2,1)S(1)}, bf16[3,128,256]{2,1,0:T(8,128)(2,1)S(1)}, u32[]{:S(2)}, u32[]{:S(2)}) collective-permute-start(bf16[3,128,256]{2,1,0:T(8,128)(2,1)S(1)} %maximum_select_fusion.own), channel_id=1, source_target_pairs={{0,2},{1,3},{2,0},{3,1},{4,6},{5,7},{6,4},{7,5},{8,40},{9,41},{10,... | collective-permute-start | bytes 589832 | tf_op jit(solution)/shard_map/ppermute | solution.py:32
  11.1 5.0 %collective-permute-start.9 = (bf16[144,512]{1,0:T(8,128)(2,1)S(1)}, bf16[144,512]{1,0:T(8,128)(2,1)S(1)}, u32[]{:S(2)}, u32[]{:S(2)}) collective-permute-start(bf16[144,512]{1,0:T(8,128)(2,1)S(1)} %get-tuple-element.55), channel_id=1, source_target_pairs={{1,0},{2,1},{3,2},{4,3},{5,4},{6,5},{7,6},{8,7},{9,8},{10,9},{11,1... | collective-permute-start | bytes 442376 | tf_op jit(solution)/shard_map/ppermute | solution.py:453
  18.1 1.5 %collective-permute-start.4 = (bf16[2,4,128,256]{3,2,1,0:T(8,128)(2,1)S(1)}, bf16[2,4,128,256]{3,2,1,0:T(8,128)(2,1)S(1)}, u32[]{:S(2)}, u32[]{:S(2)}) collective-permute-start(bf16[2,4,128,256]{3,2,1,0:T(8,128)(2,1)S(1)} %get-tuple-element.44), channel_id=1, source_target_pairs={{0,64},{1,65},{2,66},{3,67},{4,68},{5,69},{6,70},{7,71},{8,76},{9,... | collective-permute-start | bytes 1572872 | tf_op jit(solution)/shard_map/ppermute | solution.py:32
  20.3 4.0 %collective-permute-start.7 = (bf16[4,128,256]{2,1,0:T(8,128)(2,1)S(1)}, bf16[4,128,256]{2,1,0:T(8,128)(2,1)S(1)}, u32[]{:S(2)}, u32[]{:S(2)}) collective-permute-start(bf16[4,128,256]{2,1,0:T(8,128)(2,1)S(1)} %get-tuple-element.40), channel_id=1, source_target_pairs={{0,48},{1,49},{2,50},{3,51},{4,52},{5,53},{6,54},{7,55},{8,11},{9,... | collective-permute-start | bytes 786440 | tf_op jit(solution)/shard_map/ppermute | solution.py:32
  25.3 9.2 %fine_attention.1.mid = f32[576,512]{1,0:T(8,128)S(1)} custom-call(s32[1]{0:T(128)S(6)} %copy.15.offset, f32[576,512]{1,0:T(8,128)S(1)} %copy-done.7, bf16[576,512]{1,0:T(8,128)(2,1)S(1)} %norm.1.normed, bf16[144,512]{1,0:T(8,128)(2,1)S(1)} %collective-permute-done.8.low, bf16[144,512]{1,0:T(8,128)(2,1)S(1)} %collective-permute-done.9.high, ...), custom_call_target="tpu_custom_call" | custom-call | flops 2500000000 | bytes 6000000 | tf_op jit(solution)/shard_map/fine_attention/pallas_call | solution.py:203
  34.9 2.8 %collective-permute-start.10 = (bf16[2,4,128,256]{3,2,1,0:T(8,128)(2,1)S(1)}, bf16[2,4,128,256]{3,2,1,0:T(8,128)(2,1)S(1)}, u32[]{:S(2)}, u32[]{:S(2)}) collective-permute-start(bf16[2,4,128,256]{3,2,1,0:T(8,128)(2,1)S(1)} %collective-permute-done.4), channel_id=1, source_target_pairs={{0,64},{1,65},{2,66},{3,67},{4,68},{5,69},{6,70},{7,71},{8,76},{9,... | collective-permute-start | bytes 1572872 | tf_op jit(solution)/shard_map/ppermute | solution.py:32
  37.8 4.6 %fine_mlp.1 = (f32[576,512]{1,0:T(8,128)S(1)}, f32[152,1024]{1,0:T(8,128)S(1)}) custom-call(s32[4]{0:T(128)S(1)} %copy-done.2, s32[8]{0:T(128)S(1)} %copy-done.9, f32[576,512]{1,0:T(8,128)S(1)} %fine_attention.1.mid, bf16[512,2048]{1,0:T(8,128)(2,1)S(1)} %copy-done.4, bf16[2048,512]{1,0:T(8,128)(2,1)S(1)} %copy-done.5, bf16[2048,1024]{1,0:T(8,128)(2,1)S(1)} %copy-done.3, ...), custom_call_target="tpu_custom_call" | custom-call | flops 3500000000 | bytes 12000000 | tf_op jit(solution)/shard_map/fine_mlp/pallas_call | solution.py:248
  42.5 1.4 %collective-permute-done.10 = bf16[2,4,128,256]{3,2,1,0:T(8,128)(2,1)S(1)} collective-permute-done((bf16[2,4,128,256]{3,2,1,0:T(8,128)(2,1)S(1)}, bf16[2,4,128,256]{3,2,1,0:T(8,128)(2,1)S(1)}, u32[]{:S(2)}, u32[]{:S(2)}) %collective-permute-start.10) | collective-permute-done | bytes 524320 | tf_op jit(solution)/shard_map/ppermute | solution.py:32
  45.2 2.1 %collective-permute-start.15 = (bf16[4,4,128,256]{3,2,1,0:T(8,128)(2,1)S(1)}, bf16[4,4,128,256]{3,2,1,0:T(8,128)(2,1)S(1)}, u32[]{:S(2)}, u32[]{:S(2)}) collective-permute-start(bf16[4,4,128,256]{3,2,1,0:T(8,128)(2,1)S(1)} %pad_maximum_fusion.a0), channel_id=1, source_target_pairs={{0,32},{1,33},{2,34},{3,35},{4,36},{5,37},{6,38},{7,39},{8,10},{9,... | collective-permute-start | bytes 3145736 | tf_op jit(solution)/shard_map/ppermute | solution.py:32
  48.1 3.2 %collective-permute-start.20 = (bf16[4,4,128,256]{3,2,1,0:T(8,128)(2,1)S(1)}, bf16[4,4,128,256]{3,2,1,0:T(8,128)(2,1)S(1)}, u32[]{:S(2)}, u32[]{:S(2)}) collective-permute-start(bf16[4,4,128,256]{3,2,1,0:T(8,128)(2,1)S(1)} %pad_maximum_fusion.2.d0), channel_id=1, source_target_pairs={{0,64},{1,65},{2,66},{3,67},{4,68},{5,69},{6,70},{7,71},{8,76},{9,... | collective-permute-start | bytes 3145736 | tf_op jit(solution)/shard_map/ppermute | solution.py:32
  51.3 3.7 %collective-permute-start.12 = (f32[152,1024]{1,0:T(8,128)S(1)}, f32[152,1024]{1,0:T(8,128)S(1)}, u32[]{:S(2)}, u32[]{:S(2)}) collective-permute-start(f32[152,1024]{1,0:T(8,128)S(1)} %get-tuple-element.43.own), channel_id=1, source_target_pairs={{0,8},{8,0},{1,9},{9,1},{2,10},{10,2},{3,11},{11,3},{4,12},{12,4},... | collective-permute-start | bytes 1867784 | tf_op jit(solution)/shard_map/ppermute | solution.py:40
  55.0 3.1 %collective-permute-done.14.a2 = bf16[4,4,128,256]{3,2,1,0:T(8,128)(2,1)S(1)} collective-permute-done((bf16[4,4,128,256]{3,2,1,0:T(8,128)(2,1)S(1)}, bf16[4,4,128,256]{3,2,1,0:T(8,128)(2,1)S(1)}, u32[]{:S(2)}, u32[]{:S(2)}) %collective-permute-start.14) | collective-permute-done | bytes 1048608 | tf_op jit(solution)/shard_map/ppermute | solution.py:32
  58.7 3.0 %collective-permute-start.19 = (bf16[4,4,128,256]{3,2,1,0:T(8,128)(2,1)S(1)}, bf16[4,4,128,256]{3,2,1,0:T(8,128)(2,1)S(1)}, u32[]{:S(2)}, u32[]{:S(2)}) collective-permute-start(bf16[4,4,128,256]{3,2,1,0:T(8,128)(2,1)S(1)} %pad_maximum_fusion.1.u0), channel_id=1, source_target_pairs={{0,32},{1,33},{2,34},{3,35},{4,36},{5,37},{6,38},{7,39},{8,10},{9,... | collective-permute-start | bytes 3145736 | tf_op jit(solution)/shard_map/ppermute | solution.py:32
  61.7 9.7 %collective-permute-start.18 = (bf16[4,4,128,256]{3,2,1,0:T(8,128)(2,1)S(1)}, bf16[4,4,128,256]{3,2,1,0:T(8,128)(2,1)S(1)}, u32[]{:S(2)}, u32[]{:S(2)}) collective-permute-start(bf16[4,4,128,256]{3,2,1,0:T(8,128)(2,1)S(1)} %pad_maximum_fusion.1.u0), channel_id=1, source_target_pairs={{0,48},{1,49},{2,50},{3,51},{4,52},{5,53},{6,54},{7,55},{8,11},{9,... | collective-permute-start | bytes 3145736 | tf_op jit(solution)/shard_map/ppermute | solution.py:32
  72.5 3.0 %collective-permute-start.22 = (bf16[4,4,128,256]{3,2,1,0:T(8,128)(2,1)S(1)}, bf16[4,4,128,256]{3,2,1,0:T(8,128)(2,1)S(1)}, u32[]{:S(2)}, u32[]{:S(2)}) collective-permute-start(bf16[4,4,128,256]{3,2,1,0:T(8,128)(2,1)S(1)} %collective-permute-done.20.d1), channel_id=1, source_target_pairs={{0,64},{1,65},{2,66},{3,67},{4,68},{5,69},{6,70},{7,71},{8,76},{9,... | collective-permute-start | bytes 3145736 | tf_op jit(solution)/shard_map/ppermute | solution.py:32
  75.5 10.3 %coarse_attention.1.sent = bf16[2,144,1024]{2,1,0:T(8,128)(2,1)S(1)} custom-call(s32[4]{0:T(128)S(1)} %copy-done.2, f32[152,1024]{1,0:T(8,128)S(1)} %get-tuple-element.43.own, f32[152,1024]{1,0:T(8,128)S(1)} %collective-permute-done.12.other, bf16[4,4,128,256]{3,2,1,0:T(8,128)(2,1)S(1)} %pad_maximum_fusion.a0, ...), custom_call_target="tpu_custom_call" | custom-call | flops 1400000000 | bytes 7000000 | tf_op jit(solution)/shard_map/coarse_attention/pallas_call | solution.py:335
  85.8 4.0 %collective-permute-start.16 = (bf16[2,144,1024]{2,1,0:T(8,128)(2,1)S(1)}, bf16[2,144,1024]{2,1,0:T(8,128)(2,1)S(1)}, u32[]{:S(2)}, u32[]{:S(2)}) collective-permute-start(bf16[2,144,1024]{2,1,0:T(8,128)(2,1)S(1)} %coarse_attention.1.sent), channel_id=1, source_target_pairs={{0,8},{8,0},{1,9},{9,1},{2,10},{10,2},{3,11},{11,3},{4,12},{12,4},... | collective-permute-start | bytes 1769480 | tf_op jit(solution)/shard_map/ppermute | solution.py:40
  89.8 1.6 %collective-permute-done.16.came = bf16[2,144,1024]{2,1,0:T(8,128)(2,1)S(1)} collective-permute-done((bf16[2,144,1024]{2,1,0:T(8,128)(2,1)S(1)}, bf16[2,144,1024]{2,1,0:T(8,128)(2,1)S(1)}, u32[]{:S(2)}, u32[]{:S(2)}) %collective-permute-start.16) | collective-permute-done | bytes 589856 | tf_op jit(solution)/shard_map/ppermute | solution.py:40
  91.8 2.6 %collective-permute-done.17.u1 = bf16[4,4,128,256]{3,2,1,0:T(8,128)(2,1)S(1)} collective-permute-done((bf16[4,4,128,256]{3,2,1,0:T(8,128)(2,1)S(1)}, bf16[4,4,128,256]{3,2,1,0:T(8,128)(2,1)S(1)}, u32[]{:S(2)}, u32[]{:S(2)}) %collective-permute-start.17) | collective-permute-done | bytes 1048608 | tf_op jit(solution)/shard_map/ppermute | solution.py:32
  94.4 5.4 %coarse_mlp.1 = (f32[144,1024]{1,0:T(8,128)S(1)}, bf16[144,1024]{1,0:T(8,128)(2,1)S(1)}) custom-call(s32[4]{0:T(128)S(1)} %copy-done.2, f32[152,1024]{1,0:T(8,128)S(1)} %get-tuple-element.43.own, f32[152,1024]{1,0:T(8,128)S(1)} %collective-permute-done.12.other, bf16[2,144,1024]{2,1,0:T(8,128)(2,1)S(1)} %coarse_attention.1.sent, ...), custom_call_target="tpu_custom_call" | custom-call | flops 2400000000 | bytes 14000000 | tf_op jit(solution)/shard_map/coarse_mlp/pallas_call | solution.py:378
  99.7 6.7 %collective-permute-start.23 = (bf16[144,1024]{1,0:T(8,128)(2,1)S(1)}, bf16[144,1024]{1,0:T(8,128)(2,1)S(1)}, u32[]{:S(2)}, u32[]{:S(2)}) collective-permute-start(bf16[144,1024]{1,0:T(8,128)(2,1)S(1)} %get-tuple-element.53), channel_id=1, source_target_pairs={{0,8},{8,0},{1,9},{9,1},{2,10},{10,2},{3,11},{11,3},{4,12},{12,4},... | collective-permute-start | bytes 884744 | tf_op jit(solution)/shard_map/ppermute | solution.py:40
  107.6 2.7 %tail.1 = f32[576,512]{1,0:T(8,128)} custom-call(f32[144,1024]{1,0:T(8,128)S(1)} %get-tuple-element.52.base, bf16[144,1024]{1,0:T(8,128)(2,1)S(1)} %collective-permute-done.23.came, f32[576,512]{1,0:T(8,128)S(1)} %get-tuple-element.54.skip, bf16[1024,2048]{1,0:T(8,128)(2,1)S(1)} %copy-done, bf16[1024,512]{1,0:T(8,128)(2,1)S(1)} %copy-done.1), custom_call_target="tpu_custom_call" | custom-call | flops 900000000 | bytes 8000000 | tf_op jit(solution)/shard_map/tail/pallas_call | solution.py:415
  (63 shorter events, 12.1 us)
Async XLA Ops:
  3.1 2.6 %collective-permute-start = (bf16[3,64,256]{2,1,0:T(8,128)(2,1)}, bf16[3,64,256]{2,1,0:T(8,128)(2,1)S(1)}, u32[]{:S(2)}, u32[]{:S(2)}) collective-permute-start(bf16[3,64,256]{2,1,0:T(8,128)(2,1)} %get-tuple-element.32), channel_id=1, source_target_pairs={{0,8},{8,0},{1,9},{9,1},{2,10},{10,2},{3,11},{11,3},{4,12},{12,4},... | collective-permute-start | bytes 294920 | tf_op jit(solution)/shard_map/ppermute | solution.py:40
  5.9 10.3 %collective-permute-start.3 = (bf16[3,128,256]{2,1,0:T(8,128)(2,1)S(1)}, bf16[3,128,256]{2,1,0:T(8,128)(2,1)S(1)}, u32[]{:S(2)}, u32[]{:S(2)}) collective-permute-start(bf16[3,128,256]{2,1,0:T(8,128)(2,1)S(1)} %maximum_select_fusion.own), channel_id=1, source_target_pairs={{0,2},{1,3},{2,0},{3,1},{4,6},{5,7},{6,4},{7,5},{8,40},{9,41},{10,... | collective-permute-start | bytes 589832 | tf_op jit(solution)/shard_map/ppermute | solution.py:32
  9.6 6.5 %collective-permute-start.2 = (bf16[3,128,256]{2,1,0:T(8,128)(2,1)S(1)}, bf16[3,128,256]{2,1,0:T(8,128)(2,1)S(1)}, u32[]{:S(2)}, u32[]{:S(2)}) collective-permute-start(bf16[3,128,256]{2,1,0:T(8,128)(2,1)S(1)} %maximum_select_fusion.own), channel_id=1, source_target_pairs={{0,3},{1,0},{2,1},{3,2},{4,7},{5,4},{6,5},{7,6},{8,56},{9,57},{10,... | collective-permute-start | bytes 589832 | tf_op jit(solution)/shard_map/ppermute | solution.py:32
  10.0 6.1 %collective-permute-start.1 = (bf16[3,128,256]{2,1,0:T(8,128)(2,1)S(1)}, bf16[3,128,256]{2,1,0:T(8,128)(2,1)S(1)}, u32[]{:S(2)}, u32[]{:S(2)}) collective-permute-start(bf16[3,128,256]{2,1,0:T(8,128)(2,1)S(1)} %maximum_select_fusion.own), channel_id=1, source_target_pairs={{0,1},{1,2},{2,3},{3,0},{4,5},{5,6},{6,7},{7,4},{8,24},{9,25},{10,... | collective-permute-start | bytes 589832 | tf_op jit(solution)/shard_map/ppermute | solution.py:32
  11.1 13.1 %collective-permute-start.9 = (bf16[144,512]{1,0:T(8,128)(2,1)S(1)}, bf16[144,512]{1,0:T(8,128)(2,1)S(1)}, u32[]{:S(2)}, u32[]{:S(2)}) collective-permute-start(bf16[144,512]{1,0:T(8,128)(2,1)S(1)} %get-tuple-element.55), channel_id=1, source_target_pairs={{1,0},{2,1},{3,2},{4,3},{5,4},{6,5},{7,6},{8,7},{9,8},{10,9},{11,1... | collective-permute-start | bytes 442376 | tf_op jit(solution)/shard_map/ppermute | solution.py:453
  16.1 9.2 %collective-permute-start.8 = (bf16[144,512]{1,0:T(8,128)(2,1)S(1)}, bf16[144,512]{1,0:T(8,128)(2,1)S(1)}, u32[]{:S(2)}, u32[]{:S(2)}) collective-permute-start(bf16[144,512]{1,0:T(8,128)(2,1)S(1)} %get-tuple-element.56), channel_id=1, source_target_pairs={{0,1},{1,2},{2,3},{3,4},{4,5},{5,6},{6,7},{7,8},{8,9},{9,10},{10,1... | collective-permute-start | bytes 442376 | tf_op jit(solution)/shard_map/ppermute | solution.py:452
  16.8 17.8 %collective-permute-start.5 = (bf16[2,4,128,256]{3,2,1,0:T(8,128)(2,1)S(1)}, bf16[2,4,128,256]{3,2,1,0:T(8,128)(2,1)S(1)}, u32[]{:S(2)}, u32[]{:S(2)}) collective-permute-start(bf16[2,4,128,256]{3,2,1,0:T(8,128)(2,1)S(1)} %get-tuple-element.44), channel_id=1, source_target_pairs={{0,68},{1,69},{2,70},{3,71},{4,64},{5,65},{6,66},{7,67},{8,72},{9,... | collective-permute-start | bytes 1572872 | tf_op jit(solution)/shard_map/ppermute | solution.py:32
  18.1 16.7 %collective-permute-start.4 = (bf16[2,4,128,256]{3,2,1,0:T(8,128)(2,1)S(1)}, bf16[2,4,128,256]{3,2,1,0:T(8,128)(2,1)S(1)}, u32[]{:S(2)}, u32[]{:S(2)}) collective-permute-start(bf16[2,4,128,256]{3,2,1,0:T(8,128)(2,1)S(1)} %get-tuple-element.44), channel_id=1, source_target_pairs={{0,64},{1,65},{2,66},{3,67},{4,68},{5,69},{6,70},{7,71},{8,76},{9,... | collective-permute-start | bytes 1572872 | tf_op jit(solution)/shard_map/ppermute | solution.py:32
  20.3 14.3 %collective-permute-start.7 = (bf16[4,128,256]{2,1,0:T(8,128)(2,1)S(1)}, bf16[4,128,256]{2,1,0:T(8,128)(2,1)S(1)}, u32[]{:S(2)}, u32[]{:S(2)}) collective-permute-start(bf16[4,128,256]{2,1,0:T(8,128)(2,1)S(1)} %get-tuple-element.40), channel_id=1, source_target_pairs={{0,48},{1,49},{2,50},{3,51},{4,52},{5,53},{6,54},{7,55},{8,11},{9,... | collective-permute-start | bytes 786440 | tf_op jit(solution)/shard_map/ppermute | solution.py:32
  24.2 10.4 %collective-permute-start.6 = (bf16[4,128,256]{2,1,0:T(8,128)(2,1)S(1)}, bf16[4,128,256]{2,1,0:T(8,128)(2,1)S(1)}, u32[]{:S(2)}, u32[]{:S(2)}) collective-permute-start(bf16[4,128,256]{2,1,0:T(8,128)(2,1)S(1)} %get-tuple-element.40), channel_id=1, source_target_pairs={{0,16},{1,17},{2,18},{3,19},{4,20},{5,21},{6,22},{7,23},{8,9},{9,1... | collective-permute-start | bytes 786440 | tf_op jit(solution)/shard_map/ppermute | solution.py:32
  34.8 7.7 %collective-permute-start.11 = (bf16[4,128,256]{2,1,0:T(8,128)(2,1)S(1)}, bf16[4,128,256]{2,1,0:T(8,128)(2,1)S(1)}, u32[]{:S(2)}, u32[]{:S(2)}) collective-permute-start(bf16[4,128,256]{2,1,0:T(8,128)(2,1)S(1)} %get-tuple-element.40), channel_id=1, source_target_pairs={{0,32},{1,33},{2,34},{3,35},{4,36},{5,37},{6,38},{7,39},{8,10},{9,... | collective-permute-start | bytes 786440 | tf_op jit(solution)/shard_map/ppermute | solution.py:32
  34.9 8.9 %collective-permute-start.10 = (bf16[2,4,128,256]{3,2,1,0:T(8,128)(2,1)S(1)}, bf16[2,4,128,256]{3,2,1,0:T(8,128)(2,1)S(1)}, u32[]{:S(2)}, u32[]{:S(2)}) collective-permute-start(bf16[2,4,128,256]{3,2,1,0:T(8,128)(2,1)S(1)} %collective-permute-done.4), channel_id=1, source_target_pairs={{0,64},{1,65},{2,66},{3,67},{4,68},{5,69},{6,70},{7,71},{8,76},{9,... | collective-permute-start | bytes 1572872 | tf_op jit(solution)/shard_map/ppermute | solution.py:32
  44.0 14.0 %collective-permute-start.14 = (bf16[4,4,128,256]{3,2,1,0:T(8,128)(2,1)S(1)}, bf16[4,4,128,256]{3,2,1,0:T(8,128)(2,1)S(1)}, u32[]{:S(2)}, u32[]{:S(2)}) collective-permute-start(bf16[4,4,128,256]{3,2,1,0:T(8,128)(2,1)S(1)} %pad_maximum_fusion.a0), channel_id=1, source_target_pairs={{0,48},{1,49},{2,50},{3,51},{4,52},{5,53},{6,54},{7,55},{8,11},{9,... | collective-permute-start | bytes 3145736 | tf_op jit(solution)/shard_map/ppermute | solution.py:32
  45.2 16.6 %collective-permute-start.15 = (bf16[4,4,128,256]{3,2,1,0:T(8,128)(2,1)S(1)}, bf16[4,4,128,256]{3,2,1,0:T(8,128)(2,1)S(1)}, u32[]{:S(2)}, u32[]{:S(2)}) collective-permute-start(bf16[4,4,128,256]{3,2,1,0:T(8,128)(2,1)S(1)} %pad_maximum_fusion.a0), channel_id=1, source_target_pairs={{0,32},{1,33},{2,34},{3,35},{4,36},{5,37},{6,38},{7,39},{8,10},{9,... | collective-permute-start | bytes 3145736 | tf_op jit(solution)/shard_map/ppermute | solution.py:32
  47.3 24.6 %collective-permute-start.13 = (bf16[4,4,128,256]{3,2,1,0:T(8,128)(2,1)S(1)}, bf16[4,4,128,256]{3,2,1,0:T(8,128)(2,1)S(1)}, u32[]{:S(2)}, u32[]{:S(2)}) collective-permute-start(bf16[4,4,128,256]{3,2,1,0:T(8,128)(2,1)S(1)} %pad_maximum_fusion.a0), channel_id=1, source_target_pairs={{0,16},{1,17},{2,18},{3,19},{4,20},{5,21},{6,22},{7,23},{8,9},{9,1... | collective-permute-start | bytes 3145736 | tf_op jit(solution)/shard_map/ppermute | solution.py:32
  48.1 24.4 %collective-permute-start.20 = (bf16[4,4,128,256]{3,2,1,0:T(8,128)(2,1)S(1)}, bf16[4,4,128,256]{3,2,1,0:T(8,128)(2,1)S(1)}, u32[]{:S(2)}, u32[]{:S(2)}) collective-permute-start(bf16[4,4,128,256]{3,2,1,0:T(8,128)(2,1)S(1)} %pad_maximum_fusion.2.d0), channel_id=1, source_target_pairs={{0,64},{1,65},{2,66},{3,67},{4,68},{5,69},{6,70},{7,71},{8,76},{9,... | collective-permute-start | bytes 3145736 | tf_op jit(solution)/shard_map/ppermute | solution.py:32
  51.3 7.4 %collective-permute-start.12 = (f32[152,1024]{1,0:T(8,128)S(1)}, f32[152,1024]{1,0:T(8,128)S(1)}, u32[]{:S(2)}, u32[]{:S(2)}) collective-permute-start(f32[152,1024]{1,0:T(8,128)S(1)} %get-tuple-element.43.own), channel_id=1, source_target_pairs={{0,8},{8,0},{1,9},{9,1},{2,10},{10,2},{3,11},{11,3},{4,12},{12,4},... | collective-permute-start | bytes 1867784 | tf_op jit(solution)/shard_map/ppermute | solution.py:40
  58.1 27.8 %collective-permute-start.21 = (bf16[4,4,128,256]{3,2,1,0:T(8,128)(2,1)S(1)}, bf16[4,4,128,256]{3,2,1,0:T(8,128)(2,1)S(1)}, u32[]{:S(2)}, u32[]{:S(2)}) collective-permute-start(bf16[4,4,128,256]{3,2,1,0:T(8,128)(2,1)S(1)} %pad_maximum_fusion.2.d0), channel_id=1, source_target_pairs={{0,68},{1,69},{2,70},{3,71},{4,64},{5,65},{6,66},{7,67},{8,72},{9,... | collective-permute-start | bytes 3145736 | tf_op jit(solution)/shard_map/ppermute | solution.py:32
  58.7 32.8 %collective-permute-start.19 = (bf16[4,4,128,256]{3,2,1,0:T(8,128)(2,1)S(1)}, bf16[4,4,128,256]{3,2,1,0:T(8,128)(2,1)S(1)}, u32[]{:S(2)}, u32[]{:S(2)}) collective-permute-start(bf16[4,4,128,256]{3,2,1,0:T(8,128)(2,1)S(1)} %pad_maximum_fusion.1.u0), channel_id=1, source_target_pairs={{0,32},{1,33},{2,34},{3,35},{4,36},{5,37},{6,38},{7,39},{8,10},{9,... | collective-permute-start | bytes 3145736 | tf_op jit(solution)/shard_map/ppermute | solution.py:32
  61.7 30.1 %collective-permute-start.18 = (bf16[4,4,128,256]{3,2,1,0:T(8,128)(2,1)S(1)}, bf16[4,4,128,256]{3,2,1,0:T(8,128)(2,1)S(1)}, u32[]{:S(2)}, u32[]{:S(2)}) collective-permute-start(bf16[4,4,128,256]{3,2,1,0:T(8,128)(2,1)S(1)} %pad_maximum_fusion.1.u0), channel_id=1, source_target_pairs={{0,48},{1,49},{2,50},{3,51},{4,52},{5,53},{6,54},{7,55},{8,11},{9,... | collective-permute-start | bytes 3145736 | tf_op jit(solution)/shard_map/ppermute | solution.py:32
  71.9 22.5 %collective-permute-start.17 = (bf16[4,4,128,256]{3,2,1,0:T(8,128)(2,1)S(1)}, bf16[4,4,128,256]{3,2,1,0:T(8,128)(2,1)S(1)}, u32[]{:S(2)}, u32[]{:S(2)}) collective-permute-start(bf16[4,4,128,256]{3,2,1,0:T(8,128)(2,1)S(1)} %pad_maximum_fusion.1.u0), channel_id=1, source_target_pairs={{0,16},{1,17},{2,18},{3,19},{4,20},{5,21},{6,22},{7,23},{8,9},{9,1... | collective-permute-start | bytes 3145736 | tf_op jit(solution)/shard_map/ppermute | solution.py:32
  72.5 21.9 %collective-permute-start.22 = (bf16[4,4,128,256]{3,2,1,0:T(8,128)(2,1)S(1)}, bf16[4,4,128,256]{3,2,1,0:T(8,128)(2,1)S(1)}, u32[]{:S(2)}, u32[]{:S(2)}) collective-permute-start(bf16[4,4,128,256]{3,2,1,0:T(8,128)(2,1)S(1)} %collective-permute-done.20.d1), channel_id=1, source_target_pairs={{0,64},{1,65},{2,66},{3,67},{4,68},{5,69},{6,70},{7,71},{8,76},{9,... | collective-permute-start | bytes 3145736 | tf_op jit(solution)/shard_map/ppermute | solution.py:32
  85.8 5.6 %collective-permute-start.16 = (bf16[2,144,1024]{2,1,0:T(8,128)(2,1)S(1)}, bf16[2,144,1024]{2,1,0:T(8,128)(2,1)S(1)}, u32[]{:S(2)}, u32[]{:S(2)}) collective-permute-start(bf16[2,144,1024]{2,1,0:T(8,128)(2,1)S(1)} %coarse_attention.1.sent), channel_id=1, source_target_pairs={{0,8},{8,0},{1,9},{9,1},{2,10},{10,2},{3,11},{11,3},{4,12},{12,4},... | collective-permute-start | bytes 1769480 | tf_op jit(solution)/shard_map/ppermute | solution.py:40
  99.7 7.9 %collective-permute-start.23 = (bf16[144,1024]{1,0:T(8,128)(2,1)S(1)}, bf16[144,1024]{1,0:T(8,128)(2,1)S(1)}, u32[]{:S(2)}, u32[]{:S(2)}) collective-permute-start(bf16[144,1024]{1,0:T(8,128)(2,1)S(1)} %get-tuple-element.53), channel_id=1, source_target_pairs={{0,8},{8,0},{1,9},{9,1},{2,10},{10,2},{3,11},{11,3},{4,12},{12,4},... | collective-permute-start | bytes 884744 | tf_op jit(solution)/shard_map/ppermute | solution.py:40
  (11 other events, 145.9 us)

commit v3 on v2

--- a/solution.py
+++ b/solution.py
@@ -148,21 +148,25 @@
     )(place, *arrays)
 
 
+UP = 96
+
+
 def arrange_kernel(place, own, r1, r2, r3, turned, down):
     here = jnp.where(place[3] == 0, place[0], place[2])
     for part, step in zip((own, r1, r2, r3), STEPS):
         at = along(here, -step)
-        turned[0, at] = part[0]
-        turned[1, at] = part[1]
-        down[at] = part[2]
+        turned[at, :128] = part[0]
+        turned[at, 128:] = part[1, :UP]
+        down[at, :128] = part[2]
+        down[at, 128:] = part[1, UP:]
 
 
 def arrange(place, parts):
     return pl.pallas_call(
         arrange_kernel,
         out_shape=(
-            jax.ShapeDtypeStruct((2, 4, 128, 256), BF16),
-            jax.ShapeDtypeStruct((4, 128, 256), BF16),
+            jax.ShapeDtypeStruct((4, 128 + UP, 256), BF16),
+            jax.ShapeDtypeStruct((4, 256 - UP, 256), BF16),
         ),
         in_specs=[pl.BlockSpec(memory_space=pltpu.SMEM)] + vmem(4),
         out_specs=tuple(vmem(2)),
@@ -260,23 +264,29 @@
     )(place, counts, mid, up, down, merge, out_weight)
 
 
-def fetch(place, pieces, weight, sems):
-    copies = []
+def fetch(place, pieces, weight, sems, first=0):
+    zeros, ones = [], []
     for at, (source, y, z, x) in enumerate(pieces):
         yhi, ylo = lax.div(y, 2), lax.rem(y, 2)
-        zero = pltpu.make_async_copy(source, weight.at[yhi, :, ylo, z], sems.at[at])
-        one = pltpu.make_async_copy(source, weight.at[yhi, x, ylo], sems.at[at])
-
-        @pl.when(place[3] == 0)
-        def _():
-            zero.start()
-
-        @pl.when(place[3] == 1)
-        def _():
-            one.start()
-
-        copies.append(zero)
-    return copies
+        rows = pl.ds(first, source.shape[1])
+        zeros.append(
+            pltpu.make_async_copy(source, weight.at[yhi, :, ylo, z, rows], sems.at[at])
+        )
+        ones.append(
+            pltpu.make_async_copy(source, weight.at[yhi, x, ylo, :, rows], sems.at[at])
+        )
+
+    @pl.when(place[3] == 0)
+    def _():
+        for copy in zeros:
+            copy.start()
+
+    @pl.when(place[3] == 1)
+    def _():
+        for copy in ones:
+            copy.start()
+
+    return zeros
 
 
 def fetch_turned(place, parts, weight, sems):
@@ -294,18 +304,19 @@
     )
 
 
-def fetch_down(place, parts, weight, sems):
+def fetch_down(place, parts, rows, weight, sems, first=0):
     x, y, z = place[0], place[1], place[2]
     turn = 1 - 2 * place[3]
     return fetch(
         place,
         [
-            (part.at[slot], along(y, step), along(z, -STEPS[slot]), along(x, -STEPS[slot]))
+            (part.at[slot, :, rows], along(y, step), along(z, -STEPS[slot]), along(x, -STEPS[slot]))
             for part, step in zip(parts, (0, -turn, turn, 2))
             for slot in range(4)
         ],
         weight,
         sems,
+        first,
     )
 
 
@@ -353,14 +364,16 @@
 
 
 def coarse_mlp_kernel(
-    place, own, other, sent, came, u0, u1, u2, u3, d0, d1, d2, d3, base, give, up, down, x, hid, sems, late_sems
+    place, own, other, sent, came, u0, u1, u2, u3, d0, d1, d2, d3, base, give, up, down, x, hid, sems, rest_sems, late_sems
 ):
     copies = fetch_turned(place, (u0, u1, u2, u3), up, sems)
-    late = fetch_down(place, (d0, d1, d2, d3), down, late_sems)
+    downs = (d0, d1, d2, d3)
+    copies += fetch_down(place, downs, pl.ds(128, 128 - UP), up, rest_sems, UP)
     mid = own[:WIN, :] + (sent[0].astype(F32) + came[1].astype(F32))
     base[...] = mid
     x[:WIN, :] = normalised(mid).astype(BF16)
     x[WIN:, :] = normalised(other[:WIN, :] + (sent[1].astype(F32) + came[0].astype(F32))).astype(BF16)
+    late = fetch_down(place, downs, pl.ds(0, 128), down, late_sems)
     for copy in copies:
         copy.wait()
     for h in range(8):
@@ -390,6 +403,7 @@
             pltpu.VMEM((2, 4, 2, 4, 128, 256), BF16),
             pltpu.VMEM((2 * WIN, 2 * C), BF16),
             pltpu.VMEM((8, 2 * WIN, 256), BF16),
+            pltpu.SemaphoreType.DMA((16,)),
             pltpu.SemaphoreType.DMA((16,)),
             pltpu.SemaphoreType.DMA((16,)),
         ],
@@ -468,13 +482,16 @@
     skip, coarse = fine_mlp(place, window_counts, mid, fine_up, fine_down, merge_weight, out_weight)
 
     qu_far, d_far, coarse = lax.optimization_barrier((qu_far, d_far, coarse))
-    q_two, u_two = (jnp.stack([v[i] for v in (qu, qu_one, qu_other, qu_far)]) for i in range(2))
+    qu_all = (qu, qu_one, qu_other, qu_far)
+    q_two, u_two = jnp.stack([v[:, :128] for v in qu_all]), jnp.stack([v[:, 128:] for v in qu_all])
     d_two = jnp.stack([*d_near, d_far])
     q_one, q_other, q_far = (hopped(q_two, ("z", "x"), (step, step)) for step in (1, -1, 2))
-    d_one, d_other = (hopped(d_two, ("y", "y"), (step, -step)) for step in (1, -1))
+    d_one = hopped(d_two, ("y", "y"), (1, -1))
     other = core_swap(coarse)
-    q_other, u_two = lax.optimization_barrier((q_other, u_two))
+    other, u_two, d_late = lax.optimization_barrier((other, u_two, d_two))
+    d_other = hopped(d_late, ("y", "y"), (-1, 1))
     u_parts = direct(u_two, ("z", "x"))
+    q_far, d_one = lax.optimization_barrier((q_far, d_one))
     d_far = hopped(d_one, ("y", "y"), (1, -1))
     sent = coarse_attention(place, coarse, other, (q_two, q_one, q_other, q_far))
     came = core_swap(sent)

time: 111 us -> 109 us (0.982); the launches traced: 110 us -> 107 us
  starting transfers between devices: 59.7 us -> 41.7 us
  waiting for transfers between devices: 12.9 us -> 26.8 us
    ppermute x18, waiting for transfers between devices: 8.13 us -> 23.1 us  [hopped(): return lax.ppermute(value, AXES, pairs)]
    ppermute x18, starting transfers between devices: 38.8 us -> 24.3 us  [hopped(): return lax.ppermute(value, AXES, pairs)]
    ppermute x4, starting transfers between devices: 15.8 us -> 12.4 us  [core_swap(): return lax.ppermute(value, 'core', [(0, 1), (1, 0)])]
    ppermute x1, starting transfers between devices: 5 us -> 3.71 us  [body(): high = lax.ppermute(normed[:WIN], AXES, [(b, a) for a, b in up_one])]
    ppermute x1, starting transfers between devices: 0.01 us -> 1.29 us  [body(): low = lax.ppermute(normed[-WIN:], AXES, up_one)]
where the time goes in v3:
time: 109 us; the launch traced here: 107 us
  starting transfers between devices  41.7 us (38%)
  Pallas kernels  36.5 us (33%)
  waiting for transfers between devices  26.8 us (25%)
    ppermute x18, starting transfers between devices, hopped(): return lax.ppermute(value, AXES, pairs)  24.3 us
    ppermute x18, waiting for transfers between devices, hopped(): return lax.ppermute(value, AXES, pairs)  23.1 us
    ppermute x4, starting transfers between devices, core_swap(): return lax.ppermute(value, 'core', [(0, 1), (1, 0)])  12.4 us
    pallas_call x1, Pallas kernels, coarse_attention(): pl.pallas_call(coarse_attention_kernel, out_shape=jax.ShapeDtypeStruct((2...  10.1 us
    pallas_call x1, Pallas kernels, fine_attention(): pl.pallas_call(fine_attention_kernel, out_shape=jax.ShapeDtypeStruct((row...  9.24 us
    pallas_call x1, Pallas kernels, coarse_mlp(): pl.pallas_call(coarse_mlp_kernel, out_shape=(jax.ShapeDtypeStruct((WIN, 2...  6.43 us
    pallas_call x1, Pallas kernels, fine_mlp(): pl.pallas_call(fine_mlp_kernel, out_shape=(jax.ShapeDtypeStruct((rows, C)...  4.6 us
    ppermute x1, starting transfers between devices, body(): high = lax.ppermute(normed[:WIN], AXES, [(b, a) for a, b in up_one])  3.71 us
  transfers between devices with their start and end apart: 24, of which 10 were waited for; matrix products, arithmetic and copies ran while one was open for 0% of the time, Pallas kernels for 23%

profile of v3, /device:TPU:1, one launch (start us, length us, event | category | flops | bytes accessed | tf_op | source)
XLA Modules:
  0.0 107.2 jit_solution(1860704701725581786)
XLA Ops:
  0.6 2.5 %prepare.1 = (bf16[3,64,256]{2,1,0:T(8,128)(2,1)}, bf16[3,64,256]{2,1,0:T(8,128)(2,1)}) custom-call(s32[4]{0:T(128)} %pad_add_fusion.place, bf16[64,384]{1,0:T(8,128)(2,1)} %refs_0_.1, bf16[64,128]{1,0:T(8,128)(2,1)} %bitcast.31, bf16[64,512]{1,0:T(8,128)(2,1)} %refs_2_.1, bf16[64,512]{1,0:T(8,128)(2,1)} %bitcast.30), custom_call_target="tpu_custom_call" | custom-call | flops 1724999936 | tf_op jit(solution)/shard_map/prepare/pallas_call | solution.py:137
  5.9 1.8 %collective-permute-start.1 = (bf16[3,128,256]{2,1,0:T(8,128)(2,1)S(1)}, bf16[3,128,256]{2,1,0:T(8,128)(2,1)S(1)}, u32[]{:S(2)}, u32[]{:S(2)}) collective-permute-start(bf16[3,128,256]{2,1,0:T(8,128)(2,1)S(1)} %maximum_select_fusion.own), channel_id=1, source_target_pairs={{0,1},{1,2},{2,3},{3,0},{4,5},{5,6},{6,7},{7,4},{8,24},{9,25},{10,... | collective-permute-start | bytes 589832 | tf_op jit(solution)/shard_map/ppermute | solution.py:32
  7.6 2.2 %collective-permute-start.2 = (bf16[3,128,256]{2,1,0:T(8,128)(2,1)S(1)}, bf16[3,128,256]{2,1,0:T(8,128)(2,1)S(1)}, u32[]{:S(2)}, u32[]{:S(2)}) collective-permute-start(bf16[3,128,256]{2,1,0:T(8,128)(2,1)S(1)} %maximum_select_fusion.own), channel_id=1, source_target_pairs={{0,3},{1,0},{2,1},{3,2},{4,7},{5,4},{6,5},{7,6},{8,56},{9,57},{10,... | collective-permute-start | bytes 589832 | tf_op jit(solution)/shard_map/ppermute | solution.py:32
  12.8 1.7 %collective-permute-done.2.r2 = bf16[3,128,256]{2,1,0:T(8,128)(2,1)S(1)} collective-permute-done((bf16[3,128,256]{2,1,0:T(8,128)(2,1)S(1)}, bf16[3,128,256]{2,1,0:T(8,128)(2,1)S(1)}, u32[]{:S(2)}, u32[]{:S(2)}) %collective-permute-start.2) | collective-permute-done | bytes 196640 | tf_op jit(solution)/shard_map/ppermute | solution.py:32
  14.6 1.8 %collective-permute-done.3.r3 = bf16[3,128,256]{2,1,0:T(8,128)(2,1)S(1)} collective-permute-done((bf16[3,128,256]{2,1,0:T(8,128)(2,1)S(1)}, bf16[3,128,256]{2,1,0:T(8,128)(2,1)S(1)}, u32[]{:S(2)}, u32[]{:S(2)}) %collective-permute-start.3) | collective-permute-done | bytes 196640 | tf_op jit(solution)/shard_map/ppermute | solution.py:32
  17.0 2.8 %collective-permute-start.4 = (bf16[4,224,256]{2,1,0:T(8,128)(2,1)S(1)}, bf16[4,224,256]{2,1,0:T(8,128)(2,1)S(1)}, u32[]{:S(2)}, u32[]{:S(2)}) collective-permute-start(bf16[4,224,256]{2,1,0:T(8,128)(2,1)S(1)} %get-tuple-element.47), channel_id=1, source_target_pairs={{0,64},{1,65},{2,66},{3,67},{4,68},{5,69},{6,70},{7,71},{8,76},{9,... | collective-permute-start | bytes 1376264 | tf_op jit(solution)/shard_map/ppermute | solution.py:32
  19.8 3.7 %collective-permute-start.9 = (bf16[144,512]{1,0:T(8,128)(2,1)S(1)}, bf16[144,512]{1,0:T(8,128)(2,1)S(1)}, u32[]{:S(2)}, u32[]{:S(2)}) collective-permute-start(bf16[144,512]{1,0:T(8,128)(2,1)S(1)} %get-tuple-element.61), channel_id=1, source_target_pairs={{1,0},{2,1},{3,2},{4,3},{5,4},{6,5},{7,6},{8,7},{9,8},{10,9},{11,1... | collective-permute-start | bytes 442376 | tf_op jit(solution)/shard_map/ppermute | solution.py:467
  23.5 2.7 %collective-permute-start.7 = (bf16[4,160,256]{2,1,0:T(8,128)(2,1)S(1)}, bf16[4,160,256]{2,1,0:T(8,128)(2,1)S(1)}, u32[]{:S(2)}, u32[]{:S(2)}) collective-permute-start(bf16[4,160,256]{2,1,0:T(8,128)(2,1)S(1)} %get-tuple-element.43), channel_id=1, source_target_pairs={{0,48},{1,49},{2,50},{3,51},{4,52},{5,53},{6,54},{7,55},{8,11},{9,... | collective-permute-start | bytes 983048 | tf_op jit(solution)/shard_map/ppermute | solution.py:32
  27.0 9.2 %fine_attention.1.mid = f32[576,512]{1,0:T(8,128)S(1)} custom-call(s32[1]{0:T(128)S(6)} %copy.15.offset, f32[576,512]{1,0:T(8,128)S(1)} %copy-done.7, bf16[576,512]{1,0:T(8,128)(2,1)S(1)} %norm.1.normed, bf16[144,512]{1,0:T(8,128)(2,1)S(1)} %collective-permute-done.8.low, bf16[144,512]{1,0:T(8,128)(2,1)S(1)} %collective-permute-done.9.high, ...), custom_call_target="tpu_custom_call" | custom-call | flops 2500000000 | bytes 6000000 | tf_op jit(solution)/shard_map/fine_attention/pallas_call | solution.py:207
  37.4 2.2 %collective-permute-start.11 = (bf16[4,160,256]{2,1,0:T(8,128)(2,1)S(1)}, bf16[4,160,256]{2,1,0:T(8,128)(2,1)S(1)}, u32[]{:S(2)}, u32[]{:S(2)}) collective-permute-start(bf16[4,160,256]{2,1,0:T(8,128)(2,1)S(1)} %get-tuple-element.43), channel_id=1, source_target_pairs={{0,32},{1,33},{2,34},{3,35},{4,36},{5,37},{6,38},{7,39},{8,10},{9,... | collective-permute-start | bytes 983048 | tf_op jit(solution)/shard_map/ppermute | solution.py:32
  39.7 4.6 %fine_mlp.1 = (f32[576,512]{1,0:T(8,128)S(1)}, f32[152,1024]{1,0:T(8,128)S(1)}) custom-call(s32[4]{0:T(128)S(1)} %copy-done.2, s32[8]{0:T(128)S(1)} %copy-done.9, f32[576,512]{1,0:T(8,128)S(1)} %fine_attention.1.mid, bf16[512,2048]{1,0:T(8,128)(2,1)S(1)} %copy-done.4, bf16[2048,512]{1,0:T(8,128)(2,1)S(1)} %copy-done.5, bf16[2048,1024]{1,0:T(8,128)(2,1)S(1)} %copy-done.3, ...), custom_call_target="tpu_custom_call" | custom-call | flops 3500000000 | bytes 12000000 | tf_op jit(solution)/shard_map/fine_mlp/pallas_call | solution.py:252
  46.4 2.6 %collective-permute-start.15 = (bf16[4,4,128,256]{3,2,1,0:T(8,128)(2,1)S(1)}, bf16[4,4,128,256]{3,2,1,0:T(8,128)(2,1)S(1)}, u32[]{:S(2)}, u32[]{:S(2)}) collective-permute-start(bf16[4,4,128,256]{3,2,1,0:T(8,128)(2,1)S(1)} %pad_maximum_fusion.1.a0), channel_id=1, source_target_pairs={{0,32},{1,33},{2,34},{3,35},{4,36},{5,37},{6,38},{7,39},{8,10},{9,... | collective-permute-start | bytes 3145736 | tf_op jit(solution)/shard_map/ppermute | solution.py:32
  49.0 4.2 %collective-permute-start.12 = (f32[152,1024]{1,0:T(8,128)S(1)}, f32[152,1024]{1,0:T(8,128)S(1)}, u32[]{:S(2)}, u32[]{:S(2)}) collective-permute-start(f32[152,1024]{1,0:T(8,128)S(1)} %get-tuple-element.46.own), channel_id=1, source_target_pairs={{0,8},{8,0},{1,9},{9,1},{2,10},{10,2},{3,11},{11,3},{4,12},{12,4},... | collective-permute-start | bytes 1867784 | tf_op jit(solution)/shard_map/ppermute | solution.py:40
  54.1 2.1 %collective-permute-start.14 = (bf16[4,4,128,256]{3,2,1,0:T(8,128)(2,1)S(1)}, bf16[4,4,128,256]{3,2,1,0:T(8,128)(2,1)S(1)}, u32[]{:S(2)}, u32[]{:S(2)}) collective-permute-start(bf16[4,4,128,256]{3,2,1,0:T(8,128)(2,1)S(1)} %pad_maximum_fusion.1.a0), channel_id=1, source_target_pairs={{0,48},{1,49},{2,50},{3,51},{4,52},{5,53},{6,54},{7,55},{8,11},{9,... | collective-permute-start | bytes 3145736 | tf_op jit(solution)/shard_map/ppermute | solution.py:32
  56.5 5.5 %collective-permute-done.15.a3 = bf16[4,4,128,256]{3,2,1,0:T(8,128)(2,1)S(1)} collective-permute-done((bf16[4,4,128,256]{3,2,1,0:T(8,128)(2,1)S(1)}, bf16[4,4,128,256]{3,2,1,0:T(8,128)(2,1)S(1)}, u32[]{:S(2)}, u32[]{:S(2)}) %collective-permute-start.15) | collective-permute-done | bytes 1048608 | tf_op jit(solution)/shard_map/ppermute | solution.py:32
  62.6 2.0 %collective-permute-start.22 = (bf16[4,4,160,256]{3,2,1,0:T(8,128)(2,1)S(1)}, bf16[4,4,160,256]{3,2,1,0:T(8,128)(2,1)S(1)}, u32[]{:S(2)}, u32[]{:S(2)}) collective-permute-start(bf16[4,4,160,256]{3,2,1,0:T(8,128)(2,1)S(1)} %collective-permute-done.16.d1), channel_id=1, source_target_pairs={{0,64},{1,65},{2,66},{3,67},{4,68},{5,69},{6,70},{7,71},{8,76},{9,... | collective-permute-start | bytes 3932168 | tf_op jit(solution)/shard_map/ppermute | solution.py:32
  64.6 8.5 %collective-permute-done.13.a1 = bf16[4,4,128,256]{3,2,1,0:T(8,128)(2,1)S(1)} collective-permute-done((bf16[4,4,128,256]{3,2,1,0:T(8,128)(2,1)S(1)}, bf16[4,4,128,256]{3,2,1,0:T(8,128)(2,1)S(1)}, u32[]{:S(2)}, u32[]{:S(2)}) %collective-permute-start.13) | collective-permute-done | bytes 1048608 | tf_op jit(solution)/shard_map/ppermute | solution.py:32
  73.5 4.3 %collective-permute-done.14.a2 = bf16[4,4,128,256]{3,2,1,0:T(8,128)(2,1)S(1)} collective-permute-done((bf16[4,4,128,256]{3,2,1,0:T(8,128)(2,1)S(1)}, bf16[4,4,128,256]{3,2,1,0:T(8,128)(2,1)S(1)}, u32[]{:S(2)}, u32[]{:S(2)}) %collective-permute-start.14) | collective-permute-done | bytes 1048608 | tf_op jit(solution)/shard_map/ppermute | solution.py:32
  78.3 10.1 %coarse_attention.1.sent = bf16[2,144,1024]{2,1,0:T(8,128)(2,1)S(1)} custom-call(s32[4]{0:T(128)S(1)} %copy-done.2, f32[152,1024]{1,0:T(8,128)S(1)} %get-tuple-element.46.own, f32[152,1024]{1,0:T(8,128)S(1)} %collective-permute-done.12.other, bf16[4,4,128,256]{3,2,1,0:T(8,128)(2,1)S(1)} %pad_maximum_fusion.1.a0, ...), custom_call_target="tpu_custom_call" | custom-call | flops 1400000000 | bytes 7000000 | tf_op jit(solution)/shard_map/coarse_attention/pallas_call | solution.py:346
  88.4 3.0 %collective-permute-start.17 = (bf16[2,144,1024]{2,1,0:T(8,128)(2,1)S(1)}, bf16[2,144,1024]{2,1,0:T(8,128)(2,1)S(1)}, u32[]{:S(2)}, u32[]{:S(2)}) collective-permute-start(bf16[2,144,1024]{2,1,0:T(8,128)(2,1)S(1)} %coarse_attention.1.sent), channel_id=1, source_target_pairs={{0,8},{8,0},{1,9},{9,1},{2,10},{10,2},{3,11},{11,3},{4,12},{12,4},... | collective-permute-start | bytes 1769480 | tf_op jit(solution)/shard_map/ppermute | solution.py:40
  91.5 1.6 %collective-permute-done.17.came = bf16[2,144,1024]{2,1,0:T(8,128)(2,1)S(1)} collective-permute-done((bf16[2,144,1024]{2,1,0:T(8,128)(2,1)S(1)}, bf16[2,144,1024]{2,1,0:T(8,128)(2,1)S(1)}, u32[]{:S(2)}, u32[]{:S(2)}) %collective-permute-start.17) | collective-permute-done | bytes 589856 | tf_op jit(solution)/shard_map/ppermute | solution.py:40
  93.1 6.4 %coarse_mlp.1 = (f32[144,1024]{1,0:T(8,128)S(1)}, bf16[144,1024]{1,0:T(8,128)(2,1)S(1)}) custom-call(s32[4]{0:T(128)S(1)} %copy-done.2, f32[152,1024]{1,0:T(8,128)S(1)} %get-tuple-element.46.own, f32[152,1024]{1,0:T(8,128)S(1)} %collective-permute-done.12.other, bf16[2,144,1024]{2,1,0:T(8,128)(2,1)S(1)} %coarse_attention.1.sent, ...), custom_call_target="tpu_custom_call" | custom-call | flops 2400000000 | bytes 14000000 | tf_op jit(solution)/shard_map/coarse_mlp/pallas_call | solution.py:391
  99.6 3.7 %collective-permute-start.23 = (bf16[144,1024]{1,0:T(8,128)(2,1)S(1)}, bf16[144,1024]{1,0:T(8,128)(2,1)S(1)}, u32[]{:S(2)}, u32[]{:S(2)}) collective-permute-start(bf16[144,1024]{1,0:T(8,128)(2,1)S(1)} %get-tuple-element.59), channel_id=1, source_target_pairs={{0,8},{8,0},{1,9},{9,1},{2,10},{10,2},{3,11},{11,3},{4,12},{12,4},... | collective-permute-start | bytes 884744 | tf_op jit(solution)/shard_map/ppermute | solution.py:40
  104.5 2.7 %tail.1 = f32[576,512]{1,0:T(8,128)} custom-call(f32[144,1024]{1,0:T(8,128)S(1)} %get-tuple-element.58.base, bf16[144,1024]{1,0:T(8,128)(2,1)S(1)} %collective-permute-done.23.came, f32[576,512]{1,0:T(8,128)S(1)} %get-tuple-element.60.skip, bf16[1024,2048]{1,0:T(8,128)(2,1)S(1)} %copy-done, bf16[1024,512]{1,0:T(8,128)(2,1)S(1)} %copy-done.1), custom_call_target="tpu_custom_call" | custom-call | flops 900000000 | bytes 8000000 | tf_op jit(solution)/shard_map/tail/pallas_call | solution.py:429
  (65 shorter events, 14.1 us)
Async XLA Ops:
  3.1 2.6 %collective-permute-start = (bf16[3,64,256]{2,1,0:T(8,128)(2,1)}, bf16[3,64,256]{2,1,0:T(8,128)(2,1)S(1)}, u32[]{:S(2)}, u32[]{:S(2)}) collective-permute-start(bf16[3,64,256]{2,1,0:T(8,128)(2,1)} %get-tuple-element.35), channel_id=1, source_target_pairs={{0,8},{8,0},{1,9},{9,1},{2,10},{10,2},{3,11},{11,3},{4,12},{12,4},... | collective-permute-start | bytes 294920 | tf_op jit(solution)/shard_map/ppermute | solution.py:40
  5.9 7.0 %collective-permute-start.1 = (bf16[3,128,256]{2,1,0:T(8,128)(2,1)S(1)}, bf16[3,128,256]{2,1,0:T(8,128)(2,1)S(1)}, u32[]{:S(2)}, u32[]{:S(2)}) collective-permute-start(bf16[3,128,256]{2,1,0:T(8,128)(2,1)S(1)} %maximum_select_fusion.own), channel_id=1, source_target_pairs={{0,1},{1,2},{2,3},{3,0},{4,5},{5,6},{6,7},{7,4},{8,24},{9,25},{10,... | collective-permute-start | bytes 589832 | tf_op jit(solution)/shard_map/ppermute | solution.py:32
  7.6 6.9 %collective-permute-start.2 = (bf16[3,128,256]{2,1,0:T(8,128)(2,1)S(1)}, bf16[3,128,256]{2,1,0:T(8,128)(2,1)S(1)}, u32[]{:S(2)}, u32[]{:S(2)}) collective-permute-start(bf16[3,128,256]{2,1,0:T(8,128)(2,1)S(1)} %maximum_select_fusion.own), channel_id=1, source_target_pairs={{0,3},{1,0},{2,1},{3,2},{4,7},{5,4},{6,5},{7,6},{8,56},{9,57},{10,... | collective-permute-start | bytes 589832 | tf_op jit(solution)/shard_map/ppermute | solution.py:32
  9.9 6.6 %collective-permute-start.3 = (bf16[3,128,256]{2,1,0:T(8,128)(2,1)S(1)}, bf16[3,128,256]{2,1,0:T(8,128)(2,1)S(1)}, u32[]{:S(2)}, u32[]{:S(2)}) collective-permute-start(bf16[3,128,256]{2,1,0:T(8,128)(2,1)S(1)} %maximum_select_fusion.own), channel_id=1, source_target_pairs={{0,2},{1,3},{2,0},{3,1},{4,6},{5,7},{6,4},{7,5},{8,40},{9,41},{10,... | collective-permute-start | bytes 589832 | tf_op jit(solution)/shard_map/ppermute | solution.py:32
  11.1 12.4 %collective-permute-start.8 = (bf16[144,512]{1,0:T(8,128)(2,1)S(1)}, bf16[144,512]{1,0:T(8,128)(2,1)S(1)}, u32[]{:S(2)}, u32[]{:S(2)}) collective-permute-start(bf16[144,512]{1,0:T(8,128)(2,1)S(1)} %get-tuple-element.62), channel_id=1, source_target_pairs={{0,1},{1,2},{2,3},{3,4},{4,5},{5,6},{6,7},{7,8},{8,9},{9,10},{10,1... | collective-permute-start | bytes 442376 | tf_op jit(solution)/shard_map/ppermute | solution.py:466
  17.0 19.2 %collective-permute-start.4 = (bf16[4,224,256]{2,1,0:T(8,128)(2,1)S(1)}, bf16[4,224,256]{2,1,0:T(8,128)(2,1)S(1)}, u32[]{:S(2)}, u32[]{:S(2)}) collective-permute-start(bf16[4,224,256]{2,1,0:T(8,128)(2,1)S(1)} %get-tuple-element.47), channel_id=1, source_target_pairs={{0,64},{1,65},{2,66},{3,67},{4,68},{5,69},{6,70},{7,71},{8,76},{9,... | collective-permute-start | bytes 1376264 | tf_op jit(solution)/shard_map/ppermute | solution.py:32
  19.8 16.4 %collective-permute-start.5 = (bf16[4,224,256]{2,1,0:T(8,128)(2,1)S(1)}, bf16[4,224,256]{2,1,0:T(8,128)(2,1)S(1)}, u32[]{:S(2)}, u32[]{:S(2)}) collective-permute-start(bf16[4,224,256]{2,1,0:T(8,128)(2,1)S(1)} %get-tuple-element.47), channel_id=1, source_target_pairs={{0,68},{1,69},{2,70},{3,71},{4,64},{5,65},{6,66},{7,67},{8,72},{9,... | collective-permute-start | bytes 1376264 | tf_op jit(solution)/shard_map/ppermute | solution.py:32
  19.8 7.1 %collective-permute-start.9 = (bf16[144,512]{1,0:T(8,128)(2,1)S(1)}, bf16[144,512]{1,0:T(8,128)(2,1)S(1)}, u32[]{:S(2)}, u32[]{:S(2)}) collective-permute-start(bf16[144,512]{1,0:T(8,128)(2,1)S(1)} %get-tuple-element.61), channel_id=1, source_target_pairs={{1,0},{2,1},{3,2},{4,3},{5,4},{6,5},{7,6},{8,7},{9,8},{10,9},{11,1... | collective-permute-start | bytes 442376 | tf_op jit(solution)/shard_map/ppermute | solution.py:467
  23.5 12.7 %collective-permute-start.6 = (bf16[4,160,256]{2,1,0:T(8,128)(2,1)S(1)}, bf16[4,160,256]{2,1,0:T(8,128)(2,1)S(1)}, u32[]{:S(2)}, u32[]{:S(2)}) collective-permute-start(bf16[4,160,256]{2,1,0:T(8,128)(2,1)S(1)} %get-tuple-element.43), channel_id=1, source_target_pairs={{0,16},{1,17},{2,18},{3,19},{4,20},{5,21},{6,22},{7,23},{8,9},{9,1... | collective-permute-start | bytes 983048 | tf_op jit(solution)/shard_map/ppermute | solution.py:32
  23.5 12.7 %collective-permute-start.7 = (bf16[4,160,256]{2,1,0:T(8,128)(2,1)S(1)}, bf16[4,160,256]{2,1,0:T(8,128)(2,1)S(1)}, u32[]{:S(2)}, u32[]{:S(2)}) collective-permute-start(bf16[4,160,256]{2,1,0:T(8,128)(2,1)S(1)} %get-tuple-element.43), channel_id=1, source_target_pairs={{0,48},{1,49},{2,50},{3,51},{4,52},{5,53},{6,54},{7,55},{8,11},{9,... | collective-permute-start | bytes 983048 | tf_op jit(solution)/shard_map/ppermute | solution.py:32
  36.3 8.9 %collective-permute-start.10 = (bf16[4,224,256]{2,1,0:T(8,128)(2,1)S(1)}, bf16[4,224,256]{2,1,0:T(8,128)(2,1)S(1)}, u32[]{:S(2)}, u32[]{:S(2)}) collective-permute-start(bf16[4,224,256]{2,1,0:T(8,128)(2,1)S(1)} %collective-permute-done.4), channel_id=1, source_target_pairs={{0,64},{1,65},{2,66},{3,67},{4,68},{5,69},{6,70},{7,71},{8,76},{9,... | collective-permute-start | bytes 1376264 | tf_op jit(solution)/shard_map/ppermute | solution.py:32
  37.4 7.7 %collective-permute-start.11 = (bf16[4,160,256]{2,1,0:T(8,128)(2,1)S(1)}, bf16[4,160,256]{2,1,0:T(8,128)(2,1)S(1)}, u32[]{:S(2)}, u32[]{:S(2)}) collective-permute-start(bf16[4,160,256]{2,1,0:T(8,128)(2,1)S(1)} %get-tuple-element.43), channel_id=1, source_target_pairs={{0,32},{1,33},{2,34},{3,35},{4,36},{5,37},{6,38},{7,39},{8,10},{9,... | collective-permute-start | bytes 983048 | tf_op jit(solution)/shard_map/ppermute | solution.py:32
  45.3 17.3 %collective-permute-start.16 = (bf16[4,4,160,256]{3,2,1,0:T(8,128)(2,1)S(1)}, bf16[4,4,160,256]{3,2,1,0:T(8,128)(2,1)S(1)}, u32[]{:S(2)}, u32[]{:S(2)}) collective-permute-start(bf16[4,4,160,256]{3,2,1,0:T(8,128)(2,1)S(1)} %pad_maximum_fusion.d0), channel_id=1, source_target_pairs={{0,64},{1,65},{2,66},{3,67},{4,68},{5,69},{6,70},{7,71},{8,76},{9,... | collective-permute-start | bytes 3932168 | tf_op jit(solution)/shard_map/ppermute | solution.py:32
  46.4 15.6 %collective-permute-start.15 = (bf16[4,4,128,256]{3,2,1,0:T(8,128)(2,1)S(1)}, bf16[4,4,128,256]{3,2,1,0:T(8,128)(2,1)S(1)}, u32[]{:S(2)}, u32[]{:S(2)}) collective-permute-start(bf16[4,4,128,256]{3,2,1,0:T(8,128)(2,1)S(1)} %pad_maximum_fusion.1.a0), channel_id=1, source_target_pairs={{0,32},{1,33},{2,34},{3,35},{4,36},{5,37},{6,38},{7,39},{8,10},{9,... | collective-permute-start | bytes 3145736 | tf_op jit(solution)/shard_map/ppermute | solution.py:32
  49.0 7.4 %collective-permute-start.12 = (f32[152,1024]{1,0:T(8,128)S(1)}, f32[152,1024]{1,0:T(8,128)S(1)}, u32[]{:S(2)}, u32[]{:S(2)}) collective-permute-start(f32[152,1024]{1,0:T(8,128)S(1)} %get-tuple-element.46.own), channel_id=1, source_target_pairs={{0,8},{8,0},{1,9},{9,1},{2,10},{10,2},{3,11},{11,3},{4,12},{12,4},... | collective-permute-start | bytes 1867784 | tf_op jit(solution)/shard_map/ppermute | solution.py:40
  53.2 20.0 %collective-permute-start.13 = (bf16[4,4,128,256]{3,2,1,0:T(8,128)(2,1)S(1)}, bf16[4,4,128,256]{3,2,1,0:T(8,128)(2,1)S(1)}, u32[]{:S(2)}, u32[]{:S(2)}) collective-permute-start(bf16[4,4,128,256]{3,2,1,0:T(8,128)(2,1)S(1)} %pad_maximum_fusion.1.a0), channel_id=1, source_target_pairs={{0,16},{1,17},{2,18},{3,19},{4,20},{5,21},{6,22},{7,23},{8,9},{9,1... | collective-permute-start | bytes 3145736 | tf_op jit(solution)/shard_map/ppermute | solution.py:32
  54.1 23.7 %collective-permute-start.14 = (bf16[4,4,128,256]{3,2,1,0:T(8,128)(2,1)S(1)}, bf16[4,4,128,256]{3,2,1,0:T(8,128)(2,1)S(1)}, u32[]{:S(2)}, u32[]{:S(2)}) collective-permute-start(bf16[4,4,128,256]{3,2,1,0:T(8,128)(2,1)S(1)} %pad_maximum_fusion.1.a0), channel_id=1, source_target_pairs={{0,48},{1,49},{2,50},{3,51},{4,52},{5,53},{6,54},{7,55},{8,11},{9,... | collective-permute-start | bytes 3145736 | tf_op jit(solution)/shard_map/ppermute | solution.py:32
  56.4 32.1 %collective-permute-start.18 = (bf16[4,4,96,256]{3,2,1,0:T(8,128)(2,1)S(1)}, bf16[4,4,96,256]{3,2,1,0:T(8,128)(2,1)S(1)}, u32[]{:S(2)}, u32[]{:S(2)}) collective-permute-start(bf16[4,4,96,256]{3,2,1,0:T(8,128)(2,1)S(1)} %pad_maximum_fusion.2.u0), channel_id=1, source_target_pairs={{0,16},{1,17},{2,18},{3,19},{4,20},{5,21},{6,22},{7,23},{8,9},{9,1... | collective-permute-start | bytes 2359304 | tf_op jit(solution)/shard_map/ppermute | solution.py:32
  61.9 31.2 %collective-permute-start.21 = (bf16[4,4,160,256]{3,2,1,0:T(8,128)(2,1)S(1)}, bf16[4,4,160,256]{3,2,1,0:T(8,128)(2,1)S(1)}, u32[]{:S(2)}, u32[]{:S(2)}) collective-permute-start(bf16[4,4,160,256]{3,2,1,0:T(8,128)(2,1)S(1)} %pad_maximum_fusion.d0), channel_id=1, source_target_pairs={{0,68},{1,69},{2,70},{3,71},{4,64},{5,65},{6,66},{7,67},{8,72},{9,... | collective-permute-start | bytes 3932168 | tf_op jit(solution)/shard_map/ppermute | solution.py:32
  62.6 30.5 %collective-permute-start.22 = (bf16[4,4,160,256]{3,2,1,0:T(8,128)(2,1)S(1)}, bf16[4,4,160,256]{3,2,1,0:T(8,128)(2,1)S(1)}, u32[]{:S(2)}, u32[]{:S(2)}) collective-permute-start(bf16[4,4,160,256]{3,2,1,0:T(8,128)(2,1)S(1)} %collective-permute-done.16.d1), channel_id=1, source_target_pairs={{0,64},{1,65},{2,66},{3,67},{4,68},{5,69},{6,70},{7,71},{8,76},{9,... | collective-permute-start | bytes 3932168 | tf_op jit(solution)/shard_map/ppermute | solution.py:32
  73.1 18.3 %collective-permute-start.19 = (bf16[4,4,96,256]{3,2,1,0:T(8,128)(2,1)S(1)}, bf16[4,4,96,256]{3,2,1,0:T(8,128)(2,1)S(1)}, u32[]{:S(2)}, u32[]{:S(2)}) collective-permute-start(bf16[4,4,96,256]{3,2,1,0:T(8,128)(2,1)S(1)} %pad_maximum_fusion.2.u0), channel_id=1, source_target_pairs={{0,48},{1,49},{2,50},{3,51},{4,52},{5,53},{6,54},{7,55},{8,11},{9,... | collective-permute-start | bytes 2359304 | tf_op jit(solution)/shard_map/ppermute | solution.py:32
  77.7 13.8 %collective-permute-start.20 = (bf16[4,4,96,256]{3,2,1,0:T(8,128)(2,1)S(1)}, bf16[4,4,96,256]{3,2,1,0:T(8,128)(2,1)S(1)}, u32[]{:S(2)}, u32[]{:S(2)}) collective-permute-start(bf16[4,4,96,256]{3,2,1,0:T(8,128)(2,1)S(1)} %pad_maximum_fusion.2.u0), channel_id=1, source_target_pairs={{0,32},{1,33},{2,34},{3,35},{4,36},{5,37},{6,38},{7,39},{8,10},{9,... | collective-permute-start | bytes 2359304 | tf_op jit(solution)/shard_map/ppermute | solution.py:32
  88.4 4.7 %collective-permute-start.17 = (bf16[2,144,1024]{2,1,0:T(8,128)(2,1)S(1)}, bf16[2,144,1024]{2,1,0:T(8,128)(2,1)S(1)}, u32[]{:S(2)}, u32[]{:S(2)}) collective-permute-start(bf16[2,144,1024]{2,1,0:T(8,128)(2,1)S(1)} %coarse_attention.1.sent), channel_id=1, source_target_pairs={{0,8},{8,0},{1,9},{9,1},{2,10},{10,2},{3,11},{11,3},{4,12},{12,4},... | collective-permute-start | bytes 1769480 | tf_op jit(solution)/shard_map/ppermute | solution.py:40
  99.6 4.9 %collective-permute-start.23 = (bf16[144,1024]{1,0:T(8,128)(2,1)S(1)}, bf16[144,1024]{1,0:T(8,128)(2,1)S(1)}, u32[]{:S(2)}, u32[]{:S(2)}) collective-permute-start(bf16[144,1024]{1,0:T(8,128)(2,1)S(1)} %get-tuple-element.59), channel_id=1, source_target_pairs={{0,8},{8,0},{1,9},{9,1},{2,10},{10,2},{3,11},{11,3},{4,12},{12,4},... | collective-permute-start | bytes 884744 | tf_op jit(solution)/shard_map/ppermute | solution.py:40
  (11 other events, 124.0 us)

commit v4 on v3

--- a/solution.py
+++ b/solution.py
@@ -380,11 +380,16 @@
         hid[h] = gelu(dot(x[...], whole(up, h))).astype(BF16)
     for copy in late:
         copy.wait()
-    result = dot_t(hid[0], whole(down, 0))
-    for h in range(1, 8):
-        result = result + dot_t(hid[h], whole(down, h))
-    base[...] += result[:WIN]
-    give[...] = result[WIN:].astype(BF16)
+    for chunk in range(4):
+        ylo, z = chunk // 2, chunk % 2 * 2
+        result = None
+        for h in range(8):
+            block = down[h // 4, h % 4, ylo, z : z + 2].reshape(256, 256)
+            term = dot_t(hid[h], block)
+            result = term if result is None else result + term
+        at = slice(chunk * 256, (chunk + 1) * 256)
+        base[:, at] += result[:WIN]
+        give[:, at] = result[WIN:].astype(BF16)
 
 
 def coarse_mlp(place, own, other, sent, came, ups, downs):

time: 109 us -> 109 us (level)
  no operation moved by 1% of the time
where the time goes in v4:
time: 109 us; the launch traced here: 107 us
  starting transfers between devices  41.7 us (38%)
  Pallas kernels  36.5 us (33%)
  waiting for transfers between devices  26.7 us (24%)
    ppermute x18, starting transfers between devices, hopped(): return lax.ppermute(value, AXES, pairs)  24.3 us
    ppermute x18, waiting for transfers between devices, hopped(): return lax.ppermute(value, AXES, pairs)  23.1 us
    ppermute x4, starting transfers between devices, core_swap(): return lax.ppermute(value, 'core', [(0, 1), (1, 0)])  12.4 us
    pallas_call x1, Pallas kernels, coarse_attention(): pl.pallas_call(coarse_attention_kernel, out_shape=jax.ShapeDtypeStruct((2...  10.1 us
    pallas_call x1, Pallas kernels, fine_attention(): pl.pallas_call(fine_attention_kernel, out_shape=jax.ShapeDtypeStruct((row...  9.24 us
    pallas_call x1, Pallas kernels, coarse_mlp(): pl.pallas_call(coarse_mlp_kernel, out_shape=(jax.ShapeDtypeStruct((WIN, 2...  6.43 us
    pallas_call x1, Pallas kernels, fine_mlp(): pl.pallas_call(fine_mlp_kernel, out_shape=(jax.ShapeDtypeStruct((rows, C)...  4.6 us
    ppermute x1, starting transfers between devices, body(): high = lax.ppermute(normed[:WIN], AXES, [(b, a) for a, b in up_one])  3.71 us
  transfers between devices with their start and end apart: 24, of which 10 were waited for; matrix products, arithmetic and copies ran while one was open for 0% of the time, Pallas kernels for 23%

profile of v4, /device:TPU:1, one launch (start us, length us, event | category | flops | bytes accessed | tf_op | source)
XLA Modules:
  0.0 107.2 jit_solution(12685133038107604459)
XLA Ops:
  0.6 2.5 %prepare.1 = (bf16[3,64,256]{2,1,0:T(8,128)(2,1)}, bf16[3,64,256]{2,1,0:T(8,128)(2,1)}) custom-call(s32[4]{0:T(128)} %pad_add_fusion.place, bf16[64,384]{1,0:T(8,128)(2,1)} %refs_0_.1, bf16[64,128]{1,0:T(8,128)(2,1)} %bitcast.31, bf16[64,512]{1,0:T(8,128)(2,1)} %refs_2_.1, bf16[64,512]{1,0:T(8,128)(2,1)} %bitcast.30), custom_call_target="tpu_custom_call" | custom-call | flops 1724999936 | tf_op jit(solution)/shard_map/prepare/pallas_call | solution.py:137
  5.9 1.8 %collective-permute-start.1 = (bf16[3,128,256]{2,1,0:T(8,128)(2,1)S(1)}, bf16[3,128,256]{2,1,0:T(8,128)(2,1)S(1)}, u32[]{:S(2)}, u32[]{:S(2)}) collective-permute-start(bf16[3,128,256]{2,1,0:T(8,128)(2,1)S(1)} %maximum_select_fusion.own), channel_id=1, source_target_pairs={{0,1},{1,2},{2,3},{3,0},{4,5},{5,6},{6,7},{7,4},{8,24},{9,25},{10,... | collective-permute-start | bytes 589832 | tf_op jit(solution)/shard_map/ppermute | solution.py:32
  7.6 2.2 %collective-permute-start.2 = (bf16[3,128,256]{2,1,0:T(8,128)(2,1)S(1)}, bf16[3,128,256]{2,1,0:T(8,128)(2,1)S(1)}, u32[]{:S(2)}, u32[]{:S(2)}) collective-permute-start(bf16[3,128,256]{2,1,0:T(8,128)(2,1)S(1)} %maximum_select_fusion.own), channel_id=1, source_target_pairs={{0,3},{1,0},{2,1},{3,2},{4,7},{5,4},{6,5},{7,6},{8,56},{9,57},{10,... | collective-permute-start | bytes 589832 | tf_op jit(solution)/shard_map/ppermute | solution.py:32
  12.8 1.7 %collective-permute-done.2.r2 = bf16[3,128,256]{2,1,0:T(8,128)(2,1)S(1)} collective-permute-done((bf16[3,128,256]{2,1,0:T(8,128)(2,1)S(1)}, bf16[3,128,256]{2,1,0:T(8,128)(2,1)S(1)}, u32[]{:S(2)}, u32[]{:S(2)}) %collective-permute-start.2) | collective-permute-done | bytes 196640 | tf_op jit(solution)/shard_map/ppermute | solution.py:32
  14.6 1.8 %collective-permute-done.3.r3 = bf16[3,128,256]{2,1,0:T(8,128)(2,1)S(1)} collective-permute-done((bf16[3,128,256]{2,1,0:T(8,128)(2,1)S(1)}, bf16[3,128,256]{2,1,0:T(8,128)(2,1)S(1)}, u32[]{:S(2)}, u32[]{:S(2)}) %collective-permute-start.3) | collective-permute-done | bytes 196640 | tf_op jit(solution)/shard_map/ppermute | solution.py:32
  17.0 2.8 %collective-permute-start.4 = (bf16[4,224,256]{2,1,0:T(8,128)(2,1)S(1)}, bf16[4,224,256]{2,1,0:T(8,128)(2,1)S(1)}, u32[]{:S(2)}, u32[]{:S(2)}) collective-permute-start(bf16[4,224,256]{2,1,0:T(8,128)(2,1)S(1)} %get-tuple-element.47), channel_id=1, source_target_pairs={{0,64},{1,65},{2,66},{3,67},{4,68},{5,69},{6,70},{7,71},{8,76},{9,... | collective-permute-start | bytes 1376264 | tf_op jit(solution)/shard_map/ppermute | solution.py:32
  19.8 3.7 %collective-permute-start.9 = (bf16[144,512]{1,0:T(8,128)(2,1)S(1)}, bf16[144,512]{1,0:T(8,128)(2,1)S(1)}, u32[]{:S(2)}, u32[]{:S(2)}) collective-permute-start(bf16[144,512]{1,0:T(8,128)(2,1)S(1)} %get-tuple-element.61), channel_id=1, source_target_pairs={{1,0},{2,1},{3,2},{4,3},{5,4},{6,5},{7,6},{8,7},{9,8},{10,9},{11,1... | collective-permute-start | bytes 442376 | tf_op jit(solution)/shard_map/ppermute | solution.py:472
  23.5 2.7 %collective-permute-start.7 = (bf16[4,160,256]{2,1,0:T(8,128)(2,1)S(1)}, bf16[4,160,256]{2,1,0:T(8,128)(2,1)S(1)}, u32[]{:S(2)}, u32[]{:S(2)}) collective-permute-start(bf16[4,160,256]{2,1,0:T(8,128)(2,1)S(1)} %get-tuple-element.43), channel_id=1, source_target_pairs={{0,48},{1,49},{2,50},{3,51},{4,52},{5,53},{6,54},{7,55},{8,11},{9,... | collective-permute-start | bytes 983048 | tf_op jit(solution)/shard_map/ppermute | solution.py:32
  27.0 9.2 %fine_attention.1.mid = f32[576,512]{1,0:T(8,128)S(1)} custom-call(s32[1]{0:T(128)S(6)} %copy.15.offset, f32[576,512]{1,0:T(8,128)S(1)} %copy-done.7, bf16[576,512]{1,0:T(8,128)(2,1)S(1)} %norm.1.normed, bf16[144,512]{1,0:T(8,128)(2,1)S(1)} %collective-permute-done.8.low, bf16[144,512]{1,0:T(8,128)(2,1)S(1)} %collective-permute-done.9.high, ...), custom_call_target="tpu_custom_call" | custom-call | flops 2500000000 | bytes 6000000 | tf_op jit(solution)/shard_map/fine_attention/pallas_call | solution.py:207
  37.4 2.2 %collective-permute-start.11 = (bf16[4,160,256]{2,1,0:T(8,128)(2,1)S(1)}, bf16[4,160,256]{2,1,0:T(8,128)(2,1)S(1)}, u32[]{:S(2)}, u32[]{:S(2)}) collective-permute-start(bf16[4,160,256]{2,1,0:T(8,128)(2,1)S(1)} %get-tuple-element.43), channel_id=1, source_target_pairs={{0,32},{1,33},{2,34},{3,35},{4,36},{5,37},{6,38},{7,39},{8,10},{9,... | collective-permute-start | bytes 983048 | tf_op jit(solution)/shard_map/ppermute | solution.py:32
  39.7 4.6 %fine_mlp.1 = (f32[576,512]{1,0:T(8,128)S(1)}, f32[152,1024]{1,0:T(8,128)S(1)}) custom-call(s32[4]{0:T(128)S(1)} %copy-done.2, s32[8]{0:T(128)S(1)} %copy-done.9, f32[576,512]{1,0:T(8,128)S(1)} %fine_attention.1.mid, bf16[512,2048]{1,0:T(8,128)(2,1)S(1)} %copy-done.4, bf16[2048,512]{1,0:T(8,128)(2,1)S(1)} %copy-done.5, bf16[2048,1024]{1,0:T(8,128)(2,1)S(1)} %copy-done.3, ...), custom_call_target="tpu_custom_call" | custom-call | flops 3500000000 | bytes 12000000 | tf_op jit(solution)/shard_map/fine_mlp/pallas_call | solution.py:252
  46.4 2.6 %collective-permute-start.15 = (bf16[4,4,128,256]{3,2,1,0:T(8,128)(2,1)S(1)}, bf16[4,4,128,256]{3,2,1,0:T(8,128)(2,1)S(1)}, u32[]{:S(2)}, u32[]{:S(2)}) collective-permute-start(bf16[4,4,128,256]{3,2,1,0:T(8,128)(2,1)S(1)} %pad_maximum_fusion.1.a0), channel_id=1, source_target_pairs={{0,32},{1,33},{2,34},{3,35},{4,36},{5,37},{6,38},{7,39},{8,10},{9,... | collective-permute-start | bytes 3145736 | tf_op jit(solution)/shard_map/ppermute | solution.py:32
  49.0 4.2 %collective-permute-start.12 = (f32[152,1024]{1,0:T(8,128)S(1)}, f32[152,1024]{1,0:T(8,128)S(1)}, u32[]{:S(2)}, u32[]{:S(2)}) collective-permute-start(f32[152,1024]{1,0:T(8,128)S(1)} %get-tuple-element.46.own), channel_id=1, source_target_pairs={{0,8},{8,0},{1,9},{9,1},{2,10},{10,2},{3,11},{11,3},{4,12},{12,4},... | collective-permute-start | bytes 1867784 | tf_op jit(solution)/shard_map/ppermute | solution.py:40
  54.1 2.1 %collective-permute-start.14 = (bf16[4,4,128,256]{3,2,1,0:T(8,128)(2,1)S(1)}, bf16[4,4,128,256]{3,2,1,0:T(8,128)(2,1)S(1)}, u32[]{:S(2)}, u32[]{:S(2)}) collective-permute-start(bf16[4,4,128,256]{3,2,1,0:T(8,128)(2,1)S(1)} %pad_maximum_fusion.1.a0), channel_id=1, source_target_pairs={{0,48},{1,49},{2,50},{3,51},{4,52},{5,53},{6,54},{7,55},{8,11},{9,... | collective-permute-start | bytes 3145736 | tf_op jit(solution)/shard_map/ppermute | solution.py:32
  56.5 5.5 %collective-permute-done.15.a3 = bf16[4,4,128,256]{3,2,1,0:T(8,128)(2,1)S(1)} collective-permute-done((bf16[4,4,128,256]{3,2,1,0:T(8,128)(2,1)S(1)}, bf16[4,4,128,256]{3,2,1,0:T(8,128)(2,1)S(1)}, u32[]{:S(2)}, u32[]{:S(2)}) %collective-permute-start.15) | collective-permute-done | bytes 1048608 | tf_op jit(solution)/shard_map/ppermute | solution.py:32
  62.6 2.0 %collective-permute-start.22 = (bf16[4,4,160,256]{3,2,1,0:T(8,128)(2,1)S(1)}, bf16[4,4,160,256]{3,2,1,0:T(8,128)(2,1)S(1)}, u32[]{:S(2)}, u32[]{:S(2)}) collective-permute-start(bf16[4,4,160,256]{3,2,1,0:T(8,128)(2,1)S(1)} %collective-permute-done.16.d1), channel_id=1, source_target_pairs={{0,64},{1,65},{2,66},{3,67},{4,68},{5,69},{6,70},{7,71},{8,76},{9,... | collective-permute-start | bytes 3932168 | tf_op jit(solution)/shard_map/ppermute | solution.py:32
  64.6 8.5 %collective-permute-done.13.a1 = bf16[4,4,128,256]{3,2,1,0:T(8,128)(2,1)S(1)} collective-permute-done((bf16[4,4,128,256]{3,2,1,0:T(8,128)(2,1)S(1)}, bf16[4,4,128,256]{3,2,1,0:T(8,128)(2,1)S(1)}, u32[]{:S(2)}, u32[]{:S(2)}) %collective-permute-start.13) | collective-permute-done | bytes 1048608 | tf_op jit(solution)/shard_map/ppermute | solution.py:32
  73.5 4.3 %collective-permute-done.14.a2 = bf16[4,4,128,256]{3,2,1,0:T(8,128)(2,1)S(1)} collective-permute-done((bf16[4,4,128,256]{3,2,1,0:T(8,128)(2,1)S(1)}, bf16[4,4,128,256]{3,2,1,0:T(8,128)(2,1)S(1)}, u32[]{:S(2)}, u32[]{:S(2)}) %collective-permute-start.14) | collective-permute-done | bytes 1048608 | tf_op jit(solution)/shard_map/ppermute | solution.py:32
  78.3 10.1 %coarse_attention.1.sent = bf16[2,144,1024]{2,1,0:T(8,128)(2,1)S(1)} custom-call(s32[4]{0:T(128)S(1)} %copy-done.2, f32[152,1024]{1,0:T(8,128)S(1)} %get-tuple-element.46.own, f32[152,1024]{1,0:T(8,128)S(1)} %collective-permute-done.12.other, bf16[4,4,128,256]{3,2,1,0:T(8,128)(2,1)S(1)} %pad_maximum_fusion.1.a0, ...), custom_call_target="tpu_custom_call" | custom-call | flops 1400000000 | bytes 7000000 | tf_op jit(solution)/shard_map/coarse_attention/pallas_call | solution.py:346
  88.4 3.0 %collective-permute-start.17 = (bf16[2,144,1024]{2,1,0:T(8,128)(2,1)S(1)}, bf16[2,144,1024]{2,1,0:T(8,128)(2,1)S(1)}, u32[]{:S(2)}, u32[]{:S(2)}) collective-permute-start(bf16[2,144,1024]{2,1,0:T(8,128)(2,1)S(1)} %coarse_attention.1.sent), channel_id=1, source_target_pairs={{0,8},{8,0},{1,9},{9,1},{2,10},{10,2},{3,11},{11,3},{4,12},{12,4},... | collective-permute-start | bytes 1769480 | tf_op jit(solution)/shard_map/ppermute | solution.py:40
  91.5 1.6 %collective-permute-done.17.came = bf16[2,144,1024]{2,1,0:T(8,128)(2,1)S(1)} collective-permute-done((bf16[2,144,1024]{2,1,0:T(8,128)(2,1)S(1)}, bf16[2,144,1024]{2,1,0:T(8,128)(2,1)S(1)}, u32[]{:S(2)}, u32[]{:S(2)}) %collective-permute-start.17) | collective-permute-done | bytes 589856 | tf_op jit(solution)/shard_map/ppermute | solution.py:40
  93.1 6.4 %coarse_mlp.1 = (f32[144,1024]{1,0:T(8,128)S(1)}, bf16[144,1024]{1,0:T(8,128)(2,1)S(1)}) custom-call(s32[4]{0:T(128)S(1)} %copy-done.2, f32[152,1024]{1,0:T(8,128)S(1)} %get-tuple-element.46.own, f32[152,1024]{1,0:T(8,128)S(1)} %collective-permute-done.12.other, bf16[2,144,1024]{2,1,0:T(8,128)(2,1)S(1)} %coarse_attention.1.sent, ...), custom_call_target="tpu_custom_call" | custom-call | flops 2400000000 | bytes 14000000 | tf_op jit(solution)/shard_map/coarse_mlp/pallas_call | solution.py:396
  99.6 3.7 %collective-permute-start.23 = (bf16[144,1024]{1,0:T(8,128)(2,1)S(1)}, bf16[144,1024]{1,0:T(8,128)(2,1)S(1)}, u32[]{:S(2)}, u32[]{:S(2)}) collective-permute-start(bf16[144,1024]{1,0:T(8,128)(2,1)S(1)} %get-tuple-element.59), channel_id=1, source_target_pairs={{0,8},{8,0},{1,9},{9,1},{2,10},{10,2},{3,11},{11,3},{4,12},{12,4},... | collective-permute-start | bytes 884744 | tf_op jit(solution)/shard_map/ppermute | solution.py:40
  104.5 2.7 %tail.1 = f32[576,512]{1,0:T(8,128)} custom-call(f32[144,1024]{1,0:T(8,128)S(1)} %get-tuple-element.58.base, bf16[144,1024]{1,0:T(8,128)(2,1)S(1)} %collective-permute-done.23.came, f32[576,512]{1,0:T(8,128)S(1)} %get-tuple-element.60.skip, bf16[1024,2048]{1,0:T(8,128)(2,1)S(1)} %copy-done, bf16[1024,512]{1,0:T(8,128)(2,1)S(1)} %copy-done.1), custom_call_target="tpu_custom_call" | custom-call | flops 900000000 | bytes 8000000 | tf_op jit(solution)/shard_map/tail/pallas_call | solution.py:434
  (65 shorter events, 14.1 us)
Async XLA Ops:
  3.1 2.6 %collective-permute-start = (bf16[3,64,256]{2,1,0:T(8,128)(2,1)}, bf16[3,64,256]{2,1,0:T(8,128)(2,1)S(1)}, u32[]{:S(2)}, u32[]{:S(2)}) collective-permute-start(bf16[3,64,256]{2,1,0:T(8,128)(2,1)} %get-tuple-element.35), channel_id=1, source_target_pairs={{0,8},{8,0},{1,9},{9,1},{2,10},{10,2},{3,11},{11,3},{4,12},{12,4},... | collective-permute-start | bytes 294920 | tf_op jit(solution)/shard_map/ppermute | solution.py:40
  5.9 7.0 %collective-permute-start.1 = (bf16[3,128,256]{2,1,0:T(8,128)(2,1)S(1)}, bf16[3,128,256]{2,1,0:T(8,128)(2,1)S(1)}, u32[]{:S(2)}, u32[]{:S(2)}) collective-permute-start(bf16[3,128,256]{2,1,0:T(8,128)(2,1)S(1)} %maximum_select_fusion.own), channel_id=1, source_target_pairs={{0,1},{1,2},{2,3},{3,0},{4,5},{5,6},{6,7},{7,4},{8,24},{9,25},{10,... | collective-permute-start | bytes 589832 | tf_op jit(solution)/shard_map/ppermute | solution.py:32
  7.6 6.9 %collective-permute-start.2 = (bf16[3,128,256]{2,1,0:T(8,128)(2,1)S(1)}, bf16[3,128,256]{2,1,0:T(8,128)(2,1)S(1)}, u32[]{:S(2)}, u32[]{:S(2)}) collective-permute-start(bf16[3,128,256]{2,1,0:T(8,128)(2,1)S(1)} %maximum_select_fusion.own), channel_id=1, source_target_pairs={{0,3},{1,0},{2,1},{3,2},{4,7},{5,4},{6,5},{7,6},{8,56},{9,57},{10,... | collective-permute-start | bytes 589832 | tf_op jit(solution)/shard_map/ppermute | solution.py:32
  9.9 6.6 %collective-permute-start.3 = (bf16[3,128,256]{2,1,0:T(8,128)(2,1)S(1)}, bf16[3,128,256]{2,1,0:T(8,128)(2,1)S(1)}, u32[]{:S(2)}, u32[]{:S(2)}) collective-permute-start(bf16[3,128,256]{2,1,0:T(8,128)(2,1)S(1)} %maximum_select_fusion.own), channel_id=1, source_target_pairs={{0,2},{1,3},{2,0},{3,1},{4,6},{5,7},{6,4},{7,5},{8,40},{9,41},{10,... | collective-permute-start | bytes 589832 | tf_op jit(solution)/shard_map/ppermute | solution.py:32
  11.1 12.4 %collective-permute-start.8 = (bf16[144,512]{1,0:T(8,128)(2,1)S(1)}, bf16[144,512]{1,0:T(8,128)(2,1)S(1)}, u32[]{:S(2)}, u32[]{:S(2)}) collective-permute-start(bf16[144,512]{1,0:T(8,128)(2,1)S(1)} %get-tuple-element.62), channel_id=1, source_target_pairs={{0,1},{1,2},{2,3},{3,4},{4,5},{5,6},{6,7},{7,8},{8,9},{9,10},{10,1... | collective-permute-start | bytes 442376 | tf_op jit(solution)/shard_map/ppermute | solution.py:471
  17.0 19.2 %collective-permute-start.4 = (bf16[4,224,256]{2,1,0:T(8,128)(2,1)S(1)}, bf16[4,224,256]{2,1,0:T(8,128)(2,1)S(1)}, u32[]{:S(2)}, u32[]{:S(2)}) collective-permute-start(bf16[4,224,256]{2,1,0:T(8,128)(2,1)S(1)} %get-tuple-element.47), channel_id=1, source_target_pairs={{0,64},{1,65},{2,66},{3,67},{4,68},{5,69},{6,70},{7,71},{8,76},{9,... | collective-permute-start | bytes 1376264 | tf_op jit(solution)/shard_map/ppermute | solution.py:32
  19.8 16.4 %collective-permute-start.5 = (bf16[4,224,256]{2,1,0:T(8,128)(2,1)S(1)}, bf16[4,224,256]{2,1,0:T(8,128)(2,1)S(1)}, u32[]{:S(2)}, u32[]{:S(2)}) collective-permute-start(bf16[4,224,256]{2,1,0:T(8,128)(2,1)S(1)} %get-tuple-element.47), channel_id=1, source_target_pairs={{0,68},{1,69},{2,70},{3,71},{4,64},{5,65},{6,66},{7,67},{8,72},{9,... | collective-permute-start | bytes 1376264 | tf_op jit(solution)/shard_map/ppermute | solution.py:32
  19.8 7.1 %collective-permute-start.9 = (bf16[144,512]{1,0:T(8,128)(2,1)S(1)}, bf16[144,512]{1,0:T(8,128)(2,1)S(1)}, u32[]{:S(2)}, u32[]{:S(2)}) collective-permute-start(bf16[144,512]{1,0:T(8,128)(2,1)S(1)} %get-tuple-element.61), channel_id=1, source_target_pairs={{1,0},{2,1},{3,2},{4,3},{5,4},{6,5},{7,6},{8,7},{9,8},{10,9},{11,1... | collective-permute-start | bytes 442376 | tf_op jit(solution)/shard_map/ppermute | solution.py:472
  23.5 12.7 %collective-permute-start.6 = (bf16[4,160,256]{2,1,0:T(8,128)(2,1)S(1)}, bf16[4,160,256]{2,1,0:T(8,128)(2,1)S(1)}, u32[]{:S(2)}, u32[]{:S(2)}) collective-permute-start(bf16[4,160,256]{2,1,0:T(8,128)(2,1)S(1)} %get-tuple-element.43), channel_id=1, source_target_pairs={{0,16},{1,17},{2,18},{3,19},{4,20},{5,21},{6,22},{7,23},{8,9},{9,1... | collective-permute-start | bytes 983048 | tf_op jit(solution)/shard_map/ppermute | solution.py:32
  23.5 12.7 %collective-permute-start.7 = (bf16[4,160,256]{2,1,0:T(8,128)(2,1)S(1)}, bf16[4,160,256]{2,1,0:T(8,128)(2,1)S(1)}, u32[]{:S(2)}, u32[]{:S(2)}) collective-permute-start(bf16[4,160,256]{2,1,0:T(8,128)(2,1)S(1)} %get-tuple-element.43), channel_id=1, source_target_pairs={{0,48},{1,49},{2,50},{3,51},{4,52},{5,53},{6,54},{7,55},{8,11},{9,... | collective-permute-start | bytes 983048 | tf_op jit(solution)/shard_map/ppermute | solution.py:32
  36.3 8.9 %collective-permute-start.10 = (bf16[4,224,256]{2,1,0:T(8,128)(2,1)S(1)}, bf16[4,224,256]{2,1,0:T(8,128)(2,1)S(1)}, u32[]{:S(2)}, u32[]{:S(2)}) collective-permute-start(bf16[4,224,256]{2,1,0:T(8,128)(2,1)S(1)} %collective-permute-done.4), channel_id=1, source_target_pairs={{0,64},{1,65},{2,66},{3,67},{4,68},{5,69},{6,70},{7,71},{8,76},{9,... | collective-permute-start | bytes 1376264 | tf_op jit(solution)/shard_map/ppermute | solution.py:32
  37.4 7.7 %collective-permute-start.11 = (bf16[4,160,256]{2,1,0:T(8,128)(2,1)S(1)}, bf16[4,160,256]{2,1,0:T(8,128)(2,1)S(1)}, u32[]{:S(2)}, u32[]{:S(2)}) collective-permute-start(bf16[4,160,256]{2,1,0:T(8,128)(2,1)S(1)} %get-tuple-element.43), channel_id=1, source_target_pairs={{0,32},{1,33},{2,34},{3,35},{4,36},{5,37},{6,38},{7,39},{8,10},{9,... | collective-permute-start | bytes 983048 | tf_op jit(solution)/shard_map/ppermute | solution.py:32
  45.3 17.3 %collective-permute-start.16 = (bf16[4,4,160,256]{3,2,1,0:T(8,128)(2,1)S(1)}, bf16[4,4,160,256]{3,2,1,0:T(8,128)(2,1)S(1)}, u32[]{:S(2)}, u32[]{:S(2)}) collective-permute-start(bf16[4,4,160,256]{3,2,1,0:T(8,128)(2,1)S(1)} %pad_maximum_fusion.d0), channel_id=1, source_target_pairs={{0,64},{1,65},{2,66},{3,67},{4,68},{5,69},{6,70},{7,71},{8,76},{9,... | collective-permute-start | bytes 3932168 | tf_op jit(solution)/shard_map/ppermute | solution.py:32
  46.4 15.6 %collective-permute-start.15 = (bf16[4,4,128,256]{3,2,1,0:T(8,128)(2,1)S(1)}, bf16[4,4,128,256]{3,2,1,0:T(8,128)(2,1)S(1)}, u32[]{:S(2)}, u32[]{:S(2)}) collective-permute-start(bf16[4,4,128,256]{3,2,1,0:T(8,128)(2,1)S(1)} %pad_maximum_fusion.1.a0), channel_id=1, source_target_pairs={{0,32},{1,33},{2,34},{3,35},{4,36},{5,37},{6,38},{7,39},{8,10},{9,... | collective-permute-start | bytes 3145736 | tf_op jit(solution)/shard_map/ppermute | solution.py:32
  49.0 7.4 %collective-permute-start.12 = (f32[152,1024]{1,0:T(8,128)S(1)}, f32[152,1024]{1,0:T(8,128)S(1)}, u32[]{:S(2)}, u32[]{:S(2)}) collective-permute-start(f32[152,1024]{1,0:T(8,128)S(1)} %get-tuple-element.46.own), channel_id=1, source_target_pairs={{0,8},{8,0},{1,9},{9,1},{2,10},{10,2},{3,11},{11,3},{4,12},{12,4},... | collective-permute-start | bytes 1867784 | tf_op jit(solution)/shard_map/ppermute | solution.py:40
  53.2 20.0 %collective-permute-start.13 = (bf16[4,4,128,256]{3,2,1,0:T(8,128)(2,1)S(1)}, bf16[4,4,128,256]{3,2,1,0:T(8,128)(2,1)S(1)}, u32[]{:S(2)}, u32[]{:S(2)}) collective-permute-start(bf16[4,4,128,256]{3,2,1,0:T(8,128)(2,1)S(1)} %pad_maximum_fusion.1.a0), channel_id=1, source_target_pairs={{0,16},{1,17},{2,18},{3,19},{4,20},{5,21},{6,22},{7,23},{8,9},{9,1... | collective-permute-start | bytes 3145736 | tf_op jit(solution)/shard_map/ppermute | solution.py:32
  54.1 23.7 %collective-permute-start.14 = (bf16[4,4,128,256]{3,2,1,0:T(8,128)(2,1)S(1)}, bf16[4,4,128,256]{3,2,1,0:T(8,128)(2,1)S(1)}, u32[]{:S(2)}, u32[]{:S(2)}) collective-permute-start(bf16[4,4,128,256]{3,2,1,0:T(8,128)(2,1)S(1)} %pad_maximum_fusion.1.a0), channel_id=1, source_target_pairs={{0,48},{1,49},{2,50},{3,51},{4,52},{5,53},{6,54},{7,55},{8,11},{9,... | collective-permute-start | bytes 3145736 | tf_op jit(solution)/shard_map/ppermute | solution.py:32
  56.4 32.1 %collective-permute-start.18 = (bf16[4,4,96,256]{3,2,1,0:T(8,128)(2,1)S(1)}, bf16[4,4,96,256]{3,2,1,0:T(8,128)(2,1)S(1)}, u32[]{:S(2)}, u32[]{:S(2)}) collective-permute-start(bf16[4,4,96,256]{3,2,1,0:T(8,128)(2,1)S(1)} %pad_maximum_fusion.2.u0), channel_id=1, source_target_pairs={{0,16},{1,17},{2,18},{3,19},{4,20},{5,21},{6,22},{7,23},{8,9},{9,1... | collective-permute-start | bytes 2359304 | tf_op jit(solution)/shard_map/ppermute | solution.py:32
  61.9 31.2 %collective-permute-start.21 = (bf16[4,4,160,256]{3,2,1,0:T(8,128)(2,1)S(1)}, bf16[4,4,160,256]{3,2,1,0:T(8,128)(2,1)S(1)}, u32[]{:S(2)}, u32[]{:S(2)}) collective-permute-start(bf16[4,4,160,256]{3,2,1,0:T(8,128)(2,1)S(1)} %pad_maximum_fusion.d0), channel_id=1, source_target_pairs={{0,68},{1,69},{2,70},{3,71},{4,64},{5,65},{6,66},{7,67},{8,72},{9,... | collective-permute-start | bytes 3932168 | tf_op jit(solution)/shard_map/ppermute | solution.py:32
  62.6 30.5 %collective-permute-start.22 = (bf16[4,4,160,256]{3,2,1,0:T(8,128)(2,1)S(1)}, bf16[4,4,160,256]{3,2,1,0:T(8,128)(2,1)S(1)}, u32[]{:S(2)}, u32[]{:S(2)}) collective-permute-start(bf16[4,4,160,256]{3,2,1,0:T(8,128)(2,1)S(1)} %collective-permute-done.16.d1), channel_id=1, source_target_pairs={{0,64},{1,65},{2,66},{3,67},{4,68},{5,69},{6,70},{7,71},{8,76},{9,... | collective-permute-start | bytes 3932168 | tf_op jit(solution)/shard_map/ppermute | solution.py:32
  73.1 18.3 %collective-permute-start.19 = (bf16[4,4,96,256]{3,2,1,0:T(8,128)(2,1)S(1)}, bf16[4,4,96,256]{3,2,1,0:T(8,128)(2,1)S(1)}, u32[]{:S(2)}, u32[]{:S(2)}) collective-permute-start(bf16[4,4,96,256]{3,2,1,0:T(8,128)(2,1)S(1)} %pad_maximum_fusion.2.u0), channel_id=1, source_target_pairs={{0,48},{1,49},{2,50},{3,51},{4,52},{5,53},{6,54},{7,55},{8,11},{9,... | collective-permute-start | bytes 2359304 | tf_op jit(solution)/shard_map/ppermute | solution.py:32
  77.7 13.8 %collective-permute-start.20 = (bf16[4,4,96,256]{3,2,1,0:T(8,128)(2,1)S(1)}, bf16[4,4,96,256]{3,2,1,0:T(8,128)(2,1)S(1)}, u32[]{:S(2)}, u32[]{:S(2)}) collective-permute-start(bf16[4,4,96,256]{3,2,1,0:T(8,128)(2,1)S(1)} %pad_maximum_fusion.2.u0), channel_id=1, source_target_pairs={{0,32},{1,33},{2,34},{3,35},{4,36},{5,37},{6,38},{7,39},{8,10},{9,... | collective-permute-start | bytes 2359304 | tf_op jit(solution)/shard_map/ppermute | solution.py:32
  88.4 4.7 %collective-permute-start.17 = (bf16[2,144,1024]{2,1,0:T(8,128)(2,1)S(1)}, bf16[2,144,1024]{2,1,0:T(8,128)(2,1)S(1)}, u32[]{:S(2)}, u32[]{:S(2)}) collective-permute-start(bf16[2,144,1024]{2,1,0:T(8,128)(2,1)S(1)} %coarse_attention.1.sent), channel_id=1, source_target_pairs={{0,8},{8,0},{1,9},{9,1},{2,10},{10,2},{3,11},{11,3},{4,12},{12,4},... | collective-permute-start | bytes 1769480 | tf_op jit(solution)/shard_map/ppermute | solution.py:40
  99.6 4.9 %collective-permute-start.23 = (bf16[144,1024]{1,0:T(8,128)(2,1)S(1)}, bf16[144,1024]{1,0:T(8,128)(2,1)S(1)}, u32[]{:S(2)}, u32[]{:S(2)}) collective-permute-start(bf16[144,1024]{1,0:T(8,128)(2,1)S(1)} %get-tuple-element.59), channel_id=1, source_target_pairs={{0,8},{8,0},{1,9},{9,1},{2,10},{10,2},{3,11},{11,3},{4,12},{12,4},... | collective-permute-start | bytes 884744 | tf_op jit(solution)/shard_map/ppermute | solution.py:40
  (11 other events, 124.0 us)
